TPU v7x, 32 devices: a whole 2x2x4 slice. The times are simulated.
32 devices in a mesh: wide: 8 (over y, x, core), narrow: 4 (over z).
Axes of the slice: x: 2, y: 2, z: 4, core: 2. Of those that a mesh axis runs over, the one named last changes fastest.
Arguments:
- raster: int32 [512, 1024], P('narrow', 'wide'), may hold values from 0 to 1
- transmission: bfloat16 [512, 1024], P('narrow', 'wide'), may hold values from 0.5 to 1.5
- kernels: float32 [8, 2, 64, 64], replicated, may hold values from -0.09375 to 0.09375
- kernel_weight: float32 [8], replicated, may hold values from 0.1 to 1
- library: bfloat16 [65536, 256], P(('wide', 'narrow')), may hold values from -40 to 40
- clip_tile: int32 [128], replicated, may hold values from 0 to 31, as said below
- clip_corner: int32 [2, 128], replicated, may hold values from 0 to 64
Outputs:
- aerial: float32 [512, 1024], P('narrow', 'wide')
- scores: float32 [128], P(('wide', 'narrow'))
Inputs may be any that keep to these rules, and one draw needn't show every extreme that they name: `clip_tile`: each tile owns at most 16 clips, and some tile owns exactly 16.
All inputs are finite; a program needn't handle non-finite values.
Results may differ from a plain program's by a relative error of at most 0.0011.
Values may be sent and summed in bfloat16 or wider, within the bound.
No kernel may reach another device: no remote copies, remote signals or barrier semaphores. Data moves between devices by JAX's collectives and lax.ppermute only.
A program may use at most 64 MiB of HBM per device.

v0:
```python
import math

import jax
import jax.numpy as jnp
import numpy as np
from jax import lax
from jax.experimental import pallas as pl
from jax.experimental.pallas import tpu as pltpu
from jax.sharding import PartitionSpec as P

KSIZE = 64
CLIP = 64
KSIG = 16
CAP = 16
SIGD = KSIG * KSIG
LANES = 128

sharpness = 400.0
f32 = jnp.float32
bf16 = jnp.bfloat16
VMEM_SPEC = pl.BlockSpec(memory_space=pltpu.VMEM)


def ceil_to(value, step):
    return -(-value // step) * step


def halves(table):
    high = table.astype(bf16)
    return high, (table - high.astype(np.float64)).astype(bf16)


def tables(tile):
    full = tile + KSIZE
    half = full // 2
    wide = ceil_to(full, 2 * LANES)
    unit = 2.0 * math.pi / full
    place = np.arange(full)
    place = np.where(place < tile + KSIZE // 2, place, place - full)
    taps = np.arange(KSIZE) - KSIZE // 2
    odd = np.arange(half) + 0.5
    freq = np.arange(full)

    def padded(table, rows, cols):
        out = np.zeros((rows, cols))
        out[: table.shape[0], : table.shape[1]] = table
        return out

    def side_by_side(angle, rows, cols):
        return np.concatenate(
            [padded(np.cos(angle), rows, cols), padded(np.sin(angle), rows, cols)], axis=1
        )

    angle = unit * odd[:, None] * place[None, :]
    rows_in = padded(np.concatenate([np.cos(angle), -np.sin(angle)]), full, wide)
    cols_in = side_by_side(unit * place[:, None] * freq[None, :], wide, wide)
    cols_out = side_by_side(unit * freq[:, None] * np.arange(tile)[None, :], wide, tile)
    angle = unit * np.arange(tile)[:, None] * odd[None, :]
    rows_out = padded(np.concatenate([np.cos(angle), -np.sin(angle)], axis=1), tile, wide)
    angle = unit * odd[:, None] * taps[None, :]
    taps_rows = np.concatenate([np.cos(angle), np.sin(angle)]) * (2.0 / (full * full))
    taps_cols = side_by_side(unit * taps[:, None] * freq[None, :], KSIZE, wide)
    high, low = halves(taps_rows)
    taps_rows = np.concatenate([high, low, high, low], axis=1)
    high, low = halves(taps_cols)
    taps_cols = np.concatenate([high, high, low, low], axis=0)
    return {
        "rows_in": halves(rows_in),
        "cols_in": halves(cols_in),
        "cols_out": halves(cols_out),
        "rows_out": halves(rows_out),
        "taps_rows": taps_rows,
        "taps_cols": taps_cols,
    }


def dot(left, right):
    return jnp.dot(left, right, preferred_element_type=f32)


def split(value):
    high = value.astype(bf16)
    return high, (value - high.astype(f32)).astype(bf16)


def dot3(left, right):
    return dot(left[0], right[0]) + dot(left[1], right[0]) + dot(left[0], right[1])


def dot3_t(left, right):
    def single(a, b):
        return lax.dot_general(a, b, (((1,), (1,)), ((), ())), preferred_element_type=f32)

    return single(left[0], right[0]) + single(left[1], right[0]) + single(left[0], right[1])


def iota(shape, dim):
    return lax.broadcasted_iota(jnp.int32, shape, dim)


def shifted_basis(corner, tile):
    shape = (CAP * KSIG, tile)
    freq = iota(shape, 0) & (KSIG - 1)
    offset = iota(shape, 1) - corner
    turn = ((2 * offset + 1) * freq) & (4 * CLIP - 1)
    fold = jnp.abs(turn.astype(f32) * (1.0 / (2 * CLIP)) - 1.0) - 0.5
    x = fold * math.pi
    square = x * x
    series = jnp.full(shape, -1.0 / math.factorial(15), f32)
    for order in (13, 11, 9, 7, 5, 3, 1):
        sign = 1.0 if order % 4 == 1 else -1.0
        series = series * square + sign / math.factorial(order)
    weight = jnp.where(freq == 0, math.sqrt(1.0 / CLIP), math.sqrt(2.0 / CLIP))
    inside = (offset >= 0) & (offset < CLIP)
    return jnp.where(inside, weight * (series * x), 0.0)


def filters_body(
    cols_wide, taps_ref, rows_ref, cols_ref, tile_ref, corner_ref, out_ref, rb_ref, cb_ref
):
    real_count = out_ref.shape[0]
    half = out_ref.shape[2]
    wide = out_ref.shape[3]

    def one(index, carry):
        taps = taps_ref[index]
        spread = jnp.concatenate([taps, taps, taps, taps], axis=1)
        high, low = split(spread)
        stacked = jnp.concatenate([high, high, low, low], axis=0)
        rows = dot(rows_ref[...], stacked)
        kept = rows.astype(bf16).astype(f32)
        is_low = (iota(rows.shape, 1) & KSIZE) != 0
        mixed = jnp.where(is_low, rows - kept, rows).astype(bf16)
        both = dot(mixed, cols_ref[...])
        out_ref[index, 0] = both[:half, :wide] - both[half:, wide:]
        out_ref[index, 1] = both[:half, wide:] + both[half:, :wide]
        return carry

    lax.fori_loop(0, real_count, one, 0, unroll=2)

    clip_count = tile_ref.shape[1]
    own_tile = lax.axis_index("narrow") * cols_wide + lax.axis_index("wide")
    owned = tile_ref[...] == own_tile
    owned8 = jnp.broadcast_to(owned.astype(f32), (8, clip_count))
    square = (clip_count, clip_count)
    earlier = (iota(square, 0) < iota(square, 1)).astype(f32).astype(bf16)
    rank = dot(owned8.astype(bf16), earlier)[:1]
    rank = jnp.where(owned, rank, -1.0)
    slot = (iota((CAP * KSIG, clip_count), 0) // KSIG).astype(f32)
    select = (slot == rank).astype(f32).astype(bf16)
    tile = rb_ref.shape[2]
    for axis, basis_ref in ((0, rb_ref), (1, cb_ref)):
        line = corner_ref[axis : axis + 1, :].astype(f32).astype(bf16)
        table = jnp.broadcast_to(line, (tile, clip_count))
        corner = lax.dot_general(
            select, table, (((1,), (1,)), ((), ())), preferred_element_type=f32
        )
        high, low = split(shifted_basis(corner.astype(jnp.int32), tile))
        basis_ref[0] = high
        basis_ref[1] = low


def image_body(
    raster_ref,
    light_ref,
    side_ref,
    after_ref,
    before_ref,
    weight_ref,
    filter_ref,
    rb_ref,
    cb_ref,
    rows_in_ref,
    cols_in_ref,
    cols_out_ref,
    rows_out_ref,
    aerial_ref,
    units_ref,
    mask_ref,
    spec_ref,
    prod_ref,
    mid_ref,
):
    tile = raster_ref.shape[0]
    half = filter_ref.shape[2]
    full = 2 * half
    wide = filter_ref.shape[3]
    border = KSIZE // 2
    mask_ref[:tile, :tile] = (raster_ref[...].astype(f32) * light_ref[...].astype(f32)).astype(bf16)
    mask_ref[:tile, tile:] = side_ref[...]
    mask_ref[tile : tile + border, :] = after_ref[...]
    mask_ref[tile + border : full, :] = before_ref[...]
    mask_ref[full:, :] = jnp.zeros((wide - full, wide), bf16)
    mask = mask_ref[...]
    rows = dot(rows_in_ref[0], mask) + dot(rows_in_ref[1], mask)
    both = dot3(split(rows), (cols_in_ref[0], cols_in_ref[1]))
    spec_ref[0] = both[:half, :wide] + both[half:, wide:]
    spec_ref[1] = both[half:, :wide] - both[:half, wide:]
    aerial_ref[...] = jnp.zeros_like(aerial_ref)
    mid_ref[:, full:, :] = jnp.zeros((2, wide - full, wide), bf16)

    def one(index, carry):
        for part in range(2):
            real = filter_ref[2 * index + part, 0]
            imag = filter_ref[2 * index + part, 1]
            base = part * full
            high, low = split(spec_ref[0] * real - spec_ref[1] * imag)
            prod_ref[0, base : base + half] = high
            prod_ref[1, base : base + half] = low
            high, low = split(spec_ref[0] * imag + spec_ref[1] * real)
            prod_ref[0, base + half : base + full] = high
            prod_ref[1, base + half : base + full] = low
        cols = dot3((prod_ref[0], prod_ref[1]), (cols_out_ref[0], cols_out_ref[1]))
        for part in range(2):
            base = part * full
            lane = part * tile
            real = cols[base : base + half]
            imag = cols[base + half : base + full]
            high, low = split(real[:, :tile] - imag[:, tile:])
            mid_ref[0, :half, lane : lane + tile] = high
            mid_ref[1, :half, lane : lane + tile] = low
            high, low = split(imag[:, :tile] + real[:, tile:])
            mid_ref[0, half:full, lane : lane + tile] = high
            mid_ref[1, half:full, lane : lane + tile] = low
        field = dot3((rows_out_ref[0], rows_out_ref[1]), (mid_ref[0], mid_ref[1]))
        energy = field * field
        aerial_ref[...] += weight_ref[index] * (energy[:, :tile] + energy[:, tile:])
        return carry

    lax.fori_loop(0, filter_ref.shape[0] // 2, one, 0, unroll=2)

    halfway = dot3((rb_ref[0], rb_ref[1]), split(aerial_ref[...]))
    crossed = dot3_t(split(halfway), (cb_ref[0], cb_ref[1]))
    shape = (CAP * KSIG, CAP * KSIG)
    crossed = jnp.where(iota(shape, 0) // KSIG == iota(shape, 1) // KSIG, crossed, 0.0)
    fold = ((iota(shape, 0) & (KSIG - 1)) == (iota(shape, 1) & (KSIG - 1))).astype(f32).astype(bf16)
    high, low = split(crossed)
    spread = dot(high, fold) + dot(low, fold)
    spread = jnp.where((iota(shape, 0) & (KSIG - 1)) == iota(shape, 1) // KSIG, spread, 0.0)
    signature = jnp.sum(spread.reshape(CAP, KSIG, SIGD), axis=1)
    signature = jnp.where(iota(signature.shape, 1) == 0, 0.0, signature)
    mean_square = jnp.mean(signature * signature, axis=1, keepdims=True)
    units = (signature / (KSIG * jnp.sqrt(mean_square + 1e-06))).astype(bf16)
    units_ref[...] = jnp.broadcast_to(units[None], units_ref.shape)


def library_body(library_ref, out_ref):
    rows = library_ref[...].astype(f32)
    mean_square = jnp.mean(rows * rows, axis=1, keepdims=True)
    out_ref[...] = (rows * (1.0 / (KSIG * jnp.sqrt(mean_square + 1e-06)))).astype(bf16)


def match_body(cols_wide, rows_narrow, tile_ref, gathered_ref, library_ref, out_ref):
    clip_count = tile_ref.shape[1]
    slot_count = gathered_ref.shape[0]
    device_count = out_ref.shape[0]
    own_count = clip_count // device_count
    row = tile_ref[...].astype(f32)
    peaks = []
    for first in range(0, clip_count, LANES):
        shape = (LANES, clip_count)
        clip = iota(shape, 0) + first
        other = iota(shape, 1)
        spread = jnp.broadcast_to(row, shape)
        column = jnp.sum(jnp.where(clip == other, spread, 0.0), axis=1, keepdims=True)
        before = (spread == column) & (other < clip)
        rank = jnp.sum(before.astype(f32), axis=1, keepdims=True)
        grid_row = jnp.floor((column + 0.5) * (1.0 / cols_wide))
        holder = (column - grid_row * cols_wide) * rows_narrow + grid_row
        place = (holder * CAP + rank).astype(jnp.int32)
        pick = (iota((LANES, slot_count), 1) == place).astype(f32).astype(bf16)
        units = dot(pick, gathered_ref[...]).astype(bf16)
        cosine = lax.dot_general(
            library_ref[...], units, (((1,), (1,)), ((), ())), preferred_element_type=f32
        )
        logits = sharpness * (cosine - 1.0)
        peak = jnp.max(logits, axis=0, keepdims=True)
        total = jnp.sum(jnp.exp(logits - peak), axis=0, keepdims=True)
        peaks.append(peak + jnp.log(total))
    slab = peaks[0] if len(peaks) == 1 else jnp.concatenate(peaks, axis=1)
    shape = (device_count, clip_count)
    spread = jnp.broadcast_to(slab, shape)
    lane = iota((device_count, LANES), 1)
    sent = jnp.zeros((device_count, LANES), f32)
    for index in range(own_count):
        mine = iota(shape, 1) == iota(shape, 0) * own_count + index
        value = jnp.sum(jnp.where(mine, spread, 0.0), axis=1, keepdims=True)
        sent = jnp.where(lane == index, value, sent)
    out_ref[...] = sent


def call(body, out_shape, operands, scratch=(), limit=24, smem=(), flops=0, name=None):
    specs = [
        pl.BlockSpec(memory_space=pltpu.SMEM) if index in smem else VMEM_SPEC
        for index in range(len(operands))
    ]
    return pl.pallas_call(
        body,
        out_shape=out_shape,
        in_specs=specs,
        out_specs=jax.tree.map(lambda _: VMEM_SPEC, out_shape),
        scratch_shapes=list(scratch),
        compiler_params=pltpu.CompilerParams(vmem_limit_bytes=limit << 20),
        cost_estimate=pl.CostEstimate(flops=flops, bytes_accessed=1 << 20, transcendentals=0),
        name=name,
    )(*operands)


def exchanged(low_edge, high_edge, axis):
    count = lax.axis_size(axis)
    forward = [(i, i + 1) for i in range(count - 1)]
    backward = [(target, source) for source, target in forward]
    return lax.ppermute(high_edge, axis, forward), lax.ppermute(low_edge, axis, backward)


def per_device(raster, transmission, kernels, kernel_weight, library, clip_tile, clip_corner):
    tile = raster.shape[0]
    border = KSIZE // 2
    full = tile + KSIZE
    half = full // 2
    wide = ceil_to(full, 2 * LANES)
    table = {
        key: jnp.stack([jnp.asarray(part) for part in value])
        if isinstance(value, tuple)
        else jnp.asarray(value)
        for key, value in tables(tile).items()
    }
    cols_wide = lax.axis_size("wide")
    rows_narrow = lax.axis_size("narrow")
    device_count = cols_wide * rows_narrow
    both = ("wide", "narrow")
    clip_count = clip_tile.shape[0]
    kernel_count = kernels.shape[0]

    def masked(rows, cols):
        return raster[rows, cols].astype(bf16) * transmission[rows, cols]

    every = slice(None)
    left, right = exchanged(
        masked(every, slice(0, border)), masked(every, slice(tile - border, tile)), "wide"
    )
    side = jnp.concatenate([right, left, jnp.zeros((tile, wide - full), bf16)], axis=1)
    top = slice(0, border)
    bottom = slice(tile - border, tile)
    before, after = exchanged(
        jnp.concatenate([masked(top, every), side[top]], axis=1),
        jnp.concatenate([masked(bottom, every), side[bottom]], axis=1),
        "narrow",
    )

    tile_line = clip_tile.reshape(1, clip_count)
    basis = jax.ShapeDtypeStruct((2, CAP * KSIG, tile), bf16)
    filters, row_basis, col_basis = call(
        lambda *refs: filters_body(cols_wide, *refs),
        (
            jax.ShapeDtypeStruct((2 * kernel_count, 2, half, wide), f32),
            basis,
            basis,
        ),
        (
            kernels.reshape(2 * kernel_count, KSIZE, KSIZE),
            table["taps_rows"],
            table["taps_cols"],
            tile_line,
            clip_corner,
        ),
        flops=3 << 30,
        name="filters",
    )
    aerial, copies = call(
        image_body,
        (
            jax.ShapeDtypeStruct((tile, tile), f32),
            jax.ShapeDtypeStruct((device_count, CAP, SIGD), bf16),
        ),
        (
            raster,
            transmission,
            side,
            after,
            before,
            kernel_weight,
            filters,
            row_basis,
            col_basis,
            table["rows_in"],
            table["cols_in"],
            table["cols_out"],
            table["rows_out"],
        ),
        scratch=(
            pltpu.VMEM((wide, wide), bf16),
            pltpu.VMEM((2, half, wide), f32),
            pltpu.VMEM((2, 2 * full, wide), bf16),
            pltpu.VMEM((2, wide, wide), bf16),
        ),
        smem=(5,),
        flops=6 << 30,
        name="image",
    )
    lib_units = call(
        library_body,
        jax.ShapeDtypeStruct(library.shape, bf16),
        (library,),
        flops=1 << 30,
        name="library",
    )
    gathered = lax.all_to_all(copies, both, 0, 0, tiled=True).reshape(device_count * CAP, SIGD)
    slab = call(
        lambda *refs: match_body(cols_wide, rows_narrow, *refs),
        jax.ShapeDtypeStruct((device_count, LANES), f32),
        (tile_line, gathered, lib_units),
        limit=40,
        flops=1 << 30,
        name="match",
    )
    slab = lax.all_to_all(slab, both, 0, 0, tiled=True)[:, : clip_count // device_count]
    peak = jnp.max(slab, axis=0)
    total = jnp.sum(jnp.exp(slab - peak[None, :]), axis=0)
    scores = -(peak + jnp.log(total)) / sharpness
    return (aerial, scores)


def solution(mesh):
    placed = (
        P("narrow", "wide"),
        P("narrow", "wide"),
        P(),
        P(),
        P(("wide", "narrow"), None),
        P(),
        P(),
    )
    return jax.shard_map(
        per_device,
        mesh=mesh,
        in_specs=placed,
        out_specs=(P("narrow", "wide"), P(("wide", "narrow"))),
        check_vma=False,
    )
```

profile of v0, /device:TPU:0, one launch (start us, length us, event | category | flops | bytes accessed | tf_op | source)
XLA Modules:
  0.0 62.0 jit_solution(8580121482814046512)
XLA Ops:
  0.6 0.8 %convert.6 = bf16[128,128]{1,0:T(8,128)(2,1)S(1)} convert(s32[128,128]{1,0:T(8,128)} %raster_ref.1) | non-fusion elementwise | flops 16384 | bytes 98304 | tf_op jit(solution)/shard_map/convert.3
  1.5 0.9 %slice_multiply_fusion.1 = (bf16[128,32]{1,0:T(8,128)(2,1)S(1)}, bf16[128,32]{1,0:T(8,128)(2,1)S(1)}) fusion(bf16[128,128]{1,0:T(8,128)(2,1)S(1)} %convert.6, bf16[128,128]{1,0:T(8,128)(2,1)} %light_ref.1), kind=kLoop, calls=%fused_computation.1 | loop fusion | flops 8192 | bytes 49152 | tf_op jit(solution)/shard_map/mul | solution.py:336
  2.4 1.3 %collective-permute-start = (bf16[128,32]{1,0:T(8,128)(2,1)S(1)}, bf16[128,32]{1,0:T(8,128)(2,1)S(1)}, u32[]{:S(2)}, u32[]{:S(2)}) collective-permute-start(bf16[128,32]{1,0:T(8,128)(2,1)S(1)} %get-tuple-element.14), channel_id=1, source_target_pairs={{4,0},{8,4},{12,8},{16,12},{20,16},{24,20},{28,24},{5,1},{9,5},{13... | collective-permute-start | bytes 24584 | tf_op jit(solution)/shard_map/ppermute | solution.py:313
  3.7 3.0 %collective-permute-start.1 = (bf16[128,32]{1,0:T(8,128)(2,1)S(1)}, bf16[128,32]{1,0:T(8,128)(2,1)S(1)}, u32[]{:S(2)}, u32[]{:S(2)}) collective-permute-start(bf16[128,32]{1,0:T(8,128)(2,1)S(1)} %get-tuple-element.15), channel_id=1, source_target_pairs={{0,4},{4,8},{8,12},{12,16},{16,20},{20,24},{24,28},{1,5},{5,9},{9,... | collective-permute-start | bytes 24584 | tf_op jit(solution)/shard_map/ppermute | solution.py:313
  6.7 0.7 %slice_multiply_fusion.2 = (bf16[32,128]{1,0:T(8,128)(2,1)S(1)}, bf16[32,128]{1,0:T(8,128)(2,1)S(1)}) fusion(bf16[128,128]{1,0:T(8,128)(2,1)S(1)} %convert.6, bf16[128,128]{1,0:T(8,128)(2,1)} %light_ref.1), kind=kLoop, calls=%fused_computation.7 | loop fusion | flops 8192 | bytes 49152 | tf_op jit(solution)/shard_map/mul | solution.py:336
  7.5 0.1 pad.6.clone
  7.5 0.0 collective-permute-done.1
  7.6 0.1 maximum_maximum_fusion.side_ref
  7.7 5.0 %collective-permute-start.3 = (bf16[32,256]{1,0:T(8,128)(2,1)S(1)}, bf16[32,256]{1,0:T(8,128)(2,1)S(1)}, u32[]{:S(2)}, u32[]{:S(2)}) collective-permute-start(bf16[32,256]{1,0:T(8,128)(2,1)S(1)} %pad_maximum_fusion.1), channel_id=1, source_target_pairs={{0,1},{1,2},{2,3},{4,5},{5,6},{6,7},{8,9},{9,10},{10,11},{12,13},{... | collective-permute-start | bytes 49160 | tf_op jit(solution)/shard_map/ppermute | solution.py:313
  12.7 1.3 %collective-permute-start.2 = (bf16[32,256]{1,0:T(8,128)(2,1)S(1)}, bf16[32,256]{1,0:T(8,128)(2,1)S(1)}, u32[]{:S(2)}, u32[]{:S(2)}) collective-permute-start(bf16[32,256]{1,0:T(8,128)(2,1)S(1)} %pad_maximum_fusion), channel_id=1, source_target_pairs={{1,0},{2,1},{3,2},{5,4},{6,5},{7,6},{9,8},{10,9},{11,10},{13,12},{... | collective-permute-start | bytes 49160 | tf_op jit(solution)/shard_map/ppermute | solution.py:313
  14.0 1.0 %copy-done.3 = f32[8,2,64,64]{3,2,1,0:T(8,128)S(1)} copy-done((f32[8,2,64,64]{3,2,1,0:T(8,128)S(1)}, f32[8,2,64,64]{3,2,1,0:T(8,128)}, u32[]{:S(2)}) %copy-start.3) | copy-done | bytes 262168
  15.0 0.7 %copy-done.4 = s32[2,128]{1,0:T(2,128)S(1)} copy-done((s32[2,128]{1,0:T(2,128)S(1)}, s32[2,128]{1,0:T(2,128)}, u32[]{:S(2)}) %copy-start.4) | copy-done | bytes 1048
  15.7 0.7 %copy-done.6 = s32[128]{0:T(128)S(1)} copy-done((s32[128]{0:T(128)S(1)}, s32[128]{0:T(128)}, u32[]{:S(2)}) %copy-start.6) | copy-done | bytes 536
  16.4 0.9 %copy-done.10 = bf16[256,512]{1,0:T(8,128)(2,1)S(1)} copy-done((bf16[256,512]{1,0:T(8,128)(2,1)S(1)}, bf16[256,512]{1,0:T(8,128)(2,1)}, u32[]{:S(2)}) %copy-start.10) | copy-done | bytes 262168
  17.3 0.9 %copy-done.13 = bf16[192,256]{1,0:T(8,128)(2,1)S(1)} copy-done((bf16[192,256]{1,0:T(8,128)(2,1)S(1)}, bf16[192,256]{1,0:T(8,128)(2,1)}, u32[]{:S(2)}) %copy-start.13) | copy-done | bytes 98328
  18.2 0.0 copy-start.11
  18.2 4.4 %filters.1 = (f32[16,2,96,256]{3,2,1,0:T(8,128)S(1)}, bf16[2,256,128]{2,1,0:T(8,128)(2,1)S(1)}, bf16[2,256,128]{2,1,0:T(8,128)(2,1)S(1)}) custom-call(f32[16,64,64]{2,1,0:T(8,128)S(1)} %bitcast.9, bf16[192,256]{1,0:T(8,128)(2,1)S(1)} %copy-done.13, bf16[256,512]{1,0:T(8,128)(2,1)S(1)} %copy-done.10, s32[1,128]{1,0:T(1,128)S(1)} %bitcast.10, ...), custom_call_target="tpu_custom_call" | custom-call | flops 3221225472 | bytes 1048576 | tf_op jit(solution)/shard_map/filters/pallas_call | solution.py:297
  22.8 7.8 %image.1 = (f32[128,128]{1,0:T(8,128)}, bf16[32,16,256]{2,1,0:T(8,128)(2,1)}) custom-call(s32[128,128]{1,0:T(8,128)S(1)} %copy-done.1, bf16[128,128]{1,0:T(8,128)(2,1)S(1)} %copy-done, bf16[128,128]{1,0:T(8,128)(2,1)S(1)} %maximum_maximum_fusion.side_ref, bf16[32,256]{1,0:T(8,128)(2,1)S(1)} %collective-permute-done.2.after_ref, ...), custom_call_target="tpu_custom_call" | custom-call | flops 6442450944 | bytes 1048576 | tf_op jit(solution)/shard_map/image/pallas_call | solution.py:297
  30.6 9.7 %all-to-all-start = ((bf16[32,16,256]{2,1,0:T(8,128)(2,1)}), bf16[32,16,256]{2,1,0:T(8,128)(2,1)S(1)}, u32[]{:S(2)}, u32[]{:S(2)}) async-start(bf16[32,16,256]{2,1,0:T(8,128)(2,1)} %get-tuple-element.11), calls=%async_computation | async-start | bytes 524288 | tf_op jit(solution)/shard_map/all_to_all | solution.py:408
  40.3 0.7 %library.1.refs_2_ = bf16[2048,256]{1,0:T(8,128)(2,1)S(1)} custom-call(bf16[2048,256]{1,0:T(8,128)(2,1)S(1)} %copy-done.2), custom_call_target="tpu_custom_call" | custom-call | flops 1073741824 | bytes 1048576 | tf_op jit(solution)/shard_map/library/pallas_call | solution.py:297
  41.0 9.6 %all-to-all-done = bf16[32,16,256]{2,1,0:T(8,128)(2,1)S(1)} async-done(((bf16[32,16,256]{2,1,0:T(8,128)(2,1)}), bf16[32,16,256]{2,1,0:T(8,128)(2,1)S(1)}, u32[]{:S(2)}, u32[]{:S(2)}) %all-to-all-start) | async-done | bytes 262176 | tf_op jit(solution)/shard_map/all_to_all | solution.py:408
  50.6 1.2 %match.1 = f32[32,128]{1,0:T(8,128)S(1)} custom-call(s32[1,128]{1,0:T(1,128)S(1)} %bitcast.11, bf16[512,256]{1,0:T(8,128)(2,1)S(1)} %bitcast.7, bf16[2048,256]{1,0:T(8,128)(2,1)S(1)} %library.1.refs_2_), custom_call_target="tpu_custom_call" | custom-call | flops 1073741824 | bytes 1048576 | tf_op jit(solution)/shard_map/match/pallas_call | solution.py:297
  51.8 9.7 %all_to_all.17 = f32[32,1,128]{2,1,0:T(1,128)S(1)} all-to-all(f32[32,1,128]{2,1,0:T(1,128)S(1)} %bitcast.8), channel_id=1, replica_groups=mesh['wide'=8,'narrow'=4] {'wide','narrow'}, dimensions={0} | all-to-all | bytes 32768 | tf_op jit(solution)/shard_map/all_to_all | solution.py:417
  61.5 0.5 negate_multiply_fusion
  (31 shorter events, 0.1 us)
Async XLA Ops:
  2.4 5.1 %collective-permute-start = (bf16[128,32]{1,0:T(8,128)(2,1)S(1)}, bf16[128,32]{1,0:T(8,128)(2,1)S(1)}, u32[]{:S(2)}, u32[]{:S(2)}) collective-permute-start(bf16[128,32]{1,0:T(8,128)(2,1)S(1)} %get-tuple-element.14), channel_id=1, source_target_pairs={{4,0},{8,4},{12,8},{16,12},{20,16},{24,20},{28,24},{5,1},{9,5},{13... | collective-permute-start | bytes 24584 | tf_op jit(solution)/shard_map/ppermute | solution.py:313
  3.7 3.9 %collective-permute-start.1 = (bf16[128,32]{1,0:T(8,128)(2,1)S(1)}, bf16[128,32]{1,0:T(8,128)(2,1)S(1)}, u32[]{:S(2)}, u32[]{:S(2)}) collective-permute-start(bf16[128,32]{1,0:T(8,128)(2,1)S(1)} %get-tuple-element.15), channel_id=1, source_target_pairs={{0,4},{4,8},{8,12},{12,16},{16,20},{20,24},{24,28},{1,5},{5,9},{9,... | collective-permute-start | bytes 24584 | tf_op jit(solution)/shard_map/ppermute | solution.py:313
  7.7 15.0 %collective-permute-start.3 = (bf16[32,256]{1,0:T(8,128)(2,1)S(1)}, bf16[32,256]{1,0:T(8,128)(2,1)S(1)}, u32[]{:S(2)}, u32[]{:S(2)}) collective-permute-start(bf16[32,256]{1,0:T(8,128)(2,1)S(1)} %pad_maximum_fusion.1), channel_id=1, source_target_pairs={{0,1},{1,2},{2,3},{4,5},{5,6},{6,7},{8,9},{9,10},{10,11},{12,13},{... | collective-permute-start | bytes 49160 | tf_op jit(solution)/shard_map/ppermute | solution.py:313
  12.7 10.0 %collective-permute-start.2 = (bf16[32,256]{1,0:T(8,128)(2,1)S(1)}, bf16[32,256]{1,0:T(8,128)(2,1)S(1)}, u32[]{:S(2)}, u32[]{:S(2)}) collective-permute-start(bf16[32,256]{1,0:T(8,128)(2,1)S(1)} %pad_maximum_fusion), channel_id=1, source_target_pairs={{1,0},{2,1},{3,2},{5,4},{6,5},{7,6},{9,8},{10,9},{11,10},{13,12},{... | collective-permute-start | bytes 49160 | tf_op jit(solution)/shard_map/ppermute | solution.py:313
  14.0 1.0 %copy-start.3 = (f32[8,2,64,64]{3,2,1,0:T(8,128)S(1)}, f32[8,2,64,64]{3,2,1,0:T(8,128)}, u32[]{:S(2)}) copy-start(f32[8,2,64,64]{3,2,1,0:T(8,128)} %param.19) | copy-start | bytes 786436
  15.0 0.7 %copy-start.4 = (s32[2,128]{1,0:T(2,128)S(1)}, s32[2,128]{1,0:T(2,128)}, u32[]{:S(2)}) copy-start(s32[2,128]{1,0:T(2,128)} %refs_4_.1) | copy-start | bytes 3076
  15.7 0.7 %copy-start.6 = (s32[128]{0:T(128)S(1)}, s32[128]{0:T(128)}, u32[]{:S(2)}) copy-start(s32[128]{0:T(128)} %param.22) | copy-start | bytes 1540
  16.4 0.9 %copy-start.10 = (bf16[256,512]{1,0:T(8,128)(2,1)S(1)}, bf16[256,512]{1,0:T(8,128)(2,1)}, u32[]{:S(2)}) copy-start(bf16[256,512]{1,0:T(8,128)(2,1)} %constant.38.clone.refs_2_) | copy-start | bytes 786436
  17.3 0.9 %copy-start.13 = (bf16[192,256]{1,0:T(8,128)(2,1)S(1)}, bf16[192,256]{1,0:T(8,128)(2,1)}, u32[]{:S(2)}) copy-start(bf16[192,256]{1,0:T(8,128)(2,1)} %constant.37.clone.refs_1_) | copy-start | bytes 294916
  18.2 4.5 %copy-start = (bf16[128,128]{1,0:T(8,128)(2,1)S(1)}, bf16[128,128]{1,0:T(8,128)(2,1)}, u32[]{:S(2)}) copy-start(bf16[128,128]{1,0:T(8,128)(2,1)} %light_ref.1) | copy-start | bytes 98308
  18.2 4.5 %copy-start.1 = (s32[128,128]{1,0:T(8,128)S(1)}, s32[128,128]{1,0:T(8,128)}, u32[]{:S(2)}) copy-start(s32[128,128]{1,0:T(8,128)} %raster_ref.1) | copy-start | bytes 196612
  18.2 4.5 %copy-start.5 = (f32[8]{0:T(128)S(1)}, f32[8]{0:T(128)}, u32[]{:S(2)}) copy-start(f32[8]{0:T(128)} %weight_ref.1) | copy-start | bytes 100
  18.2 4.5 %copy-start.8 = (bf16[2,256,512]{2,1,0:T(8,128)(2,1)S(1)}, bf16[2,256,512]{2,1,0:T(8,128)(2,1)}, u32[]{:S(2)}) copy-start(bf16[2,256,512]{2,1,0:T(8,128)(2,1)} %constant.44.cols_in_ref) | copy-start | bytes 1572868
  18.2 4.5 %copy-start.9 = (bf16[2,256,256]{2,1,0:T(8,128)(2,1)S(1)}, bf16[2,256,256]{2,1,0:T(8,128)(2,1)}, u32[]{:S(2)}) copy-start(bf16[2,256,256]{2,1,0:T(8,128)(2,1)} %constant.47.cols_out_ref) | copy-start | bytes 786436
  18.2 4.5 %copy-start.11 = (bf16[2,192,256]{2,1,0:T(8,128)(2,1)S(1)}, bf16[2,192,256]{2,1,0:T(8,128)(2,1)}, u32[]{:S(2)}) copy-start(bf16[2,192,256]{2,1,0:T(8,128)(2,1)} %constant.41.rows_in_ref) | copy-start | bytes 589828
  18.2 4.5 %copy-start.12 = (bf16[2,128,256]{2,1,0:T(8,128)(2,1)S(1)}, bf16[2,128,256]{2,1,0:T(8,128)(2,1)}, u32[]{:S(2)}) copy-start(bf16[2,128,256]{2,1,0:T(8,128)(2,1)} %constant.50.rows_out_ref) | copy-start | bytes 393220
  22.7 17.6 %copy-start.2 = (bf16[2048,256]{1,0:T(8,128)(2,1)S(1)}, bf16[2048,256]{1,0:T(8,128)(2,1)}, u32[]{:S(2)}) copy-start(bf16[2048,256]{1,0:T(8,128)(2,1)} %library_ref.1) | copy-start | bytes 3145732
  30.6 20.0 %copy-start.7 = (s32[128]{0:T(128)S(1)}, s32[128]{0:T(128)}, u32[]{:S(2)}) copy-start(s32[128]{0:T(128)} %param.22) | copy-start | bytes 1540
  30.6 20.0 %all-to-all-start = ((bf16[32,16,256]{2,1,0:T(8,128)(2,1)}), bf16[32,16,256]{2,1,0:T(8,128)(2,1)S(1)}, u32[]{:S(2)}, u32[]{:S(2)}) async-start(bf16[32,16,256]{2,1,0:T(8,128)(2,1)} %get-tuple-element.11), calls=%async_computation | async-start | bytes 524288 | tf_op jit(solution)/shard_map/all_to_all | solution.py:408
where the time goes:
time: 62.6 us; the launch traced here: 62 us
  starting transfers between devices  20.3 us (32%)
  Pallas kernels  14.1 us (23%)
  blocking collectives  9.67 us (15%)
  waiting for transfers between devices  9.59 us (15%)
  local copies, waits for them, and re-layouts  4.34 us (7%)
  other arithmetic  3.16 us (5%)
  between operations  0.85 us (1%)
    pallas_call x4, Pallas kernels, call(): pl.pallas_call(body, out_shape=out_shape, in_specs=specs, out_specs=jax.t...  14.1 us
    all_to_all x1, starting transfers between devices, per_device(): lax.all_to_all(copies, both, 0, 0, tiled=True)  9.73 us
    all_to_all x1, blocking collectives, per_device(): lax.all_to_all(slab, both, 0, 0, tiled=True)[:, :clip_count // device_count]  9.67 us
    all_to_all x1, waiting for transfers between devices, per_device(): lax.all_to_all(copies, both, 0, 0, tiled=True)  9.55 us
    ppermute x2, starting transfers between devices, exchanged(): lax.ppermute(high_edge, axis, forward)  7.99 us
    unnamed x28, local copies, waits for them, and re-layouts  4.26 us
    ppermute x2, starting transfers between devices, exchanged(): lax.ppermute(low_edge, axis, backward)  2.58 us
    mul x2, other arithmetic, masked(): return raster[rows, cols].astype(bf16) * transmission[rows, cols]  1.64 us
  transfers between devices with their start and end apart: 5, of which 1 were waited for; matrix products, arithmetic and copies ran while one was open for 1% of the time, Pallas kernels for 8%

commit v1 on v0

--- a/solution.py
+++ b/solution.py
@@ -115,29 +115,88 @@
     return jnp.where(inside, weight * (series * x), 0.0)
 
 
-def filters_body(
-    cols_wide, taps_ref, rows_ref, cols_ref, tile_ref, corner_ref, out_ref, rb_ref, cb_ref
-):
-    real_count = out_ref.shape[0]
+def edges_body(raster_hbm, light_hbm, mask_ref, low_ref, high_ref, raster_ref, light_ref, sems):
+    tile = mask_ref.shape[0]
+    border = low_ref.shape[1]
+    copies = [
+        pltpu.make_async_copy(raster_hbm, raster_ref, sems.at[0]),
+        pltpu.make_async_copy(light_hbm, light_ref, sems.at[1]),
+    ]
+    for copy in copies:
+        copy.start()
+    for copy in copies:
+        copy.wait()
+    mask = (raster_ref[...].astype(f32) * light_ref[...].astype(f32)).astype(bf16)
+    mask_ref[...] = mask
+    low_ref[...] = mask[:, :border]
+    high_ref[...] = mask[:, tile - border :]
+
+
+def transform_taps(first, count, taps_ref, rows_ref, cols_ref, out_ref, mixed_ref):
     half = out_ref.shape[2]
     wide = out_ref.shape[3]
 
-    def one(index, carry):
-        taps = taps_ref[index]
+    def along_rows(index):
+        taps = taps_ref[first + index]
         spread = jnp.concatenate([taps, taps, taps, taps], axis=1)
         high, low = split(spread)
         stacked = jnp.concatenate([high, high, low, low], axis=0)
         rows = dot(rows_ref[...], stacked)
         kept = rows.astype(bf16).astype(f32)
         is_low = (iota(rows.shape, 1) & KSIZE) != 0
-        mixed = jnp.where(is_low, rows - kept, rows).astype(bf16)
-        both = dot(mixed, cols_ref[...])
+        mixed_ref[index % 2] = jnp.where(is_low, rows - kept, rows).astype(bf16)
+
+    def along_cols(index):
+        both = dot(mixed_ref[index % 2], cols_ref[...])
         out_ref[index, 0] = both[:half, :wide] - both[half:, wide:]
         out_ref[index, 1] = both[:half, wide:] + both[half:, :wide]
-        return carry
-
-    lax.fori_loop(0, real_count, one, 0, unroll=2)
-
+
+    along_rows(0)
+    for index in range(count):
+        if index + 1 < count:
+            along_rows(index + 1)
+        along_cols(index)
+
+
+def first_body(taps_hbm, rows_hbm, cols_hbm, out_ref, taps_ref, rows_ref, cols_ref, mixed_ref, sems):
+    copies = [
+        pltpu.make_async_copy(source, target, sems.at[index])
+        for index, (source, target) in enumerate(
+            ((taps_hbm, taps_ref), (rows_hbm, rows_ref), (cols_hbm, cols_ref))
+        )
+    ]
+    for copy in copies:
+        copy.start()
+    for copy in copies:
+        copy.wait()
+    transform_taps(0, out_ref.shape[0], taps_ref, rows_ref, cols_ref, out_ref, mixed_ref)
+
+
+def second_body(
+    first,
+    cols_wide,
+    taps_ref,
+    rows_ref,
+    cols_ref,
+    tile_hbm,
+    corner_hbm,
+    out_ref,
+    rb_ref,
+    cb_ref,
+    mixed_ref,
+    tile_ref,
+    corner_ref,
+    sems,
+):
+    copies = [
+        pltpu.make_async_copy(tile_hbm, tile_ref, sems.at[0]),
+        pltpu.make_async_copy(corner_hbm, corner_ref, sems.at[1]),
+    ]
+    for copy in copies:
+        copy.start()
+    transform_taps(first, out_ref.shape[0], taps_ref, rows_ref, cols_ref, out_ref, mixed_ref)
+    for copy in copies:
+        copy.wait()
     clip_count = tile_ref.shape[1]
     own_tile = lax.axis_index("narrow") * cols_wide + lax.axis_index("wide")
     owned = tile_ref[...] == own_tile
@@ -161,13 +220,13 @@
 
 
 def image_body(
-    raster_ref,
-    light_ref,
+    own_ref,
     side_ref,
     after_ref,
     before_ref,
     weight_ref,
-    filter_ref,
+    early_ref,
+    late_ref,
     rb_ref,
     cb_ref,
     rows_in_ref,
@@ -180,54 +239,76 @@
     spec_ref,
     prod_ref,
     mid_ref,
+    sum_ref,
 ):
-    tile = raster_ref.shape[0]
-    half = filter_ref.shape[2]
+    tile = own_ref.shape[0]
+    half = early_ref.shape[2]
     full = 2 * half
-    wide = filter_ref.shape[3]
+    wide = early_ref.shape[3]
     border = KSIZE // 2
-    mask_ref[:tile, :tile] = (raster_ref[...].astype(f32) * light_ref[...].astype(f32)).astype(bf16)
+    early = early_ref.shape[0]
+    kernel_count = (early + late_ref.shape[0]) // 2
+    mask_ref[:tile, :tile] = own_ref[...]
     mask_ref[:tile, tile:] = side_ref[...]
     mask_ref[tile : tile + border, :] = after_ref[...]
     mask_ref[tile + border : full, :] = before_ref[...]
     mask_ref[full:, :] = jnp.zeros((wide - full, wide), bf16)
+    for index in range(2):
+        mid_ref[index, :, full:, :] = jnp.zeros((2, wide - full, wide), bf16)
     mask = mask_ref[...]
     rows = dot(rows_in_ref[0], mask) + dot(rows_in_ref[1], mask)
     both = dot3(split(rows), (cols_in_ref[0], cols_in_ref[1]))
     spec_ref[0] = both[:half, :wide] + both[half:, wide:]
     spec_ref[1] = both[half:, :wide] - both[:half, wide:]
-    aerial_ref[...] = jnp.zeros_like(aerial_ref)
-    mid_ref[:, full:, :] = jnp.zeros((2, wide - full, wide), bf16)
-
-    def one(index, carry):
+
+    def multiply(index):
+        place = prod_ref.at[index % 2]
         for part in range(2):
-            real = filter_ref[2 * index + part, 0]
-            imag = filter_ref[2 * index + part, 1]
+            number = 2 * index + part
+            ref = early_ref.at[number] if number < early else late_ref.at[number - early]
             base = part * full
-            high, low = split(spec_ref[0] * real - spec_ref[1] * imag)
-            prod_ref[0, base : base + half] = high
-            prod_ref[1, base : base + half] = low
-            high, low = split(spec_ref[0] * imag + spec_ref[1] * real)
-            prod_ref[0, base + half : base + full] = high
-            prod_ref[1, base + half : base + full] = low
-        cols = dot3((prod_ref[0], prod_ref[1]), (cols_out_ref[0], cols_out_ref[1]))
+            high, low = split(spec_ref[0] * ref[0] - spec_ref[1] * ref[1])
+            place[0, base : base + half] = high
+            place[1, base : base + half] = low
+            high, low = split(spec_ref[0] * ref[1] + spec_ref[1] * ref[0])
+            place[0, base + half : base + full] = high
+            place[1, base + half : base + full] = low
+
+    def along_cols(index):
+        place = mid_ref.at[index % 2]
+        source = prod_ref.at[index % 2]
+        cols = dot3((source[0], source[1]), (cols_out_ref[0], cols_out_ref[1]))
         for part in range(2):
             base = part * full
             lane = part * tile
             real = cols[base : base + half]
             imag = cols[base + half : base + full]
             high, low = split(real[:, :tile] - imag[:, tile:])
-            mid_ref[0, :half, lane : lane + tile] = high
-            mid_ref[1, :half, lane : lane + tile] = low
+            place[0, :half, lane : lane + tile] = high
+            place[1, :half, lane : lane + tile] = low
             high, low = split(imag[:, :tile] + real[:, tile:])
-            mid_ref[0, half:full, lane : lane + tile] = high
-            mid_ref[1, half:full, lane : lane + tile] = low
-        field = dot3((rows_out_ref[0], rows_out_ref[1]), (mid_ref[0], mid_ref[1]))
+            place[0, half:full, lane : lane + tile] = high
+            place[1, half:full, lane : lane + tile] = low
+
+    def along_rows(index):
+        source = mid_ref.at[index % 2]
+        field = dot3((rows_out_ref[0], rows_out_ref[1]), (source[0], source[1]))
         energy = field * field
-        aerial_ref[...] += weight_ref[index] * (energy[:, :tile] + energy[:, tile:])
-        return carry
-
-    lax.fori_loop(0, filter_ref.shape[0] // 2, one, 0, unroll=2)
+        value = weight_ref[index] * (energy[:, :tile] + energy[:, tile:])
+        if index == 0:
+            sum_ref[...] = value
+        elif index == kernel_count - 1:
+            aerial_ref[...] = sum_ref[...] + value
+        else:
+            sum_ref[...] += value
+
+    for step in range(kernel_count + 2):
+        if step < kernel_count:
+            multiply(step)
+        if 0 <= step - 1 < kernel_count:
+            along_cols(step - 1)
+        if 0 <= step - 2:
+            along_rows(step - 2)
 
     halfway = dot3((rb_ref[0], rb_ref[1]), split(aerial_ref[...]))
     crossed = dot3_t(split(halfway), (cb_ref[0], cb_ref[1]))
@@ -289,15 +370,17 @@
     out_ref[...] = sent
 
 
-def call(body, out_shape, operands, scratch=(), limit=24, smem=(), flops=0, name=None):
-    specs = [
-        pl.BlockSpec(memory_space=pltpu.SMEM) if index in smem else VMEM_SPEC
+def call(
+    body, out_shape, operands, scratch=(), limit=24, smem=(), hbm=(), flops=0, name=None
+):
+    spaces = [
+        pltpu.SMEM if index in smem else pltpu.HBM if index in hbm else pltpu.VMEM
         for index in range(len(operands))
     ]
     return pl.pallas_call(
         body,
         out_shape=out_shape,
-        in_specs=specs,
+        in_specs=[pl.BlockSpec(memory_space=space) for space in spaces],
         out_specs=jax.tree.map(lambda _: VMEM_SPEC, out_shape),
         scratch_shapes=list(scratch),
         compiler_params=pltpu.CompilerParams(vmem_limit_bytes=limit << 20),
@@ -330,42 +413,78 @@
     device_count = cols_wide * rows_narrow
     both = ("wide", "narrow")
     clip_count = clip_tile.shape[0]
-    kernel_count = kernels.shape[0]
-
-    def masked(rows, cols):
-        return raster[rows, cols].astype(bf16) * transmission[rows, cols]
-
-    every = slice(None)
-    left, right = exchanged(
-        masked(every, slice(0, border)), masked(every, slice(tile - border, tile)), "wide"
-    )
+    real_count = 2 * kernels.shape[0]
+
+    mask, low_edge, high_edge = call(
+        edges_body,
+        (
+            jax.ShapeDtypeStruct((tile, tile), bf16),
+            jax.ShapeDtypeStruct((tile, border), bf16),
+            jax.ShapeDtypeStruct((tile, border), bf16),
+        ),
+        (raster, transmission),
+        scratch=(
+            pltpu.VMEM((tile, tile), jnp.int32),
+            pltpu.VMEM((tile, tile), bf16),
+            pltpu.SemaphoreType.DMA((2,)),
+        ),
+        hbm=(0, 1),
+        limit=8,
+        name="edges",
+    )
+    left, right = exchanged(low_edge, high_edge, "wide")
+
+    early = real_count // 2
+    spectrum = (2, half, wide)
+    mixed = pltpu.VMEM((2, full, 4 * KSIZE), bf16)
+    early_filters, taps, taps_rows, taps_cols = call(
+        first_body,
+        (
+            jax.ShapeDtypeStruct((early,) + spectrum, f32),
+            jax.ShapeDtypeStruct((real_count, KSIZE, KSIZE), f32),
+            jax.ShapeDtypeStruct(table["taps_rows"].shape, bf16),
+            jax.ShapeDtypeStruct(table["taps_cols"].shape, bf16),
+        ),
+        (
+            kernels.reshape(real_count, KSIZE, KSIZE),
+            table["taps_rows"],
+            table["taps_cols"],
+        ),
+        scratch=(mixed, pltpu.SemaphoreType.DMA((3,))),
+        hbm=(0, 1, 2),
+        flops=2 << 30,
+        name="first",
+    )
+    left, right, early_filters = lax.optimization_barrier((left, right, early_filters))
+
     side = jnp.concatenate([right, left, jnp.zeros((tile, wide - full), bf16)], axis=1)
     top = slice(0, border)
     bottom = slice(tile - border, tile)
     before, after = exchanged(
-        jnp.concatenate([masked(top, every), side[top]], axis=1),
-        jnp.concatenate([masked(bottom, every), side[bottom]], axis=1),
+        jnp.concatenate([mask[top], side[top]], axis=1),
+        jnp.concatenate([mask[bottom], side[bottom]], axis=1),
         "narrow",
     )
 
     tile_line = clip_tile.reshape(1, clip_count)
     basis = jax.ShapeDtypeStruct((2, CAP * KSIG, tile), bf16)
-    filters, row_basis, col_basis = call(
-        lambda *refs: filters_body(cols_wide, *refs),
+    late_filters, row_basis, col_basis = call(
+        lambda *refs: second_body(early, cols_wide, *refs),
         (
-            jax.ShapeDtypeStruct((2 * kernel_count, 2, half, wide), f32),
+            jax.ShapeDtypeStruct((real_count - early,) + spectrum, f32),
             basis,
             basis,
         ),
-        (
-            kernels.reshape(2 * kernel_count, KSIZE, KSIZE),
-            table["taps_rows"],
-            table["taps_cols"],
-            tile_line,
-            clip_corner,
-        ),
-        flops=3 << 30,
-        name="filters",
+        (taps, taps_rows, taps_cols, tile_line, clip_corner),
+        scratch=(
+            mixed,
+            pltpu.VMEM((1, clip_count), jnp.int32),
+            pltpu.VMEM((2, clip_count), jnp.int32),
+            pltpu.SemaphoreType.DMA((2,)),
+        ),
+        hbm=(3, 4),
+        flops=2 << 30,
+        name="second",
     )
     aerial, copies = call(
         image_body,
@@ -374,13 +493,13 @@
             jax.ShapeDtypeStruct((device_count, CAP, SIGD), bf16),
         ),
         (
-            raster,
-            transmission,
+            mask,
             side,
             after,
             before,
             kernel_weight,
-            filters,
+            early_filters,
+            late_filters,
             row_basis,
             col_basis,
             table["rows_in"],
@@ -390,11 +509,12 @@
         ),
         scratch=(
             pltpu.VMEM((wide, wide), bf16),
-            pltpu.VMEM((2, half, wide), f32),
-            pltpu.VMEM((2, 2 * full, wide), bf16),
-            pltpu.VMEM((2, wide, wide), bf16),
-        ),
-        smem=(5,),
+            pltpu.VMEM(spectrum, f32),
+            pltpu.VMEM((2, 2, 2 * full, wide), bf16),
+            pltpu.VMEM((2, 2, wide, wide), bf16),
+            pltpu.VMEM((tile, tile), f32),
+        ),
+        smem=(4,),
         flops=6 << 30,
         name="image",
     )

time: 62.6 us -> 55.4 us (0.88)
  Pallas kernels: 14.1 us -> 10.3 us
  other arithmetic: 3.16 us -> 0.67 us
  starting transfers between devices: 20.3 us -> 19.1 us
    pallas_call x4 -> x6, Pallas kernels: 14.1 us -> 10.3 us  [call(): pl.pallas_call(body, out_shape=out_shape, in_specs=[pl.BlockSpec(memory_s...]
    mul x2 -> x0, other arithmetic: 1.64 us -> none  [masked(): return raster[rows, cols].astype(bf16) * transmission[rows, cols]]
    another operation x1 -> x0, other arithmetic: 0.85 us -> none
    ppermute x2, starting transfers between devices: 7.99 us -> 7.33 us  [exchanged(): lax.ppermute(high_edge, axis, forward)]
    unnamed x28 -> x26, local copies, waits for them, and re-layouts: 4.26 us -> 4.52 us
  transfers between devices with their start and end apart: 5 -> 5, of which waited for: 1 -> 1; matrix products, arithmetic and copies ran while one was open for 1% -> 0% of each run, Pallas kernels for 8% -> 6%
where the time goes in v1:
time: 55.4 us; the launch traced here: 54.9 us
  starting transfers between devices  19.1 us (34%)
  Pallas kernels  10.3 us (19%)
  blocking collectives  9.67 us (17%)
  waiting for transfers between devices  9.56 us (17%)
  local copies, waits for them, and re-layouts  4.6 us (8%)
  between operations  0.9 us (2%)
  other arithmetic  0.67 us (1%)
    pallas_call x6, Pallas kernels, call(): pl.pallas_call(body, out_shape=out_shape, in_specs=[pl.BlockSpec(memory_s...  10.3 us
    all_to_all x1, blocking collectives, per_device(): lax.all_to_all(slab, both, 0, 0, tiled=True)[:, :clip_count // device_count]  9.67 us
    all_to_all x1, waiting for transfers between devices, per_device(): lax.all_to_all(copies, both, 0, 0, tiled=True)  9.55 us
    all_to_all x1, starting transfers between devices, per_device(): lax.all_to_all(copies, both, 0, 0, tiled=True)  9.2 us
    ppermute x2, starting transfers between devices, exchanged(): lax.ppermute(high_edge, axis, forward)  7.33 us
    unnamed x26, local copies, waits for them, and re-layouts  4.52 us
    ppermute x2, starting transfers between devices, exchanged(): lax.ppermute(low_edge, axis, backward)  2.58 us
  transfers between devices with their start and end apart: 5, of which 1 were waited for; matrix products, arithmetic and copies ran while one was open for 0% of the time, Pallas kernels for 6%

profile of v1, /device:TPU:0, one launch (start us, length us, event | category | flops | bytes accessed | tf_op | source)
XLA Modules:
  0.0 54.9 jit_solution(2782744271440750979)
XLA Ops:
  0.6 0.8 %copy-done = s32[128,128]{1,0:T(8,128)S(1)} copy-done((s32[128,128]{1,0:T(8,128)S(1)}, s32[128,128]{1,0:T(8,128)}, u32[]{:S(2)}) %copy-start) | copy-done | bytes 65560
  1.5 0.8 %copy-done.1 = bf16[128,128]{1,0:T(8,128)(2,1)S(1)} copy-done((bf16[128,128]{1,0:T(8,128)(2,1)S(1)}, bf16[128,128]{1,0:T(8,128)(2,1)}, u32[]{:S(2)}) %copy-start.1) | copy-done | bytes 32792
  2.2 0.2 edges.1
  2.4 2.4 %collective-permute-start = (bf16[128,32]{1,0:T(8,128)(2,1)S(1)}, bf16[128,32]{1,0:T(8,128)(2,1)S(1)}, u32[]{:S(2)}, u32[]{:S(2)}) collective-permute-start(bf16[128,32]{1,0:T(8,128)(2,1)S(1)} %get-tuple-element.18), channel_id=1, source_target_pairs={{0,4},{4,8},{8,12},{12,16},{16,20},{20,24},{24,28},{1,5},{5,9},{9,... | collective-permute-start | bytes 24584 | tf_op jit(solution)/shard_map/ppermute | solution.py:396
  4.8 1.3 %collective-permute-start.1 = (bf16[128,32]{1,0:T(8,128)(2,1)S(1)}, bf16[128,32]{1,0:T(8,128)(2,1)S(1)}, u32[]{:S(2)}, u32[]{:S(2)}) collective-permute-start(bf16[128,32]{1,0:T(8,128)(2,1)S(1)} %get-tuple-element.19), channel_id=1, source_target_pairs={{4,0},{8,4},{12,8},{16,12},{20,16},{24,20},{28,24},{5,1},{9,5},{13... | collective-permute-start | bytes 24584 | tf_op jit(solution)/shard_map/ppermute | solution.py:396
  6.2 1.0 %copy-done.3 = f32[8,2,64,64]{3,2,1,0:T(8,128)S(1)} copy-done((f32[8,2,64,64]{3,2,1,0:T(8,128)S(1)}, f32[8,2,64,64]{3,2,1,0:T(8,128)}, u32[]{:S(2)}) %copy-start.3) | copy-done | bytes 262168
  7.2 0.9 %copy-done.9 = bf16[256,512]{1,0:T(8,128)(2,1)S(1)} copy-done((bf16[256,512]{1,0:T(8,128)(2,1)S(1)}, bf16[256,512]{1,0:T(8,128)(2,1)}, u32[]{:S(2)}) %copy-start.9) | copy-done | bytes 262168
  8.2 0.9 %copy-done.12 = bf16[192,256]{1,0:T(8,128)(2,1)S(1)} copy-done((bf16[192,256]{1,0:T(8,128)(2,1)S(1)}, bf16[192,256]{1,0:T(8,128)(2,1)}, u32[]{:S(2)}) %copy-start.12) | copy-done | bytes 98328
  9.0 1.2 %first.1 = (f32[8,2,96,256]{3,2,1,0:T(8,128)S(1)}, f32[16,64,64]{2,1,0:T(8,128)S(1)}, bf16[192,256]{1,0:T(8,128)(2,1)S(1)}, bf16[256,512]{1,0:T(8,128)(2,1)S(1)}) custom-call(f32[16,64,64]{2,1,0:T(8,128)S(1)} %bitcast.9, bf16[192,256]{1,0:T(8,128)(2,1)S(1)} %copy-done.12, bf16[256,512]{1,0:T(8,128)(2,1)S(1)} %copy-done.9), custom_call_target="tpu_custom_call" | custom-call | flops 2147483648 | bytes 1048576 | tf_op jit(solution)/shard_map/first/pallas_call | solution.py:380
  10.3 0.1 pad.6.clone
  10.4 0.1 maximum_maximum_fusion.side_ref
  10.5 1.3 %collective-permute-start.2 = (bf16[32,256]{1,0:T(8,128)(2,1)S(1)}, bf16[32,256]{1,0:T(8,128)(2,1)S(1)}, u32[]{:S(2)}, u32[]{:S(2)}) collective-permute-start(bf16[32,256]{1,0:T(8,128)(2,1)S(1)} %pad_maximum_fusion), channel_id=1, source_target_pairs={{1,0},{2,1},{3,2},{5,4},{6,5},{7,6},{9,8},{10,9},{11,10},{13,12},{... | collective-permute-start | bytes 49160 | tf_op jit(solution)/shard_map/ppermute | solution.py:396
  11.8 4.9 %collective-permute-start.3 = (bf16[32,256]{1,0:T(8,128)(2,1)S(1)}, bf16[32,256]{1,0:T(8,128)(2,1)S(1)}, u32[]{:S(2)}, u32[]{:S(2)}) collective-permute-start(bf16[32,256]{1,0:T(8,128)(2,1)S(1)} %pad_maximum_fusion.1), channel_id=1, source_target_pairs={{0,1},{1,2},{2,3},{4,5},{5,6},{6,7},{8,9},{9,10},{10,11},{12,13},{... | collective-permute-start | bytes 49160 | tf_op jit(solution)/shard_map/ppermute | solution.py:396
  16.8 0.0 copy-start.7
  16.8 0.0 copy-start.8
  16.8 0.0 copy-start.11
  16.8 1.6 %second.1 = (f32[8,2,96,256]{3,2,1,0:T(8,128)S(1)}, bf16[2,256,128]{2,1,0:T(8,128)(2,1)S(1)}, bf16[2,256,128]{2,1,0:T(8,128)(2,1)S(1)}) custom-call(f32[16,64,64]{2,1,0:T(8,128)S(1)} %get-tuple-element.24.refs_0_, bf16[192,256]{1,0:T(8,128)(2,1)S(1)} %get-tuple-element.25.refs_1_, bf16[256,512]{1,0:T(8,128)(2,1)S(1)} %get-tuple-element.26.refs_2_, ...), custom_call_target="tpu_custom_call" | custom-call | flops 2147483648 | bytes 1048576 | tf_op jit(solution)/shard_map/second/pallas_call | solution.py:380
  18.5 5.4 %image.1 = (f32[128,128]{1,0:T(8,128)}, bf16[32,16,256]{2,1,0:T(8,128)(2,1)}) custom-call(bf16[128,128]{1,0:T(8,128)(2,1)S(1)} %get-tuple-element.17.own_ref, bf16[128,128]{1,0:T(8,128)(2,1)S(1)} %maximum_maximum_fusion.side_ref, bf16[32,256]{1,0:T(8,128)(2,1)S(1)} %collective-permute-done.2.after_ref, ...), custom_call_target="tpu_custom_call" | custom-call | flops 6442450944 | bytes 1048576 | tf_op jit(solution)/shard_map/image/pallas_call | solution.py:380
  24.0 9.2 %all-to-all-start = ((bf16[32,16,256]{2,1,0:T(8,128)(2,1)}), bf16[32,16,256]{2,1,0:T(8,128)(2,1)S(1)}, u32[]{:S(2)}, u32[]{:S(2)}) async-start(bf16[32,16,256]{2,1,0:T(8,128)(2,1)} %get-tuple-element.31), calls=%async_computation | async-start | bytes 524288 | tf_op jit(solution)/shard_map/all_to_all | solution.py:528
  33.2 0.7 %library.1.refs_2_ = bf16[2048,256]{1,0:T(8,128)(2,1)S(1)} custom-call(bf16[2048,256]{1,0:T(8,128)(2,1)S(1)} %copy-done.2), custom_call_target="tpu_custom_call" | custom-call | flops 1073741824 | bytes 1048576 | tf_op jit(solution)/shard_map/library/pallas_call | solution.py:380
  33.8 9.6 %all-to-all-done = bf16[32,16,256]{2,1,0:T(8,128)(2,1)S(1)} async-done(((bf16[32,16,256]{2,1,0:T(8,128)(2,1)}), bf16[32,16,256]{2,1,0:T(8,128)(2,1)S(1)}, u32[]{:S(2)}, u32[]{:S(2)}) %all-to-all-start) | async-done | bytes 262176 | tf_op jit(solution)/shard_map/all_to_all | solution.py:528
  43.4 1.2 %match.1 = f32[32,128]{1,0:T(8,128)S(1)} custom-call(s32[1,128]{1,0:T(1,128)S(1)} %bitcast.11, bf16[512,256]{1,0:T(8,128)(2,1)S(1)} %bitcast.7, bf16[2048,256]{1,0:T(8,128)(2,1)S(1)} %library.1.refs_2_), custom_call_target="tpu_custom_call" | custom-call | flops 1073741824 | bytes 1048576 | tf_op jit(solution)/shard_map/match/pallas_call | solution.py:380
  44.6 9.7 %all_to_all.17 = f32[32,1,128]{2,1,0:T(1,128)S(1)} all-to-all(f32[32,1,128]{2,1,0:T(1,128)S(1)} %bitcast.8), channel_id=1, replica_groups=mesh['wide'=8,'narrow'=4] {'wide','narrow'}, dimensions={0} | all-to-all | bytes 32768 | tf_op jit(solution)/shard_map/all_to_all | solution.py:537
  54.3 0.5 negate_multiply_fusion
  (29 shorter events, 0.1 us)
Async XLA Ops:
  0.6 0.8 %copy-start = (s32[128,128]{1,0:T(8,128)S(1)}, s32[128,128]{1,0:T(8,128)}, u32[]{:S(2)}) copy-start(s32[128,128]{1,0:T(8,128)} %raster_hbm.1) | copy-start | bytes 196612
  1.5 0.8 %copy-start.1 = (bf16[128,128]{1,0:T(8,128)(2,1)S(1)}, bf16[128,128]{1,0:T(8,128)(2,1)}, u32[]{:S(2)}) copy-start(bf16[128,128]{1,0:T(8,128)(2,1)} %light_hbm.1) | copy-start | bytes 98308
  2.4 7.9 %collective-permute-start = (bf16[128,32]{1,0:T(8,128)(2,1)S(1)}, bf16[128,32]{1,0:T(8,128)(2,1)S(1)}, u32[]{:S(2)}, u32[]{:S(2)}) collective-permute-start(bf16[128,32]{1,0:T(8,128)(2,1)S(1)} %get-tuple-element.18), channel_id=1, source_target_pairs={{0,4},{4,8},{8,12},{12,16},{16,20},{20,24},{24,28},{1,5},{5,9},{9,... | collective-permute-start | bytes 24584 | tf_op jit(solution)/shard_map/ppermute | solution.py:396
  4.8 5.5 %collective-permute-start.1 = (bf16[128,32]{1,0:T(8,128)(2,1)S(1)}, bf16[128,32]{1,0:T(8,128)(2,1)S(1)}, u32[]{:S(2)}, u32[]{:S(2)}) collective-permute-start(bf16[128,32]{1,0:T(8,128)(2,1)S(1)} %get-tuple-element.19), channel_id=1, source_target_pairs={{4,0},{8,4},{12,8},{16,12},{20,16},{24,20},{28,24},{5,1},{9,5},{13... | collective-permute-start | bytes 24584 | tf_op jit(solution)/shard_map/ppermute | solution.py:396
  6.2 1.0 %copy-start.3 = (f32[8,2,64,64]{3,2,1,0:T(8,128)S(1)}, f32[8,2,64,64]{3,2,1,0:T(8,128)}, u32[]{:S(2)}) copy-start(f32[8,2,64,64]{3,2,1,0:T(8,128)} %param.19) | copy-start | bytes 786436
  7.2 0.9 %copy-start.9 = (bf16[256,512]{1,0:T(8,128)(2,1)S(1)}, bf16[256,512]{1,0:T(8,128)(2,1)}, u32[]{:S(2)}) copy-start(bf16[256,512]{1,0:T(8,128)(2,1)} %constant.38.clone.cols_hbm) | copy-start | bytes 786436
  8.1 0.9 %copy-start.12 = (bf16[192,256]{1,0:T(8,128)(2,1)S(1)}, bf16[192,256]{1,0:T(8,128)(2,1)}, u32[]{:S(2)}) copy-start(bf16[192,256]{1,0:T(8,128)(2,1)} %constant.37.clone.rows_hbm) | copy-start | bytes 294916
  9.0 7.7 %copy-start.4 = (s32[2,128]{1,0:T(2,128)S(1)}, s32[2,128]{1,0:T(2,128)}, u32[]{:S(2)}) copy-start(s32[2,128]{1,0:T(2,128)} %refs_4_.1) | copy-start | bytes 3076
  9.0 7.7 %copy-start.6 = (s32[128]{0:T(128)S(1)}, s32[128]{0:T(128)}, u32[]{:S(2)}) copy-start(s32[128]{0:T(128)} %param.22) | copy-start | bytes 1540
  10.5 8.0 %collective-permute-start.2 = (bf16[32,256]{1,0:T(8,128)(2,1)S(1)}, bf16[32,256]{1,0:T(8,128)(2,1)S(1)}, u32[]{:S(2)}, u32[]{:S(2)}) collective-permute-start(bf16[32,256]{1,0:T(8,128)(2,1)S(1)} %pad_maximum_fusion), channel_id=1, source_target_pairs={{1,0},{2,1},{3,2},{5,4},{6,5},{7,6},{9,8},{10,9},{11,10},{13,12},{... | collective-permute-start | bytes 49160 | tf_op jit(solution)/shard_map/ppermute | solution.py:396
  11.8 6.7 %collective-permute-start.3 = (bf16[32,256]{1,0:T(8,128)(2,1)S(1)}, bf16[32,256]{1,0:T(8,128)(2,1)S(1)}, u32[]{:S(2)}, u32[]{:S(2)}) collective-permute-start(bf16[32,256]{1,0:T(8,128)(2,1)S(1)} %pad_maximum_fusion.1), channel_id=1, source_target_pairs={{0,1},{1,2},{2,3},{4,5},{5,6},{6,7},{8,9},{9,10},{10,11},{12,13},{... | collective-permute-start | bytes 49160 | tf_op jit(solution)/shard_map/ppermute | solution.py:396
  16.7 1.7 %copy-start.5 = (f32[8]{0:T(128)S(1)}, f32[8]{0:T(128)}, u32[]{:S(2)}) copy-start(f32[8]{0:T(128)} %weight_ref.1) | copy-start | bytes 100
  16.8 1.7 %copy-start.7 = (bf16[2,256,512]{2,1,0:T(8,128)(2,1)S(1)}, bf16[2,256,512]{2,1,0:T(8,128)(2,1)}, u32[]{:S(2)}) copy-start(bf16[2,256,512]{2,1,0:T(8,128)(2,1)} %constant.44.cols_in_ref) | copy-start | bytes 1572868
  16.8 1.7 %copy-start.8 = (bf16[2,256,256]{2,1,0:T(8,128)(2,1)S(1)}, bf16[2,256,256]{2,1,0:T(8,128)(2,1)}, u32[]{:S(2)}) copy-start(bf16[2,256,256]{2,1,0:T(8,128)(2,1)} %constant.47.cols_out_ref) | copy-start | bytes 786436
  16.8 1.7 %copy-start.10 = (bf16[2,192,256]{2,1,0:T(8,128)(2,1)S(1)}, bf16[2,192,256]{2,1,0:T(8,128)(2,1)}, u32[]{:S(2)}) copy-start(bf16[2,192,256]{2,1,0:T(8,128)(2,1)} %constant.41.rows_in_ref) | copy-start | bytes 589828
  16.8 1.7 %copy-start.11 = (bf16[2,128,256]{2,1,0:T(8,128)(2,1)S(1)}, bf16[2,128,256]{2,1,0:T(8,128)(2,1)}, u32[]{:S(2)}) copy-start(bf16[2,128,256]{2,1,0:T(8,128)(2,1)} %constant.50.rows_out_ref) | copy-start | bytes 393220
  18.5 14.7 %copy-start.2 = (bf16[2048,256]{1,0:T(8,128)(2,1)S(1)}, bf16[2048,256]{1,0:T(8,128)(2,1)}, u32[]{:S(2)}) copy-start(bf16[2048,256]{1,0:T(8,128)(2,1)} %library_ref.1) | copy-start | bytes 3145732
  24.0 19.4 %all-to-all-start = ((bf16[32,16,256]{2,1,0:T(8,128)(2,1)}), bf16[32,16,256]{2,1,0:T(8,128)(2,1)S(1)}, u32[]{:S(2)}, u32[]{:S(2)}) async-start(bf16[32,16,256]{2,1,0:T(8,128)(2,1)} %get-tuple-element.31), calls=%async_computation | async-start | bytes 524288 | tf_op jit(solution)/shard_map/all_to_all | solution.py:528

commit v2 on v1

--- a/solution.py
+++ b/solution.py
@@ -14,6 +14,7 @@
 CAP = 16
 SIGD = KSIG * KSIG
 LANES = 128
+GROUP = 2
 
 sharpness = 400.0
 f32 = jnp.float32
@@ -253,18 +254,21 @@
     mask_ref[tile : tile + border, :] = after_ref[...]
     mask_ref[tile + border : full, :] = before_ref[...]
     mask_ref[full:, :] = jnp.zeros((wide - full, wide), bf16)
-    for index in range(2):
-        mid_ref[index, :, full:, :] = jnp.zeros((2, wide - full, wide), bf16)
+    for place in range(2):
+        for member in range(mid_ref.shape[1]):
+            mid_ref[place, member, :, full:, :] = jnp.zeros((2, wide - full, wide), bf16)
     mask = mask_ref[...]
     rows = dot(rows_in_ref[0], mask) + dot(rows_in_ref[1], mask)
     both = dot3(split(rows), (cols_in_ref[0], cols_in_ref[1]))
     spec_ref[0] = both[:half, :wide] + both[half:, wide:]
     spec_ref[1] = both[half:, :wide] - both[:half, wide:]
 
+    group = prod_ref.shape[2] // (2 * full)
+
     def multiply(index):
         place = prod_ref.at[index % 2]
-        for part in range(2):
-            number = 2 * index + part
+        for part in range(2 * group):
+            number = 2 * group * index + part
             ref = early_ref.at[number] if number < early else late_ref.at[number - early]
             base = part * full
             high, low = split(spec_ref[0] * ref[0] - spec_ref[1] * ref[1])
@@ -275,12 +279,12 @@
             place[1, base + half : base + full] = low
 
     def along_cols(index):
-        place = mid_ref.at[index % 2]
         source = prod_ref.at[index % 2]
         cols = dot3((source[0], source[1]), (cols_out_ref[0], cols_out_ref[1]))
-        for part in range(2):
+        for part in range(2 * group):
+            place = mid_ref.at[index % 2, part // 2]
             base = part * full
-            lane = part * tile
+            lane = part % 2 * tile
             real = cols[base : base + half]
             imag = cols[base + half : base + full]
             high, low = split(real[:, :tile] - imag[:, tile:])
@@ -291,21 +295,24 @@
             place[1, half:full, lane : lane + tile] = low
 
     def along_rows(index):
-        source = mid_ref.at[index % 2]
-        field = dot3((rows_out_ref[0], rows_out_ref[1]), (source[0], source[1]))
-        energy = field * field
-        value = weight_ref[index] * (energy[:, :tile] + energy[:, tile:])
+        value = None
+        for member in range(group):
+            source = mid_ref.at[index % 2, member]
+            field = dot3((rows_out_ref[0], rows_out_ref[1]), (source[0], source[1]))
+            energy = field * field
+            term = weight_ref[group * index + member] * (energy[:, :tile] + energy[:, tile:])
+            value = term if value is None else value + term
         if index == 0:
             sum_ref[...] = value
-        elif index == kernel_count - 1:
+        elif index == kernel_count // group - 1:
             aerial_ref[...] = sum_ref[...] + value
         else:
             sum_ref[...] += value
 
-    for step in range(kernel_count + 2):
-        if step < kernel_count:
+    for step in range(kernel_count // group + 2):
+        if step < kernel_count // group:
             multiply(step)
-        if 0 <= step - 1 < kernel_count:
+        if 0 <= step - 1 < kernel_count // group:
             along_cols(step - 1)
         if 0 <= step - 2:
             along_rows(step - 2)
@@ -386,7 +393,12 @@
         compiler_params=pltpu.CompilerParams(vmem_limit_bytes=limit << 20),
         cost_estimate=pl.CostEstimate(flops=flops, bytes_accessed=1 << 20, transcendentals=0),
         name=name,
-    )(*operands)
+    )(
+        *(
+            pltpu.with_memory_space_constraint(value, pltpu.HBM) if index in hbm else value
+            for index, value in enumerate(operands)
+        )
+    )
 
 
 def exchanged(low_edge, high_edge, axis):
@@ -510,8 +522,8 @@
         scratch=(
             pltpu.VMEM((wide, wide), bf16),
             pltpu.VMEM(spectrum, f32),
-            pltpu.VMEM((2, 2, 2 * full, wide), bf16),
-            pltpu.VMEM((2, 2, wide, wide), bf16),
+            pltpu.VMEM((2, 2, GROUP * 2 * full, wide), bf16),
+            pltpu.VMEM((2, GROUP, 2, wide, wide), bf16),
             pltpu.VMEM((tile, tile), f32),
         ),
         smem=(4,),

time: 55.4 us -> 51.9 us (0.937)
  local copies, waits for them, and re-layouts: 4.6 us -> 0.13 us
  waiting for transfers between devices: 9.56 us -> 11.2 us
  starting transfers between devices: 19.1 us -> 17.5 us
  Pallas kernels: 10.3 us -> 11.5 us
    unnamed x26 -> x14, local copies, waits for them, and re-layouts: 4.52 us -> 0.05 us
    ppermute x2, waiting for transfers between devices: 0.01 us -> 1.62 us  [exchanged(): lax.ppermute(low_edge, axis, backward)]
    all_to_all x1, starting transfers between devices: 9.2 us -> 8.01 us  [per_device(): lax.all_to_all(copies, both, 0, 0, tiled=True)]
    pallas_call x6, Pallas kernels: 10.3 us -> 11.5 us  [call(): pl.pallas_call(body, out_shape=out_shape, in_specs=[pl.BlockSpec(memory_s...]
  transfers between devices with their start and end apart: 5 -> 5, of which waited for: 1 -> 2; matrix products, arithmetic and copies ran while one was open for 0% -> 0% of each run, Pallas kernels for 6% -> 9%
where the time goes in v2:
time: 51.9 us; the launch traced here: 51.6 us
  starting transfers between devices  17.5 us (34%)
  Pallas kernels  11.5 us (22%)
  waiting for transfers between devices  11.2 us (22%)
  blocking collectives  9.67 us (19%)
  between operations  0.87 us (2%)
  other arithmetic  0.67 us (1%)
    pallas_call x6, Pallas kernels, call(): pl.pallas_call(body, out_shape=out_shape, in_specs=[pl.BlockSpec(memory_s...  11.5 us
    all_to_all x1, blocking collectives, per_device(): lax.all_to_all(slab, both, 0, 0, tiled=True)[:, :clip_count // device_count]  9.67 us
    all_to_all x1, waiting for transfers between devices, per_device(): lax.all_to_all(copies, both, 0, 0, tiled=True)  9.54 us
    all_to_all x1, starting transfers between devices, per_device(): lax.all_to_all(copies, both, 0, 0, tiled=True)  8.01 us
    ppermute x2, starting transfers between devices, exchanged(): lax.ppermute(high_edge, axis, forward)  6.95 us
    ppermute x2, starting transfers between devices, exchanged(): lax.ppermute(low_edge, axis, backward)  2.58 us
    ppermute x2, waiting for transfers between devices, exchanged(): lax.ppermute(low_edge, axis, backward)  1.62 us
  transfers between devices with their start and end apart: 5, of which 2 were waited for; matrix products, arithmetic and copies ran while one was open for 0% of the time, Pallas kernels for 9%

profile of v2, /device:TPU:0, one launch (start us, length us, event | category | flops | bytes accessed | tf_op | source)
XLA Modules:
  0.0 51.6 jit_solution(17515906677787911270)
XLA Ops:
  0.6 0.9 %edges.1 = (bf16[128,128]{1,0:T(8,128)(2,1)S(1)}, bf16[128,32]{1,0:T(8,128)(2,1)S(1)}, bf16[128,32]{1,0:T(8,128)(2,1)S(1)}) custom-call(s32[128,128]{1,0:T(8,128)} %raster_hbm.1, bf16[128,128]{1,0:T(8,128)(2,1)} %light_hbm.1), custom_call_target="tpu_custom_call" | custom-call | bytes 1048576 | tf_op jit(solution)/shard_map/edges/pallas_call | solution.py:387
  1.6 2.4 %collective-permute-start = (bf16[128,32]{1,0:T(8,128)(2,1)S(1)}, bf16[128,32]{1,0:T(8,128)(2,1)S(1)}, u32[]{:S(2)}, u32[]{:S(2)}) collective-permute-start(bf16[128,32]{1,0:T(8,128)(2,1)S(1)} %get-tuple-element.18), channel_id=1, source_target_pairs={{0,4},{4,8},{8,12},{12,16},{16,20},{20,24},{24,28},{1,5},{5,9},{9,... | collective-permute-start | bytes 24584 | tf_op jit(solution)/shard_map/ppermute | solution.py:408
  4.0 1.3 %collective-permute-start.1 = (bf16[128,32]{1,0:T(8,128)(2,1)S(1)}, bf16[128,32]{1,0:T(8,128)(2,1)S(1)}, u32[]{:S(2)}, u32[]{:S(2)}) collective-permute-start(bf16[128,32]{1,0:T(8,128)(2,1)S(1)} %get-tuple-element.19), channel_id=1, source_target_pairs={{4,0},{8,4},{12,8},{16,12},{20,16},{24,20},{28,24},{5,1},{9,5},{13... | collective-permute-start | bytes 24584 | tf_op jit(solution)/shard_map/ppermute | solution.py:408
  5.3 2.2 %first.1 = (f32[8,2,96,256]{3,2,1,0:T(8,128)S(1)}, f32[16,64,64]{2,1,0:T(8,128)S(1)}, bf16[192,256]{1,0:T(8,128)(2,1)S(1)}, bf16[256,512]{1,0:T(8,128)(2,1)S(1)}) custom-call(f32[16,64,64]{2,1,0:T(8,128)} %bitcast.13, bf16[192,256]{1,0:T(8,128)(2,1)} %constant.37.clone.rows_hbm, bf16[256,512]{1,0:T(8,128)(2,1)} %constant.38.clone.cols_hbm), custom_call_target="tpu_custom_call" | custom-call | flops 2147483648 | bytes 1048576 | tf_op jit(solution)/shard_map/first/pallas_call | solution.py:387
  7.5 0.1 pad.6.clone
  7.6 1.6 %collective-permute-done.1 = bf16[128,32]{1,0:T(8,128)(2,1)S(1)} collective-permute-done((bf16[128,32]{1,0:T(8,128)(2,1)S(1)}, bf16[128,32]{1,0:T(8,128)(2,1)S(1)}, u32[]{:S(2)}, u32[]{:S(2)}) %collective-permute-start.1) | collective-permute-done | bytes 8224 | tf_op jit(solution)/shard_map/ppermute | solution.py:408
  9.2 0.1 maximum_maximum_fusion.side_ref
  9.3 1.3 %collective-permute-start.2 = (bf16[32,256]{1,0:T(8,128)(2,1)S(1)}, bf16[32,256]{1,0:T(8,128)(2,1)S(1)}, u32[]{:S(2)}, u32[]{:S(2)}) collective-permute-start(bf16[32,256]{1,0:T(8,128)(2,1)S(1)} %pad_maximum_fusion), channel_id=1, source_target_pairs={{1,0},{2,1},{3,2},{5,4},{6,5},{7,6},{9,8},{10,9},{11,10},{13,12},{... | collective-permute-start | bytes 49160 | tf_op jit(solution)/shard_map/ppermute | solution.py:408
  10.6 4.5 %collective-permute-start.3 = (bf16[32,256]{1,0:T(8,128)(2,1)S(1)}, bf16[32,256]{1,0:T(8,128)(2,1)S(1)}, u32[]{:S(2)}, u32[]{:S(2)}) collective-permute-start(bf16[32,256]{1,0:T(8,128)(2,1)S(1)} %pad_maximum_fusion.1), channel_id=1, source_target_pairs={{0,1},{1,2},{2,3},{4,5},{5,6},{6,7},{8,9},{9,10},{10,11},{12,13},{... | collective-permute-start | bytes 49160 | tf_op jit(solution)/shard_map/ppermute | solution.py:408
  15.2 0.0 copy-start.1
  15.2 0.0 copy-start.3
  15.2 0.0 copy-start.4
  15.2 0.0 copy-start.5
  15.2 0.0 copy-start.6
  15.2 1.6 %second.1 = (f32[8,2,96,256]{3,2,1,0:T(8,128)S(1)}, bf16[2,256,128]{2,1,0:T(8,128)(2,1)S(1)}, bf16[2,256,128]{2,1,0:T(8,128)(2,1)S(1)}) custom-call(f32[16,64,64]{2,1,0:T(8,128)S(1)} %get-tuple-element.24.refs_0_, bf16[192,256]{1,0:T(8,128)(2,1)S(1)} %get-tuple-element.25.refs_1_, bf16[256,512]{1,0:T(8,128)(2,1)S(1)} %get-tuple-element.26.refs_2_, ...), custom_call_target="tpu_custom_call" | custom-call | flops 2147483648 | bytes 1048576 | tf_op jit(solution)/shard_map/second/pallas_call | solution.py:387
  16.9 0.0 copy-start
  16.9 4.9 %image.1 = (f32[128,128]{1,0:T(8,128)}, bf16[32,16,256]{2,1,0:T(8,128)(2,1)}) custom-call(bf16[128,128]{1,0:T(8,128)(2,1)S(1)} %get-tuple-element.17.own_ref, bf16[128,128]{1,0:T(8,128)(2,1)S(1)} %maximum_maximum_fusion.side_ref, bf16[32,256]{1,0:T(8,128)(2,1)S(1)} %collective-permute-done.2.after_ref, ...), custom_call_target="tpu_custom_call" | custom-call | flops 6442450944 | bytes 1048576 | tf_op jit(solution)/shard_map/image/pallas_call | solution.py:387
  21.8 8.0 %all-to-all-start = ((bf16[32,16,256]{2,1,0:T(8,128)(2,1)}), bf16[32,16,256]{2,1,0:T(8,128)(2,1)S(1)}, u32[]{:S(2)}, u32[]{:S(2)}) async-start(bf16[32,16,256]{2,1,0:T(8,128)(2,1)} %get-tuple-element.31), calls=%async_computation | async-start | bytes 524288 | tf_op jit(solution)/shard_map/all_to_all | solution.py:540
  29.9 0.0 copy-start.2
  29.9 0.7 %library.1.refs_2_ = bf16[2048,256]{1,0:T(8,128)(2,1)S(1)} custom-call(bf16[2048,256]{1,0:T(8,128)(2,1)S(1)} %copy-done), custom_call_target="tpu_custom_call" | custom-call | flops 1073741824 | bytes 1048576 | tf_op jit(solution)/shard_map/library/pallas_call | solution.py:387
  30.5 9.5 %all-to-all-done = bf16[32,16,256]{2,1,0:T(8,128)(2,1)S(1)} async-done(((bf16[32,16,256]{2,1,0:T(8,128)(2,1)}), bf16[32,16,256]{2,1,0:T(8,128)(2,1)S(1)}, u32[]{:S(2)}, u32[]{:S(2)}) %all-to-all-start) | async-done | bytes 262176 | tf_op jit(solution)/shard_map/all_to_all | solution.py:540
  40.1 1.2 %match.1 = f32[32,128]{1,0:T(8,128)S(1)} custom-call(s32[1,128]{1,0:T(1,128)S(1)} %bitcast.10, bf16[512,256]{1,0:T(8,128)(2,1)S(1)} %bitcast.7, bf16[2048,256]{1,0:T(8,128)(2,1)S(1)} %library.1.refs_2_), custom_call_target="tpu_custom_call" | custom-call | flops 1073741824 | bytes 1048576 | tf_op jit(solution)/shard_map/match/pallas_call | solution.py:387
  41.3 9.7 %all_to_all.17 = f32[32,1,128]{2,1,0:T(1,128)S(1)} all-to-all(f32[32,1,128]{2,1,0:T(1,128)S(1)} %bitcast.8), channel_id=1, replica_groups=mesh['wide'=8,'narrow'=4] {'wide','narrow'}, dimensions={0} | all-to-all | bytes 32768 | tf_op jit(solution)/shard_map/all_to_all | solution.py:549
  51.0 0.5 %negate_multiply_fusion = f32[4]{0:T(128)} fusion(f32[4]{0:T(128)S(1)} %slice_reduce_fusion, f32[4]{0:T(128)S(1)} %exponential_reduce_fusion), kind=kLoop, calls=%fused_computation.5 | loop fusion | flops 12 | bytes 48 | tf_op jit(solution)/shard_map/div | solution.py:552
  (17 shorter events, 0.1 us)
Async XLA Ops:
  1.6 6.0 %collective-permute-start = (bf16[128,32]{1,0:T(8,128)(2,1)S(1)}, bf16[128,32]{1,0:T(8,128)(2,1)S(1)}, u32[]{:S(2)}, u32[]{:S(2)}) collective-permute-start(bf16[128,32]{1,0:T(8,128)(2,1)S(1)} %get-tuple-element.18), channel_id=1, source_target_pairs={{0,4},{4,8},{8,12},{12,16},{16,20},{20,24},{24,28},{1,5},{5,9},{9,... | collective-permute-start | bytes 24584 | tf_op jit(solution)/shard_map/ppermute | solution.py:408
  4.0 5.2 %collective-permute-start.1 = (bf16[128,32]{1,0:T(8,128)(2,1)S(1)}, bf16[128,32]{1,0:T(8,128)(2,1)S(1)}, u32[]{:S(2)}, u32[]{:S(2)}) collective-permute-start(bf16[128,32]{1,0:T(8,128)(2,1)S(1)} %get-tuple-element.19), channel_id=1, source_target_pairs={{4,0},{8,4},{12,8},{16,12},{20,16},{24,20},{28,24},{5,1},{9,5},{13... | collective-permute-start | bytes 24584 | tf_op jit(solution)/shard_map/ppermute | solution.py:408
  9.3 7.6 %collective-permute-start.2 = (bf16[32,256]{1,0:T(8,128)(2,1)S(1)}, bf16[32,256]{1,0:T(8,128)(2,1)S(1)}, u32[]{:S(2)}, u32[]{:S(2)}) collective-permute-start(bf16[32,256]{1,0:T(8,128)(2,1)S(1)} %pad_maximum_fusion), channel_id=1, source_target_pairs={{1,0},{2,1},{3,2},{5,4},{6,5},{7,6},{9,8},{10,9},{11,10},{13,12},{... | collective-permute-start | bytes 49160 | tf_op jit(solution)/shard_map/ppermute | solution.py:408
  10.6 6.2 %collective-permute-start.3 = (bf16[32,256]{1,0:T(8,128)(2,1)S(1)}, bf16[32,256]{1,0:T(8,128)(2,1)S(1)}, u32[]{:S(2)}, u32[]{:S(2)}) collective-permute-start(bf16[32,256]{1,0:T(8,128)(2,1)S(1)} %pad_maximum_fusion.1), channel_id=1, source_target_pairs={{0,1},{1,2},{2,3},{4,5},{5,6},{6,7},{8,9},{9,10},{10,11},{12,13},{... | collective-permute-start | bytes 49160 | tf_op jit(solution)/shard_map/ppermute | solution.py:408
  15.2 1.7 %copy-start.1 = (f32[8]{0:T(128)S(1)}, f32[8]{0:T(128)}, u32[]{:S(2)}) copy-start(f32[8]{0:T(128)} %weight_ref.1) | copy-start | bytes 100
  15.2 1.7 %copy-start.3 = (bf16[2,256,512]{2,1,0:T(8,128)(2,1)S(1)}, bf16[2,256,512]{2,1,0:T(8,128)(2,1)}, u32[]{:S(2)}) copy-start(bf16[2,256,512]{2,1,0:T(8,128)(2,1)} %constant.44.cols_in_ref) | copy-start | bytes 1572868
  15.2 1.7 %copy-start.4 = (bf16[2,256,256]{2,1,0:T(8,128)(2,1)S(1)}, bf16[2,256,256]{2,1,0:T(8,128)(2,1)}, u32[]{:S(2)}) copy-start(bf16[2,256,256]{2,1,0:T(8,128)(2,1)} %constant.47.cols_out_ref) | copy-start | bytes 786436
  15.2 1.7 %copy-start.5 = (bf16[2,192,256]{2,1,0:T(8,128)(2,1)S(1)}, bf16[2,192,256]{2,1,0:T(8,128)(2,1)}, u32[]{:S(2)}) copy-start(bf16[2,192,256]{2,1,0:T(8,128)(2,1)} %constant.41.rows_in_ref) | copy-start | bytes 589828
  15.2 1.7 %copy-start.6 = (bf16[2,128,256]{2,1,0:T(8,128)(2,1)S(1)}, bf16[2,128,256]{2,1,0:T(8,128)(2,1)}, u32[]{:S(2)}) copy-start(bf16[2,128,256]{2,1,0:T(8,128)(2,1)} %constant.50.rows_out_ref) | copy-start | bytes 393220
  16.9 12.9 %copy-start = (bf16[2048,256]{1,0:T(8,128)(2,1)S(1)}, bf16[2048,256]{1,0:T(8,128)(2,1)}, u32[]{:S(2)}) copy-start(bf16[2048,256]{1,0:T(8,128)(2,1)} %library_ref.1) | copy-start | bytes 3145732
  21.8 18.2 %all-to-all-start = ((bf16[32,16,256]{2,1,0:T(8,128)(2,1)}), bf16[32,16,256]{2,1,0:T(8,128)(2,1)S(1)}, u32[]{:S(2)}, u32[]{:S(2)}) async-start(bf16[32,16,256]{2,1,0:T(8,128)(2,1)} %get-tuple-element.31), calls=%async_computation | async-start | bytes 524288 | tf_op jit(solution)/shard_map/all_to_all | solution.py:540
  29.9 10.2 %copy-start.2 = (s32[128]{0:T(128)S(1)}, s32[128]{0:T(128)}, u32[]{:S(2)}) copy-start(s32[128]{0:T(128)} %param.22) | copy-start | bytes 1540

commit v3 on v2

--- a/solution.py
+++ b/solution.py
@@ -116,29 +116,62 @@
     return jnp.where(inside, weight * (series * x), 0.0)
 
 
-def edges_body(raster_hbm, light_hbm, mask_ref, low_ref, high_ref, raster_ref, light_ref, sems):
-    tile = mask_ref.shape[0]
-    border = low_ref.shape[1]
+def neighbours():
+    return [(dw, dz) for dw in (-1, 0, 1) for dz in (-1, 0, 1) if dw or dz]
+
+
+def fetched(pairs, sems):
     copies = [
-        pltpu.make_async_copy(raster_hbm, raster_ref, sems.at[0]),
-        pltpu.make_async_copy(light_hbm, light_ref, sems.at[1]),
+        pltpu.make_async_copy(source, target, sems.at[index])
+        for index, (source, target) in enumerate(pairs)
     ]
     for copy in copies:
         copy.start()
+    return copies
+
+
+def edges_body(cols_wide, rows_narrow, raster_hbm, light_hbm, mask_ref, sent_ref, raster_ref, light_ref, sems):
+    tile = mask_ref.shape[0]
+    border = sent_ref.shape[1]
+    copies = fetched(((raster_hbm, raster_ref), (light_hbm, light_ref)), sems)
+    sent_ref[...] = jnp.zeros_like(sent_ref)
     for copy in copies:
         copy.wait()
-    mask = (raster_ref[...].astype(f32) * light_ref[...].astype(f32)).astype(bf16)
-    mask_ref[...] = mask
-    low_ref[...] = mask[:, :border]
-    high_ref[...] = mask[:, tile - border :]
-
-
-def transform_taps(first, count, taps_ref, rows_ref, cols_ref, out_ref, mixed_ref):
+    mask = raster_ref[...].astype(f32) * light_ref[...].astype(f32)
+    mask_ref[...] = mask.astype(bf16)
+    lane = iota((border, tile), 1)
+
+    def folded(first):
+        out = jnp.zeros((border, tile), f32)
+        for block in range(tile // border):
+            low = block * border
+            moved = pltpu.roll(mask[low : low + border], (low - first) % tile, 1)
+            out = jnp.where((lane >= low) & (lane < low + border), moved, out)
+        return out.astype(bf16)
+
+    top = mask[:border].astype(bf16)
+    bottom = mask[tile - border :].astype(bf16)
+    low_cols = folded(0)
+    high_cols = folded(tile - border)
+    col = lax.axis_index("wide")
+    row = lax.axis_index("narrow")
+    for dw, dz in neighbours():
+        strip = top if dz < 0 else bottom if dz > 0 else low_cols if dw < 0 else high_cols
+        there = (col + dw >= 0) & (col + dw < cols_wide)
+        there &= (row + dz >= 0) & (row + dz < rows_narrow)
+
+        @pl.when(there)
+        def _():
+            sent_ref[(col + dw) * rows_narrow + row + dz] = strip
+
+
+def transform_taps(taps_ref, rows_ref, cols_ref, out_ref, mixed_ref, finished):
+    count = out_ref.shape[0]
     half = out_ref.shape[2]
     wide = out_ref.shape[3]
 
     def along_rows(index):
-        taps = taps_ref[first + index]
+        taps = taps_ref[index]
         spread = jnp.concatenate([taps, taps, taps, taps], axis=1)
         high, low = split(spread)
         stacked = jnp.concatenate([high, high, low, low], axis=0)
@@ -151,6 +184,7 @@
         both = dot(mixed_ref[index % 2], cols_ref[...])
         out_ref[index, 0] = both[:half, :wide] - both[half:, wide:]
         out_ref[index, 1] = both[:half, wide:] + both[half:, :wide]
+        finished[index].start()
 
     along_rows(0)
     for index in range(count):
@@ -159,45 +193,40 @@
         along_cols(index)
 
 
-def first_body(taps_hbm, rows_hbm, cols_hbm, out_ref, taps_ref, rows_ref, cols_ref, mixed_ref, sems):
-    copies = [
-        pltpu.make_async_copy(source, target, sems.at[index])
-        for index, (source, target) in enumerate(
-            ((taps_hbm, taps_ref), (rows_hbm, rows_ref), (cols_hbm, cols_ref))
-        )
-    ]
-    for copy in copies:
-        copy.start()
-    for copy in copies:
-        copy.wait()
-    transform_taps(0, out_ref.shape[0], taps_ref, rows_ref, cols_ref, out_ref, mixed_ref)
-
-
-def second_body(
-    first,
+def filters_body(
     cols_wide,
+    taps_hbm,
+    rows_hbm,
+    cols_hbm,
+    tile_hbm,
+    corner_hbm,
+    out_hbm,
+    rb_ref,
+    cb_ref,
+    out_ref,
+    mixed_ref,
     taps_ref,
     rows_ref,
     cols_ref,
-    tile_hbm,
-    corner_hbm,
-    out_ref,
-    rb_ref,
-    cb_ref,
-    mixed_ref,
     tile_ref,
     corner_ref,
     sems,
+    out_sems,
 ):
-    copies = [
-        pltpu.make_async_copy(tile_hbm, tile_ref, sems.at[0]),
-        pltpu.make_async_copy(corner_hbm, corner_ref, sems.at[1]),
+    pairs = (
+        (taps_hbm, taps_ref),
+        (rows_hbm, rows_ref),
+        (cols_hbm, cols_ref),
+        (tile_hbm, tile_ref),
+        (corner_hbm, corner_ref),
+    )
+    for copy in fetched(pairs, sems):
+        copy.wait()
+    finished = [
+        pltpu.make_async_copy(out_ref.at[index], out_hbm.at[index], out_sems.at[index])
+        for index in range(out_ref.shape[0])
     ]
-    for copy in copies:
-        copy.start()
-    transform_taps(first, out_ref.shape[0], taps_ref, rows_ref, cols_ref, out_ref, mixed_ref)
-    for copy in copies:
-        copy.wait()
+    transform_taps(taps_ref, rows_ref, cols_ref, out_ref, mixed_ref, finished)
     clip_count = tile_ref.shape[1]
     own_tile = lax.axis_index("narrow") * cols_wide + lax.axis_index("wide")
     owned = tile_ref[...] == own_tile
@@ -218,16 +247,17 @@
         high, low = split(shifted_basis(corner.astype(jnp.int32), tile))
         basis_ref[0] = high
         basis_ref[1] = low
+    for copy in finished:
+        copy.wait()
 
 
 def image_body(
+    cols_wide,
+    rows_narrow,
     own_ref,
-    side_ref,
-    after_ref,
-    before_ref,
+    got_ref,
     weight_ref,
-    early_ref,
-    late_ref,
+    filter_hbm,
     rb_ref,
     cb_ref,
     rows_in_ref,
@@ -241,18 +271,46 @@
     prod_ref,
     mid_ref,
     sum_ref,
+    filter_ref,
+    sems,
 ):
     tile = own_ref.shape[0]
-    half = early_ref.shape[2]
+    half = filter_ref.shape[2]
     full = 2 * half
-    wide = early_ref.shape[3]
+    wide = filter_ref.shape[3]
     border = KSIZE // 2
-    early = early_ref.shape[0]
-    kernel_count = (early + late_ref.shape[0]) // 2
+    kernel_count = filter_ref.shape[0] // 2
+    group = prod_ref.shape[2] // (2 * full)
+    parts = [
+        (filter_hbm.at[pl.ds(first, 2 * group)], filter_ref.at[pl.ds(first, 2 * group)])
+        for first in range(0, 2 * kernel_count, 2 * group)
+    ]
+    arriving = fetched(parts, sems)
+    col = lax.axis_index("wide")
+    row = lax.axis_index("narrow")
+    lane = iota((border, tile), 1)
+
+    def from_neighbour(dw, dz):
+        there = (col + dw >= 0) & (col + dw < cols_wide)
+        there &= (row + dz >= 0) & (row + dz < rows_narrow)
+        place = jnp.where(there, (col + dw) * rows_narrow + row + dz, 0)
+        return jnp.where(there, got_ref[place].astype(f32), 0.0)
+
+    def beside(right, right_shift, left, left_shift):
+        right = pltpu.roll(right, right_shift % tile, 1)
+        left = pltpu.roll(left, left_shift % tile, 1)
+        return jnp.where(lane < border, right, jnp.where(lane < 2 * border, left, 0.0)).astype(bf16)
+
     mask_ref[:tile, :tile] = own_ref[...]
-    mask_ref[:tile, tile:] = side_ref[...]
-    mask_ref[tile : tile + border, :] = after_ref[...]
-    mask_ref[tile + border : full, :] = before_ref[...]
+    right = from_neighbour(1, 0)
+    left = from_neighbour(-1, 0)
+    for low in range(0, tile, border):
+        mask_ref[low : low + border, tile:] = beside(right, -low, left, border - low)
+    for low, dz in ((tile, 1), (tile + border, -1)):
+        mask_ref[low : low + border, :tile] = from_neighbour(0, dz).astype(bf16)
+        mask_ref[low : low + border, tile:] = beside(
+            from_neighbour(1, dz), 0, from_neighbour(-1, dz), 2 * border
+        )
     mask_ref[full:, :] = jnp.zeros((wide - full, wide), bf16)
     for place in range(2):
         for member in range(mid_ref.shape[1]):
@@ -263,13 +321,12 @@
     spec_ref[0] = both[:half, :wide] + both[half:, wide:]
     spec_ref[1] = both[half:, :wide] - both[:half, wide:]
 
-    group = prod_ref.shape[2] // (2 * full)
-
     def multiply(index):
+        arriving[index].wait()
         place = prod_ref.at[index % 2]
         for part in range(2 * group):
             number = 2 * group * index + part
-            ref = early_ref.at[number] if number < early else late_ref.at[number - early]
+            ref = filter_ref.at[number]
             base = part * full
             high, low = split(spec_ref[0] * ref[0] - spec_ref[1] * ref[1])
             place[0, base : base + half] = high
@@ -378,7 +435,7 @@
 
 
 def call(
-    body, out_shape, operands, scratch=(), limit=24, smem=(), hbm=(), flops=0, name=None
+    body, out_shape, operands, scratch=(), limit=24, smem=(), hbm=(), out=None, flops=0, name=None
 ):
     spaces = [
         pltpu.SMEM if index in smem else pltpu.HBM if index in hbm else pltpu.VMEM
@@ -388,7 +445,7 @@
         body,
         out_shape=out_shape,
         in_specs=[pl.BlockSpec(memory_space=space) for space in spaces],
-        out_specs=jax.tree.map(lambda _: VMEM_SPEC, out_shape),
+        out_specs=jax.tree.map(lambda _: VMEM_SPEC, out_shape) if out is None else out,
         scratch_shapes=list(scratch),
         compiler_params=pltpu.CompilerParams(vmem_limit_bytes=limit << 20),
         cost_estimate=pl.CostEstimate(flops=flops, bytes_accessed=1 << 20, transcendentals=0),
@@ -399,13 +456,6 @@
             for index, value in enumerate(operands)
         )
     )
-
-
-def exchanged(low_edge, high_edge, axis):
-    count = lax.axis_size(axis)
-    forward = [(i, i + 1) for i in range(count - 1)]
-    backward = [(target, source) for source, target in forward]
-    return lax.ppermute(high_edge, axis, forward), lax.ppermute(low_edge, axis, backward)
 
 
 def per_device(raster, transmission, kernels, kernel_weight, library, clip_tile, clip_corner):
@@ -427,12 +477,11 @@
     clip_count = clip_tile.shape[0]
     real_count = 2 * kernels.shape[0]
 
-    mask, low_edge, high_edge = call(
-        edges_body,
+    mask, sent = call(
+        lambda *refs: edges_body(cols_wide, rows_narrow, *refs),
         (
             jax.ShapeDtypeStruct((tile, tile), bf16),
-            jax.ShapeDtypeStruct((tile, border), bf16),
-            jax.ShapeDtypeStruct((tile, border), bf16),
+            jax.ShapeDtypeStruct((device_count, border, tile), bf16),
         ),
         (raster, transmission),
         scratch=(
@@ -441,77 +490,50 @@
             pltpu.SemaphoreType.DMA((2,)),
         ),
         hbm=(0, 1),
-        limit=8,
         name="edges",
     )
-    left, right = exchanged(low_edge, high_edge, "wide")
-
-    early = real_count // 2
+    got = lax.all_to_all(sent, both, 0, 0, tiled=True)
+
+    tile_line = clip_tile.reshape(1, clip_count)
     spectrum = (2, half, wide)
-    mixed = pltpu.VMEM((2, full, 4 * KSIZE), bf16)
-    early_filters, taps, taps_rows, taps_cols = call(
-        first_body,
-        (
-            jax.ShapeDtypeStruct((early,) + spectrum, f32),
-            jax.ShapeDtypeStruct((real_count, KSIZE, KSIZE), f32),
-            jax.ShapeDtypeStruct(table["taps_rows"].shape, bf16),
-            jax.ShapeDtypeStruct(table["taps_cols"].shape, bf16),
-        ),
+    basis = jax.ShapeDtypeStruct((2, CAP * KSIG, tile), bf16)
+    filters, row_basis, col_basis = call(
+        lambda *refs: filters_body(cols_wide, *refs),
+        (pltpu.HBM((real_count,) + spectrum, f32), basis, basis),
         (
             kernels.reshape(real_count, KSIZE, KSIZE),
             table["taps_rows"],
             table["taps_cols"],
-        ),
-        scratch=(mixed, pltpu.SemaphoreType.DMA((3,))),
-        hbm=(0, 1, 2),
-        flops=2 << 30,
-        name="first",
-    )
-    left, right, early_filters = lax.optimization_barrier((left, right, early_filters))
-
-    side = jnp.concatenate([right, left, jnp.zeros((tile, wide - full), bf16)], axis=1)
-    top = slice(0, border)
-    bottom = slice(tile - border, tile)
-    before, after = exchanged(
-        jnp.concatenate([mask[top], side[top]], axis=1),
-        jnp.concatenate([mask[bottom], side[bottom]], axis=1),
-        "narrow",
-    )
-
-    tile_line = clip_tile.reshape(1, clip_count)
-    basis = jax.ShapeDtypeStruct((2, CAP * KSIG, tile), bf16)
-    late_filters, row_basis, col_basis = call(
-        lambda *refs: second_body(early, cols_wide, *refs),
-        (
-            jax.ShapeDtypeStruct((real_count - early,) + spectrum, f32),
-            basis,
-            basis,
-        ),
-        (taps, taps_rows, taps_cols, tile_line, clip_corner),
+            tile_line,
+            clip_corner,
+        ),
         scratch=(
-            mixed,
+            pltpu.VMEM((real_count,) + spectrum, f32),
+            pltpu.VMEM((2, full, 4 * KSIZE), bf16),
+            pltpu.VMEM((real_count, KSIZE, KSIZE), f32),
+            pltpu.VMEM(table["taps_rows"].shape, bf16),
+            pltpu.VMEM(table["taps_cols"].shape, bf16),
             pltpu.VMEM((1, clip_count), jnp.int32),
             pltpu.VMEM((2, clip_count), jnp.int32),
-            pltpu.SemaphoreType.DMA((2,)),
-        ),
-        hbm=(3, 4),
-        flops=2 << 30,
-        name="second",
+            pltpu.SemaphoreType.DMA((5,)),
+            pltpu.SemaphoreType.DMA((real_count,)),
+        ),
+        hbm=(0, 1, 2, 3, 4),
+        out=(pl.BlockSpec(memory_space=pltpu.HBM), VMEM_SPEC, VMEM_SPEC),
+        flops=4 << 30,
+        name="filters",
     )
     aerial, copies = call(
-        image_body,
+        lambda *refs: image_body(cols_wide, rows_narrow, *refs),
         (
             jax.ShapeDtypeStruct((tile, tile), f32),
             jax.ShapeDtypeStruct((device_count, CAP, SIGD), bf16),
         ),
         (
             mask,
-            side,
-            after,
-            before,
+            got,
             kernel_weight,
-            early_filters,
-            late_filters,
+            filters,
             row_basis,
             col_basis,
             table["rows_in"],
@@ -525,8 +547,11 @@
             pltpu.VMEM((2, 2, GROUP * 2 * full, wide), bf16),
             pltpu.VMEM((2, GROUP, 2, wide, wide), bf16),
             pltpu.VMEM((tile, tile), f32),
-        ),
-        smem=(4,),
+            pltpu.VMEM((real_count,) + spectrum, f32),
+            pltpu.SemaphoreType.DMA((real_count // (2 * GROUP),)),
+        ),
+        smem=(2,),
+        hbm=(3,),
         flops=6 << 30,
         name="image",
     )

time: 51.9 us -> 51.8 us (level)
  starting transfers between devices: 17.5 us -> 10 us
  waiting for transfers between devices: 11.2 us -> 15.7 us
  Pallas kernels: 11.5 us -> 14.7 us
    ppermute x4 -> x0, starting transfers between devices: 9.53 us -> none  [the longest x2 6.95 us: exchanged(): lax.ppermute(high_edge, axis, forward)]
    all_to_all x0 -> x1, starting transfers between devices: none -> 7.33 us  [per_device(): got = lax.all_to_all(sent, both, 0, 0, tiled=True)]
    all_to_all x0 -> x1, waiting for transfers between devices: none -> 6.11 us  [per_device(): got = lax.all_to_all(sent, both, 0, 0, tiled=True)]
    all_to_all x1, starting transfers between devices: 8.01 us -> 2.67 us  [per_device(): lax.all_to_all(copies, both, 0, 0, tiled=True)]
    pallas_call x6 -> x5, Pallas kernels: 11.5 us -> 14.7 us  [call(): pl.pallas_call(body, out_shape=out_shape, in_specs=[pl.BlockSpec(memory_s...]
    ppermute x4 -> x0, waiting for transfers between devices: 1.63 us -> none  [the longest x2 1.62 us: exchanged(): lax.ppermute(low_edge, axis, backward)]
  transfers between devices with their start and end apart: 5 -> 2, of which waited for: 2 -> 2; matrix products, arithmetic and copies ran while one was open for 0% -> 0% of each run, Pallas kernels for 9% -> 9%
where the time goes in v3:
time: 51.8 us; the launch traced here: 51.4 us
  waiting for transfers between devices  15.7 us (30%)
  Pallas kernels  14.7 us (28%)
  starting transfers between devices  10 us (19%)
  blocking collectives  9.67 us (19%)
  between operations  0.77 us (1%)
  other arithmetic  0.58 us (1%)
    pallas_call x5, Pallas kernels, call(): pl.pallas_call(body, out_shape=out_shape, in_specs=[pl.BlockSpec(memory_s...  14.7 us
    all_to_all x1, blocking collectives, per_device(): lax.all_to_all(slab, both, 0, 0, tiled=True)[:, :clip_count // device_count]  9.67 us
    all_to_all x1, waiting for transfers between devices, per_device(): lax.all_to_all(copies, both, 0, 0, tiled=True)  9.55 us
    all_to_all x1, starting transfers between devices, per_device(): got = lax.all_to_all(sent, both, 0, 0, tiled=True)  7.33 us
    all_to_all x1, waiting for transfers between devices, per_device(): got = lax.all_to_all(sent, both, 0, 0, tiled=True)  6.11 us
    all_to_all x1, starting transfers between devices, per_device(): lax.all_to_all(copies, both, 0, 0, tiled=True)  2.67 us
  transfers between devices with their start and end apart: 2, of which 2 were waited for; matrix products, arithmetic and copies ran while one was open for 0% of the time, Pallas kernels for 9%

profile of v3, /device:TPU:0, one launch (start us, length us, event | category | flops | bytes accessed | tf_op | source)
XLA Modules:
  0.0 51.4 jit_solution(1617354886909891234)
XLA Ops:
  0.6 1.7 %edges.1 = (bf16[128,128]{1,0:T(8,128)(2,1)S(1)}, bf16[32,32,128]{2,1,0:T(8,128)(2,1)}) custom-call(s32[128,128]{1,0:T(8,128)} %refs_0_.1, bf16[128,128]{1,0:T(8,128)(2,1)} %refs_1_.2), custom_call_target="tpu_custom_call" | custom-call | bytes 1048576 | tf_op jit(solution)/shard_map/edges/pallas_call | solution.py:444
  2.3 7.3 %all-to-all-start = ((bf16[32,32,128]{2,1,0:T(8,128)(2,1)}), bf16[32,32,128]{2,1,0:T(8,128)(2,1)S(1)}, u32[]{:S(2)}, u32[]{:S(2)}) async-start(bf16[32,32,128]{2,1,0:T(8,128)(2,1)} %get-tuple-element.10), calls=%async_computation | async-start | bytes 524288 | tf_op jit(solution)/shard_map/all_to_all | solution.py:495
  9.7 0.0 copy-start.1
  9.7 0.0 copy-start.3
  9.7 0.0 copy-start.4
  9.7 0.0 copy-start.5
  9.7 0.0 copy-start.6
  9.7 4.0 %filters.1 = (f32[16,2,96,256]{3,2,1,0:T(8,128)}, bf16[2,256,128]{2,1,0:T(8,128)(2,1)S(1)}, bf16[2,256,128]{2,1,0:T(8,128)(2,1)S(1)}) custom-call(f32[16,64,64]{2,1,0:T(8,128)} %bitcast.13, bf16[192,256]{1,0:T(8,128)(2,1)} %constant.35.clone.refs_1_, bf16[256,512]{1,0:T(8,128)(2,1)} %constant.36.clone.refs_2_, s32[1,128]{1,0:T(1,128)} %bitcast.9, ...), custom_call_target="tpu_custom_call" | custom-call | flops 4294967296 | bytes 1048576 | tf_op jit(solution)/shard_map/filters/pallas_call | solution.py:444
  13.8 6.1 %all-to-all-done.refs_1_ = bf16[32,32,128]{2,1,0:T(8,128)(2,1)S(1)} async-done(((bf16[32,32,128]{2,1,0:T(8,128)(2,1)}), bf16[32,32,128]{2,1,0:T(8,128)(2,1)S(1)}, u32[]{:S(2)}, u32[]{:S(2)}) %all-to-all-start) | async-done | bytes 262176 | tf_op jit(solution)/shard_map/all_to_all | solution.py:495
  19.9 0.0 copy-done.1
  19.9 0.0 copy-done.3
  19.9 0.0 copy-done.4
  19.9 0.0 copy-done.5
  19.9 0.0 copy-done.6
  19.9 0.0 copy-start
  19.9 7.1 %image.1 = (f32[128,128]{1,0:T(8,128)}, bf16[32,16,256]{2,1,0:T(8,128)(2,1)}) custom-call(bf16[128,128]{1,0:T(8,128)(2,1)S(1)} %get-tuple-element.9.refs_0_, bf16[32,32,128]{2,1,0:T(8,128)(2,1)S(1)} %all-to-all-done.refs_1_, f32[8]{0:T(128)S(1)} %copy-done.1, f32[16,2,96,256]{3,2,1,0:T(8,128)} %get-tuple-element.11.refs_3_, ...), custom_call_target="tpu_custom_call" | custom-call | flops 6442450944 | bytes 1048576 | tf_op jit(solution)/shard_map/image/pallas_call | solution.py:444
  27.1 0.0 copy-start.2
  27.1 2.7 %all-to-all-start.1 = ((bf16[32,16,256]{2,1,0:T(8,128)(2,1)}), bf16[32,16,256]{2,1,0:T(8,128)(2,1)S(1)}, u32[]{:S(2)}, u32[]{:S(2)}) async-start(bf16[32,16,256]{2,1,0:T(8,128)(2,1)} %get-tuple-element.15), calls=%async_computation.1 | async-start | bytes 524288 | tf_op jit(solution)/shard_map/all_to_all | solution.py:565
  29.7 0.7 %library.1.refs_2_ = bf16[2048,256]{1,0:T(8,128)(2,1)S(1)} custom-call(bf16[2048,256]{1,0:T(8,128)(2,1)S(1)} %copy-done), custom_call_target="tpu_custom_call" | custom-call | flops 1073741824 | bytes 1048576 | tf_op jit(solution)/shard_map/library/pallas_call | solution.py:444
  30.4 9.6 %all-to-all-done.1 = bf16[32,16,256]{2,1,0:T(8,128)(2,1)S(1)} async-done(((bf16[32,16,256]{2,1,0:T(8,128)(2,1)}), bf16[32,16,256]{2,1,0:T(8,128)(2,1)S(1)}, u32[]{:S(2)}, u32[]{:S(2)}) %all-to-all-start.1) | async-done | bytes 262176 | tf_op jit(solution)/shard_map/all_to_all | solution.py:565
  40.0 0.0 copy-done.2
  40.0 1.2 %match.1 = f32[32,128]{1,0:T(8,128)S(1)} custom-call(s32[1,128]{1,0:T(1,128)S(1)} %bitcast.10, bf16[512,256]{1,0:T(8,128)(2,1)S(1)} %bitcast.7, bf16[2048,256]{1,0:T(8,128)(2,1)S(1)} %library.1.refs_2_), custom_call_target="tpu_custom_call" | custom-call | flops 1073741824 | bytes 1048576 | tf_op jit(solution)/shard_map/match/pallas_call | solution.py:444
  41.2 9.7 %all_to_all.22 = f32[32,1,128]{2,1,0:T(1,128)S(1)} all-to-all(f32[32,1,128]{2,1,0:T(1,128)S(1)} %bitcast.8), channel_id=1, replica_groups=mesh['wide'=8,'narrow'=4] {'wide','narrow'}, dimensions={0} | all-to-all | bytes 32768 | tf_op jit(solution)/shard_map/all_to_all | solution.py:574
  50.9 0.5 %negate_multiply_fusion = f32[4]{0:T(128)} fusion(f32[4]{0:T(128)S(1)} %slice_reduce_fusion, f32[4]{0:T(128)S(1)} %exponential_reduce_fusion), kind=kLoop, calls=%fused_computation.2 | loop fusion | flops 12 | bytes 48 | tf_op jit(solution)/shard_map/div | solution.py:577
  (3 shorter events, 0.1 us)
Async XLA Ops:
  2.3 17.6 %all-to-all-start = ((bf16[32,32,128]{2,1,0:T(8,128)(2,1)}), bf16[32,32,128]{2,1,0:T(8,128)(2,1)S(1)}, u32[]{:S(2)}, u32[]{:S(2)}) async-start(bf16[32,32,128]{2,1,0:T(8,128)(2,1)} %get-tuple-element.10), calls=%async_computation | async-start | bytes 524288 | tf_op jit(solution)/shard_map/all_to_all | solution.py:495
  9.7 10.2 %copy-start.1 = (f32[8]{0:T(128)S(1)}, f32[8]{0:T(128)}, u32[]{:S(2)}) copy-start(f32[8]{0:T(128)} %refs_2_.2) | copy-start | bytes 100
  9.7 10.2 %copy-start.3 = (bf16[2,256,512]{2,1,0:T(8,128)(2,1)S(1)}, bf16[2,256,512]{2,1,0:T(8,128)(2,1)}, u32[]{:S(2)}) copy-start(bf16[2,256,512]{2,1,0:T(8,128)(2,1)} %constant.42.refs_7_) | copy-start | bytes 1572868
  9.7 10.2 %copy-start.4 = (bf16[2,256,256]{2,1,0:T(8,128)(2,1)S(1)}, bf16[2,256,256]{2,1,0:T(8,128)(2,1)}, u32[]{:S(2)}) copy-start(bf16[2,256,256]{2,1,0:T(8,128)(2,1)} %constant.45.refs_8_) | copy-start | bytes 786436
  9.7 10.2 %copy-start.5 = (bf16[2,192,256]{2,1,0:T(8,128)(2,1)S(1)}, bf16[2,192,256]{2,1,0:T(8,128)(2,1)}, u32[]{:S(2)}) copy-start(bf16[2,192,256]{2,1,0:T(8,128)(2,1)} %constant.39.refs_6_) | copy-start | bytes 589828
  9.7 10.2 %copy-start.6 = (bf16[2,128,256]{2,1,0:T(8,128)(2,1)S(1)}, bf16[2,128,256]{2,1,0:T(8,128)(2,1)}, u32[]{:S(2)}) copy-start(bf16[2,128,256]{2,1,0:T(8,128)(2,1)} %constant.48.refs_9_) | copy-start | bytes 393220
  19.9 9.8 %copy-start = (bf16[2048,256]{1,0:T(8,128)(2,1)S(1)}, bf16[2048,256]{1,0:T(8,128)(2,1)}, u32[]{:S(2)}) copy-start(bf16[2048,256]{1,0:T(8,128)(2,1)} %library_ref.1) | copy-start | bytes 3145732
  27.1 12.9 %copy-start.2 = (s32[128]{0:T(128)S(1)}, s32[128]{0:T(128)}, u32[]{:S(2)}) copy-start(s32[128]{0:T(128)} %param.22) | copy-start | bytes 1540
  27.1 12.9 %all-to-all-start.1 = ((bf16[32,16,256]{2,1,0:T(8,128)(2,1)}), bf16[32,16,256]{2,1,0:T(8,128)(2,1)S(1)}, u32[]{:S(2)}, u32[]{:S(2)}) async-start(bf16[32,16,256]{2,1,0:T(8,128)(2,1)} %get-tuple-element.15), calls=%async_computation.1 | async-start | bytes 524288 | tf_op jit(solution)/shard_map/all_to_all | solution.py:565

commit v4 on v3

--- a/solution.py
+++ b/solution.py
@@ -130,11 +130,22 @@
     return copies
 
 
-def edges_body(cols_wide, rows_narrow, raster_hbm, light_hbm, mask_ref, sent_ref, raster_ref, light_ref, sems):
+def edges_body(
+    cols_wide,
+    rows_narrow,
+    raster_hbm,
+    light_hbm,
+    mask_ref,
+    sent_hbm,
+    raster_ref,
+    light_ref,
+    strip_ref,
+    sems,
+    sent_sems,
+):
     tile = mask_ref.shape[0]
-    border = sent_ref.shape[1]
+    border = sent_hbm.shape[1]
     copies = fetched(((raster_hbm, raster_ref), (light_hbm, light_ref)), sems)
-    sent_ref[...] = jnp.zeros_like(sent_ref)
     for copy in copies:
         copy.wait()
     mask = raster_ref[...].astype(f32) * light_ref[...].astype(f32)
@@ -149,29 +160,36 @@
             out = jnp.where((lane >= low) & (lane < low + border), moved, out)
         return out.astype(bf16)
 
-    top = mask[:border].astype(bf16)
-    bottom = mask[tile - border :].astype(bf16)
-    low_cols = folded(0)
-    high_cols = folded(tile - border)
+    strip_ref[0] = mask[:border].astype(bf16)
+    strip_ref[1] = mask[tile - border :].astype(bf16)
+    strip_ref[2] = folded(0)
+    strip_ref[3] = folded(tile - border)
     col = lax.axis_index("wide")
     row = lax.axis_index("narrow")
-    for dw, dz in neighbours():
-        strip = top if dz < 0 else bottom if dz > 0 else low_cols if dw < 0 else high_cols
+    sends = []
+    for index, (dw, dz) in enumerate(neighbours()):
+        strip = 0 if dz < 0 else 1 if dz > 0 else 2 if dw < 0 else 3
         there = (col + dw >= 0) & (col + dw < cols_wide)
         there &= (row + dz >= 0) & (row + dz < rows_narrow)
-
-        @pl.when(there)
-        def _():
-            sent_ref[(col + dw) * rows_narrow + row + dz] = strip
-
-
-def transform_taps(taps_ref, rows_ref, cols_ref, out_ref, mixed_ref, finished):
+        place = jnp.where(there, (col + dw) * rows_narrow + row + dz, 0)
+        copy = pltpu.make_async_copy(
+            strip_ref.at[strip], sent_hbm.at[place], sent_sems.at[index]
+        )
+        sends.append((there, copy))
+    for there, copy in sends:
+        pl.when(there)(copy.start)
+    for there, copy in sends:
+        pl.when(there)(copy.wait)
+
+
+def transform_taps(weight_ref, taps_ref, rows_ref, cols_ref, out_ref, mixed_ref, finished):
     count = out_ref.shape[0]
     half = out_ref.shape[2]
     wide = out_ref.shape[3]
 
     def along_rows(index):
         taps = taps_ref[index]
+        taps = taps * jnp.sqrt(jnp.full(taps.shape, weight_ref[index // 2], f32))
         spread = jnp.concatenate([taps, taps, taps, taps], axis=1)
         high, low = split(spread)
         stacked = jnp.concatenate([high, high, low, low], axis=0)
@@ -195,6 +213,7 @@
 
 def filters_body(
     cols_wide,
+    weight_ref,
     taps_hbm,
     rows_hbm,
     cols_hbm,
@@ -226,7 +245,7 @@
         pltpu.make_async_copy(out_ref.at[index], out_hbm.at[index], out_sems.at[index])
         for index in range(out_ref.shape[0])
     ]
-    transform_taps(taps_ref, rows_ref, cols_ref, out_ref, mixed_ref, finished)
+    transform_taps(weight_ref, taps_ref, rows_ref, cols_ref, out_ref, mixed_ref, finished)
     clip_count = tile_ref.shape[1]
     own_tile = lax.axis_index("narrow") * cols_wide + lax.axis_index("wide")
     owned = tile_ref[...] == own_tile
@@ -256,7 +275,6 @@
     rows_narrow,
     own_ref,
     got_ref,
-    weight_ref,
     filter_hbm,
     rb_ref,
     cb_ref,
@@ -281,11 +299,16 @@
     border = KSIZE // 2
     kernel_count = filter_ref.shape[0] // 2
     group = prod_ref.shape[2] // (2 * full)
-    parts = [
-        (filter_hbm.at[pl.ds(first, 2 * group)], filter_ref.at[pl.ds(first, 2 * group)])
-        for first in range(0, 2 * kernel_count, 2 * group)
-    ]
-    arriving = fetched(parts, sems)
+
+    def arriving(index):
+        part = pl.ds(index * 2 * group, 2 * group)
+        return pltpu.make_async_copy(filter_hbm.at[part], filter_ref.at[part], sems.at[index])
+
+    def request(index, carry):
+        arriving(index).start()
+        return carry
+
+    lax.fori_loop(0, kernel_count // group, request, 0)
     col = lax.axis_index("wide")
     row = lax.axis_index("narrow")
     lane = iota((border, tile), 1)
@@ -322,7 +345,7 @@
     spec_ref[1] = both[half:, :wide] - both[:half, wide:]
 
     def multiply(index):
-        arriving[index].wait()
+        arriving(index).wait()
         place = prod_ref.at[index % 2]
         for part in range(2 * group):
             number = 2 * group * index + part
@@ -357,7 +380,7 @@
             source = mid_ref.at[index % 2, member]
             field = dot3((rows_out_ref[0], rows_out_ref[1]), (source[0], source[1]))
             energy = field * field
-            term = weight_ref[group * index + member] * (energy[:, :tile] + energy[:, tile:])
+            term = energy[:, :tile] + energy[:, tile:]
             value = term if value is None else value + term
         if index == 0:
             sum_ref[...] = value
@@ -481,14 +504,17 @@
         lambda *refs: edges_body(cols_wide, rows_narrow, *refs),
         (
             jax.ShapeDtypeStruct((tile, tile), bf16),
-            jax.ShapeDtypeStruct((device_count, border, tile), bf16),
+            pltpu.HBM((device_count, border, tile), bf16),
         ),
         (raster, transmission),
         scratch=(
             pltpu.VMEM((tile, tile), jnp.int32),
             pltpu.VMEM((tile, tile), bf16),
+            pltpu.VMEM((4, border, tile), bf16),
             pltpu.SemaphoreType.DMA((2,)),
+            pltpu.SemaphoreType.DMA((8,)),
         ),
+        out=(VMEM_SPEC, pl.BlockSpec(memory_space=pltpu.HBM)),
         hbm=(0, 1),
         name="edges",
     )
@@ -501,6 +527,7 @@
         lambda *refs: filters_body(cols_wide, *refs),
         (pltpu.HBM((real_count,) + spectrum, f32), basis, basis),
         (
+            kernel_weight,
             kernels.reshape(real_count, KSIZE, KSIZE),
             table["taps_rows"],
             table["taps_cols"],
@@ -518,7 +545,8 @@
             pltpu.SemaphoreType.DMA((5,)),
             pltpu.SemaphoreType.DMA((real_count,)),
         ),
-        hbm=(0, 1, 2, 3, 4),
+        smem=(0,),
+        hbm=(1, 2, 3, 4, 5),
         out=(pl.BlockSpec(memory_space=pltpu.HBM), VMEM_SPEC, VMEM_SPEC),
         flops=4 << 30,
         name="filters",
@@ -532,7 +560,6 @@
         (
             mask,
             got,
-            kernel_weight,
             filters,
             row_basis,
             col_basis,
@@ -550,8 +577,7 @@
             pltpu.VMEM((real_count,) + spectrum, f32),
             pltpu.SemaphoreType.DMA((real_count // (2 * GROUP),)),
         ),
-        smem=(2,),
-        hbm=(3,),
+        hbm=(2,),
         flops=6 << 30,
         name="image",
     )

time: 51.8 us -> 50.7 us (0.979)
  waiting for transfers between devices: 15.7 us -> 14.6 us
  local copies, waits for them, and re-layouts: 0.05 us -> 0.68 us
  Pallas kernels: 14.7 us -> 14.1 us
    all_to_all x1, waiting for transfers between devices: 6.11 us -> 5.04 us  [per_device(): got = lax.all_to_all(sent, both, 0, 0, tiled=True)]
    unnamed x14, local copies, waits for them, and re-layouts: 0.05 us -> 0.68 us
    pallas_call x5, Pallas kernels: 14.7 us -> 14.1 us  [call(): pl.pallas_call(body, out_shape=out_shape, in_specs=[pl.BlockSpec(memory_s...]
  transfers between devices with their start and end apart: 2 -> 2, of which waited for: 2 -> 2; matrix products, arithmetic and copies ran while one was open for 0% -> 0% of each run, Pallas kernels for 9% -> 10%
where the time goes in v4:
time: 50.7 us; the launch traced here: 50.4 us
  waiting for transfers between devices  14.6 us (29%)
  Pallas kernels  14.1 us (28%)
  starting transfers between devices  10 us (20%)
  blocking collectives  9.67 us (19%)
  between operations  0.73 us (1%)
  local copies, waits for them, and re-layouts  0.68 us (1%)
  other arithmetic  0.58 us (1%)
    pallas_call x5, Pallas kernels, call(): pl.pallas_call(body, out_shape=out_shape, in_specs=[pl.BlockSpec(memory_s...  14.1 us
    all_to_all x1, blocking collectives, per_device(): lax.all_to_all(slab, both, 0, 0, tiled=True)[:, :clip_count // device_count]  9.67 us
    all_to_all x1, waiting for transfers between devices, per_device(): lax.all_to_all(copies, both, 0, 0, tiled=True)  9.55 us
    all_to_all x1, starting transfers between devices, per_device(): got = lax.all_to_all(sent, both, 0, 0, tiled=True)  7.35 us
    all_to_all x1, waiting for transfers between devices, per_device(): got = lax.all_to_all(sent, both, 0, 0, tiled=True)  5.04 us
    all_to_all x1, starting transfers between devices, per_device(): lax.all_to_all(copies, both, 0, 0, tiled=True)  2.67 us
  transfers between devices with their start and end apart: 2, of which 2 were waited for; matrix products, arithmetic and copies ran while one was open for 0% of the time, Pallas kernels for 10%

profile of v4, /device:TPU:0, one launch (start us, length us, event | category | flops | bytes accessed | tf_op | source)
XLA Modules:
  0.0 50.4 jit_solution(9387560109465300059)
XLA Ops:
  0.6 1.6 %edges.1 = (bf16[128,128]{1,0:T(8,128)(2,1)S(1)}, bf16[32,32,128]{2,1,0:T(8,128)(2,1)}) custom-call(s32[128,128]{1,0:T(8,128)} %refs_0_.2, bf16[128,128]{1,0:T(8,128)(2,1)} %refs_1_.1), custom_call_target="tpu_custom_call" | custom-call | bytes 1048576 | tf_op jit(solution)/shard_map/edges/pallas_call | solution.py:467
  2.3 7.3 %all-to-all-start = ((bf16[32,32,128]{2,1,0:T(8,128)(2,1)}), bf16[32,32,128]{2,1,0:T(8,128)(2,1)S(1)}, u32[]{:S(2)}, u32[]{:S(2)}) async-start(bf16[32,32,128]{2,1,0:T(8,128)(2,1)} %get-tuple-element.10), calls=%async_computation | async-start | bytes 524288 | tf_op jit(solution)/shard_map/all_to_all | solution.py:521
  9.6 0.0 copy-start.1
  9.6 0.6 %copy-done.1 = f32[8]{0:T(128)S(1)} copy-done((f32[8]{0:T(128)S(1)}, f32[8]{0:T(128)}, u32[]{:S(2)}) %copy-start.1) | copy-done | bytes 56
  10.3 0.0 copy-start.3
  10.3 0.0 copy-start.4
  10.3 0.0 copy-start.5
  10.3 4.5 %filters.1 = (f32[16,2,96,256]{3,2,1,0:T(8,128)}, bf16[2,256,128]{2,1,0:T(8,128)(2,1)S(1)}, bf16[2,256,128]{2,1,0:T(8,128)(2,1)S(1)}) custom-call(f32[8]{0:T(128)S(1)} %copy-done.1, f32[16,64,64]{2,1,0:T(8,128)} %bitcast.13, bf16[192,256]{1,0:T(8,128)(2,1)} %constant.35.clone.refs_2_, bf16[256,512]{1,0:T(8,128)(2,1)} %constant.36.clone.refs_3_, ...), custom_call_target="tpu_custom_call" | custom-call | flops 4294967296 | bytes 1048576 | tf_op jit(solution)/shard_map/filters/pallas_call | solution.py:467
  14.8 5.0 %all-to-all-done.refs_1_ = bf16[32,32,128]{2,1,0:T(8,128)(2,1)S(1)} async-done(((bf16[32,32,128]{2,1,0:T(8,128)(2,1)}), bf16[32,32,128]{2,1,0:T(8,128)(2,1)S(1)}, u32[]{:S(2)}, u32[]{:S(2)}) %all-to-all-start) | async-done | bytes 262176 | tf_op jit(solution)/shard_map/all_to_all | solution.py:521
  19.8 0.0 copy-done.3
  19.8 0.0 copy-done.4
  19.8 0.0 copy-done.5
  19.8 0.0 copy-done.6
  19.9 0.0 copy-start
  19.9 6.1 %image.1 = (f32[128,128]{1,0:T(8,128)}, bf16[32,16,256]{2,1,0:T(8,128)(2,1)}) custom-call(bf16[128,128]{1,0:T(8,128)(2,1)S(1)} %get-tuple-element.9.refs_0_, bf16[32,32,128]{2,1,0:T(8,128)(2,1)S(1)} %all-to-all-done.refs_1_, f32[16,2,96,256]{3,2,1,0:T(8,128)} %get-tuple-element.11.refs_2_, bf16[2,256,128]{2,1,0:T(8,128)(2,1)S(1)} %get-tuple-element.12.refs_3_, ...), custom_call_target="tpu_custom_call" | custom-call | flops 6442450944 | bytes 1048576 | tf_op jit(solution)/shard_map/image/pallas_call | solution.py:467
  26.0 0.0 copy-start.2
  26.0 2.7 %all-to-all-start.1 = ((bf16[32,16,256]{2,1,0:T(8,128)(2,1)}), bf16[32,16,256]{2,1,0:T(8,128)(2,1)S(1)}, u32[]{:S(2)}, u32[]{:S(2)}) async-start(bf16[32,16,256]{2,1,0:T(8,128)(2,1)} %get-tuple-element.15), calls=%async_computation.1 | async-start | bytes 524288 | tf_op jit(solution)/shard_map/all_to_all | solution.py:591
  28.7 0.0 copy-done
  28.7 0.7 %library.1.refs_2_ = bf16[2048,256]{1,0:T(8,128)(2,1)S(1)} custom-call(bf16[2048,256]{1,0:T(8,128)(2,1)S(1)} %copy-done), custom_call_target="tpu_custom_call" | custom-call | flops 1073741824 | bytes 1048576 | tf_op jit(solution)/shard_map/library/pallas_call | solution.py:467
  29.4 9.6 %all-to-all-done.1 = bf16[32,16,256]{2,1,0:T(8,128)(2,1)S(1)} async-done(((bf16[32,16,256]{2,1,0:T(8,128)(2,1)}), bf16[32,16,256]{2,1,0:T(8,128)(2,1)S(1)}, u32[]{:S(2)}, u32[]{:S(2)}) %all-to-all-start.1) | async-done | bytes 262176 | tf_op jit(solution)/shard_map/all_to_all | solution.py:591
  38.9 0.0 copy-done.2
  38.9 1.2 %match.1 = f32[32,128]{1,0:T(8,128)S(1)} custom-call(s32[1,128]{1,0:T(1,128)S(1)} %bitcast.10, bf16[512,256]{1,0:T(8,128)(2,1)S(1)} %bitcast.7, bf16[2048,256]{1,0:T(8,128)(2,1)S(1)} %library.1.refs_2_), custom_call_target="tpu_custom_call" | custom-call | flops 1073741824 | bytes 1048576 | tf_op jit(solution)/shard_map/match/pallas_call | solution.py:467
  40.2 9.7 %all_to_all.22 = f32[32,1,128]{2,1,0:T(1,128)S(1)} all-to-all(f32[32,1,128]{2,1,0:T(1,128)S(1)} %bitcast.8), channel_id=1, replica_groups=mesh['wide'=8,'narrow'=4] {'wide','narrow'}, dimensions={0} | all-to-all | bytes 32768 | tf_op jit(solution)/shard_map/all_to_all | solution.py:600
  49.9 0.5 %negate_multiply_fusion = f32[4]{0:T(128)} fusion(f32[4]{0:T(128)S(1)} %slice_reduce_fusion, f32[4]{0:T(128)S(1)} %exponential_reduce_fusion), kind=kLoop, calls=%fused_computation.2 | loop fusion | flops 12 | bytes 48 | tf_op jit(solution)/shard_map/div | solution.py:603
  (3 shorter events, 0.1 us)
Async XLA Ops:
  2.3 17.6 %all-to-all-start = ((bf16[32,32,128]{2,1,0:T(8,128)(2,1)}), bf16[32,32,128]{2,1,0:T(8,128)(2,1)S(1)}, u32[]{:S(2)}, u32[]{:S(2)}) async-start(bf16[32,32,128]{2,1,0:T(8,128)(2,1)} %get-tuple-element.10), calls=%async_computation | async-start | bytes 524288 | tf_op jit(solution)/shard_map/all_to_all | solution.py:521
  9.6 0.7 %copy-start.1 = (f32[8]{0:T(128)S(1)}, f32[8]{0:T(128)}, u32[]{:S(2)}) copy-start(f32[8]{0:T(128)} %refs_0_.3) | copy-start | bytes 100
  10.3 9.6 %copy-start.3 = (bf16[2,256,512]{2,1,0:T(8,128)(2,1)S(1)}, bf16[2,256,512]{2,1,0:T(8,128)(2,1)}, u32[]{:S(2)}) copy-start(bf16[2,256,512]{2,1,0:T(8,128)(2,1)} %constant.42.refs_6_) | copy-start | bytes 1572868
  10.3 9.6 %copy-start.4 = (bf16[2,256,256]{2,1,0:T(8,128)(2,1)S(1)}, bf16[2,256,256]{2,1,0:T(8,128)(2,1)}, u32[]{:S(2)}) copy-start(bf16[2,256,256]{2,1,0:T(8,128)(2,1)} %constant.45.refs_7_) | copy-start | bytes 786436
  10.3 9.6 %copy-start.5 = (bf16[2,192,256]{2,1,0:T(8,128)(2,1)S(1)}, bf16[2,192,256]{2,1,0:T(8,128)(2,1)}, u32[]{:S(2)}) copy-start(bf16[2,192,256]{2,1,0:T(8,128)(2,1)} %constant.39.refs_5_) | copy-start | bytes 589828
  10.3 9.6 %copy-start.6 = (bf16[2,128,256]{2,1,0:T(8,128)(2,1)S(1)}, bf16[2,128,256]{2,1,0:T(8,128)(2,1)}, u32[]{:S(2)}) copy-start(bf16[2,128,256]{2,1,0:T(8,128)(2,1)} %constant.48.refs_8_) | copy-start | bytes 393220
  19.9 8.9 %copy-start = (bf16[2048,256]{1,0:T(8,128)(2,1)S(1)}, bf16[2048,256]{1,0:T(8,128)(2,1)}, u32[]{:S(2)}) copy-start(bf16[2048,256]{1,0:T(8,128)(2,1)} %library_ref.1) | copy-start | bytes 3145732
  26.0 12.9 %copy-start.2 = (s32[128]{0:T(128)S(1)}, s32[128]{0:T(128)}, u32[]{:S(2)}) copy-start(s32[128]{0:T(128)} %param.22) | copy-start | bytes 1540
  26.0 12.9 %all-to-all-start.1 = ((bf16[32,16,256]{2,1,0:T(8,128)(2,1)}), bf16[32,16,256]{2,1,0:T(8,128)(2,1)S(1)}, u32[]{:S(2)}, u32[]{:S(2)}) async-start(bf16[32,16,256]{2,1,0:T(8,128)(2,1)} %get-tuple-element.15), calls=%async_computation.1 | async-start | bytes 524288 | tf_op jit(solution)/shard_map/all_to_all | solution.py:591

commit v5 on v4

--- a/solution.py
+++ b/solution.py
@@ -31,44 +31,53 @@
     return high, (table - high.astype(np.float64)).astype(bf16)
 
 
+def thirds(table):
+    high, rest = table.astype(bf16), table - table.astype(bf16).astype(np.float64)
+    middle = rest.astype(bf16)
+    return high, middle, (rest - middle.astype(np.float64)).astype(bf16)
+
+
 def tables(tile):
     full = tile + KSIZE
     half = full // 2
-    wide = ceil_to(full, 2 * LANES)
+    lanes = ceil_to(half, LANES)
+    wide = 2 * lanes
     unit = 2.0 * math.pi / full
     place = np.arange(full)
     place = np.where(place < tile + KSIZE // 2, place, place - full)
     taps = np.arange(KSIZE) - KSIZE // 2
     odd = np.arange(half) + 0.5
-    freq = np.arange(full)
 
     def padded(table, rows, cols):
         out = np.zeros((rows, cols))
         out[: table.shape[0], : table.shape[1]] = table
         return out
 
-    def side_by_side(angle, rows, cols):
+    def side_by_side(angle, rows):
         return np.concatenate(
-            [padded(np.cos(angle), rows, cols), padded(np.sin(angle), rows, cols)], axis=1
+            [padded(np.cos(angle), rows, lanes), padded(np.sin(angle), rows, lanes)], axis=1
         )
 
     angle = unit * odd[:, None] * place[None, :]
     rows_in = padded(np.concatenate([np.cos(angle), -np.sin(angle)]), full, wide)
-    cols_in = side_by_side(unit * place[:, None] * freq[None, :], wide, wide)
-    cols_out = side_by_side(unit * freq[:, None] * np.arange(tile)[None, :], wide, tile)
+    cols_in = side_by_side(unit * place[:, None] * odd[None, :], wide)
+    angle = unit * odd[:, None] * np.arange(tile)[None, :]
+    cols_out = np.concatenate(
+        [padded(np.cos(angle), lanes, tile), padded(np.sin(angle), lanes, tile)]
+    )
     angle = unit * np.arange(tile)[:, None] * odd[None, :]
     rows_out = padded(np.concatenate([np.cos(angle), -np.sin(angle)], axis=1), tile, wide)
     angle = unit * odd[:, None] * taps[None, :]
     taps_rows = np.concatenate([np.cos(angle), np.sin(angle)]) * (2.0 / (full * full))
-    taps_cols = side_by_side(unit * taps[:, None] * freq[None, :], KSIZE, wide)
-    high, low = halves(taps_rows)
-    taps_rows = np.concatenate([high, low, high, low], axis=1)
-    high, low = halves(taps_cols)
-    taps_cols = np.concatenate([high, high, low, low], axis=0)
+    taps_cols = side_by_side(unit * taps[:, None] * odd[None, :], KSIZE)
+    high, middle, low = thirds(taps_rows)
+    taps_rows = np.concatenate([high, middle, low, high, middle, high], axis=1)
+    high, middle, low = thirds(taps_cols)
+    taps_cols = np.concatenate([high, middle, low, high, middle, high], axis=0)
     return {
-        "rows_in": halves(rows_in),
-        "cols_in": halves(cols_in),
-        "cols_out": halves(cols_out),
+        "rows_in": thirds(rows_in),
+        "cols_in": thirds(cols_in),
+        "cols_out": np.concatenate(halves(cols_out), axis=1),
         "rows_out": halves(rows_out),
         "taps_rows": taps_rows,
         "taps_cols": taps_cols,
@@ -82,6 +91,12 @@
 def split(value):
     high = value.astype(bf16)
     return high, (value - high.astype(f32)).astype(bf16)
+
+
+def split3(value):
+    high = value.astype(bf16)
+    middle, low = split(value - high.astype(f32))
+    return high, middle, low
 
 
 def dot3(left, right):
@@ -185,23 +200,27 @@
 def transform_taps(weight_ref, taps_ref, rows_ref, cols_ref, out_ref, mixed_ref, finished):
     count = out_ref.shape[0]
     half = out_ref.shape[2]
-    wide = out_ref.shape[3]
+    lanes = out_ref.shape[3] // 2
 
     def along_rows(index):
         taps = taps_ref[index]
         taps = taps * jnp.sqrt(jnp.full(taps.shape, weight_ref[index // 2], f32))
-        spread = jnp.concatenate([taps, taps, taps, taps], axis=1)
-        high, low = split(spread)
-        stacked = jnp.concatenate([high, high, low, low], axis=0)
+        high, middle, low = split3(jnp.concatenate([taps, taps], axis=1))
+        stacked = jnp.concatenate([high, high, high, middle, middle, low], axis=0)
         rows = dot(rows_ref[...], stacked)
-        kept = rows.astype(bf16).astype(f32)
-        is_low = (iota(rows.shape, 1) & KSIZE) != 0
-        mixed_ref[index % 2] = jnp.where(is_low, rows - kept, rows).astype(bf16)
+        high, middle, low = split3(rows)
+        first = iota(rows.shape, 1) < KSIZE
+        pairs = ((high, high), (high, middle), (middle, low))
+        for place, (left, right) in enumerate(pairs):
+            value = jnp.where(first, left.astype(f32), right.astype(f32)).astype(bf16)
+            mixed_ref[index % 2, :, place * 2 * KSIZE : (place + 1) * 2 * KSIZE] = value
 
     def along_cols(index):
         both = dot(mixed_ref[index % 2], cols_ref[...])
-        out_ref[index, 0] = both[:half, :wide] - both[half:, wide:]
-        out_ref[index, 1] = both[:half, wide:] + both[half:, :wide]
+        out_ref[index, 0, :, :lanes] = both[:half, :lanes] - both[half:, lanes:]
+        out_ref[index, 0, :, lanes:] = both[:half, :lanes] + both[half:, lanes:]
+        out_ref[index, 1, :, :lanes] = both[half:, :lanes] + both[:half, lanes:]
+        out_ref[index, 1, :, lanes:] = both[half:, :lanes] - both[:half, lanes:]
         finished[index].start()
 
     along_rows(0)
@@ -301,14 +320,14 @@
     group = prod_ref.shape[2] // (2 * full)
 
     def arriving(index):
-        part = pl.ds(index * 2 * group, 2 * group)
+        part = pl.ds(index * kernel_count, kernel_count)
         return pltpu.make_async_copy(filter_hbm.at[part], filter_ref.at[part], sems.at[index])
 
     def request(index, carry):
         arriving(index).start()
         return carry
 
-    lax.fori_loop(0, kernel_count // group, request, 0)
+    lax.fori_loop(0, 2, request, 0)
     col = lax.axis_index("wide")
     row = lax.axis_index("narrow")
     lane = iota((border, tile), 1)
@@ -339,40 +358,44 @@
         for member in range(mid_ref.shape[1]):
             mid_ref[place, member, :, full:, :] = jnp.zeros((2, wide - full, wide), bf16)
     mask = mask_ref[...]
-    rows = dot(rows_in_ref[0], mask) + dot(rows_in_ref[1], mask)
-    both = dot3(split(rows), (cols_in_ref[0], cols_in_ref[1]))
-    spec_ref[0] = both[:half, :wide] + both[half:, wide:]
-    spec_ref[1] = both[half:, :wide] - both[:half, wide:]
+    rows = (dot(rows_in_ref[2], mask) + dot(rows_in_ref[1], mask)) + dot(rows_in_ref[0], mask)
+    high, middle, low = split3(rows)
+    both = dot(low, cols_in_ref[0]) + dot(high, cols_in_ref[2]) + dot(middle, cols_in_ref[1])
+    both = (both + dot(middle, cols_in_ref[0]) + dot(high, cols_in_ref[1])) + dot(high, cols_in_ref[0])
+    lanes = wide // 2
+    spec_ref[0, :, :lanes] = both[:half, :lanes] + both[half:, lanes:]
+    spec_ref[0, :, lanes:] = both[:half, :lanes] - both[half:, lanes:]
+    spec_ref[1, :, :lanes] = both[half:, :lanes] - both[:half, lanes:]
+    spec_ref[1, :, lanes:] = both[half:, :lanes] + both[:half, lanes:]
 
     def multiply(index):
-        arriving(index).wait()
         place = prod_ref.at[index % 2]
         for part in range(2 * group):
-            number = 2 * group * index + part
-            ref = filter_ref.at[number]
+            ref = filter_ref.at[2 * group * index + part]
             base = part * full
-            high, low = split(spec_ref[0] * ref[0] - spec_ref[1] * ref[1])
-            place[0, base : base + half] = high
-            place[1, base : base + half] = low
-            high, low = split(spec_ref[0] * ref[1] + spec_ref[1] * ref[0])
-            place[0, base + half : base + full] = high
-            place[1, base + half : base + full] = low
+            real = spec_ref[0] * ref[0] - spec_ref[1] * ref[1]
+            imag = spec_ref[0] * ref[1] + spec_ref[1] * ref[0]
+            pieces = (
+                (0, 0, real[:, :lanes] + real[:, lanes:]),
+                (0, lanes, imag[:, lanes:] - imag[:, :lanes]),
+                (half, 0, imag[:, :lanes] + imag[:, lanes:]),
+                (half, lanes, real[:, :lanes] - real[:, lanes:]),
+            )
+            for down, lane, piece in pieces:
+                for order, value in enumerate(split3(piece)):
+                    place[order, base + down : base + down + half, lane : lane + lanes] = value
 
     def along_cols(index):
         source = prod_ref.at[index % 2]
-        cols = dot3((source[0], source[1]), (cols_out_ref[0], cols_out_ref[1]))
+        table = cols_out_ref[...]
+        cols = dot(source[2], table) + dot(source[1], table) + dot(source[0], table)
         for part in range(2 * group):
             place = mid_ref.at[index % 2, part // 2]
             base = part * full
             lane = part % 2 * tile
-            real = cols[base : base + half]
-            imag = cols[base + half : base + full]
-            high, low = split(real[:, :tile] - imag[:, tile:])
-            place[0, :half, lane : lane + tile] = high
-            place[1, :half, lane : lane + tile] = low
-            high, low = split(imag[:, :tile] + real[:, tile:])
-            place[0, half:full, lane : lane + tile] = high
-            place[1, half:full, lane : lane + tile] = low
+            high, low = split(cols[base : base + full, :tile] + cols[base : base + full, tile:])
+            place[0, :full, lane : lane + tile] = high
+            place[1, :full, lane : lane + tile] = low
 
     def along_rows(index):
         value = None
@@ -390,6 +413,8 @@
             sum_ref[...] += value
 
     for step in range(kernel_count // group + 2):
+        if step % (kernel_count // (2 * group)) == 0 and step < kernel_count // group:
+            arriving(step // (kernel_count // (2 * group))).wait()
         if step < kernel_count // group:
             multiply(step)
         if 0 <= step - 1 < kernel_count // group:
@@ -402,8 +427,9 @@
     shape = (CAP * KSIG, CAP * KSIG)
     crossed = jnp.where(iota(shape, 0) // KSIG == iota(shape, 1) // KSIG, crossed, 0.0)
     fold = ((iota(shape, 0) & (KSIG - 1)) == (iota(shape, 1) & (KSIG - 1))).astype(f32).astype(bf16)
-    high, low = split(crossed)
-    spread = dot(high, fold) + dot(low, fold)
+    high = crossed.astype(bf16)
+    middle, low = split(crossed - high.astype(f32))
+    spread = (dot(low, fold) + dot(middle, fold)) + dot(high, fold)
     spread = jnp.where((iota(shape, 0) & (KSIG - 1)) == iota(shape, 1) // KSIG, spread, 0.0)
     signature = jnp.sum(spread.reshape(CAP, KSIG, SIGD), axis=1)
     signature = jnp.where(iota(signature.shape, 1) == 0, 0.0, signature)
@@ -486,7 +512,7 @@
     border = KSIZE // 2
     full = tile + KSIZE
     half = full // 2
-    wide = ceil_to(full, 2 * LANES)
+    wide = 2 * ceil_to(half, LANES)
     table = {
         key: jnp.stack([jnp.asarray(part) for part in value])
         if isinstance(value, tuple)
@@ -536,7 +562,7 @@
         ),
         scratch=(
             pltpu.VMEM((real_count,) + spectrum, f32),
-            pltpu.VMEM((2, full, 4 * KSIZE), bf16),
+            pltpu.VMEM((2, full, 6 * KSIZE), bf16),
             pltpu.VMEM((real_count, KSIZE, KSIZE), f32),
             pltpu.VMEM(table["taps_rows"].shape, bf16),
             pltpu.VMEM(table["taps_cols"].shape, bf16),
@@ -551,6 +577,14 @@
         flops=4 << 30,
         name="filters",
     )
+    lib_units = call(
+        library_body,
+        jax.ShapeDtypeStruct(library.shape, bf16),
+        (library,),
+        flops=1 << 30,
+        name="library",
+    )
+    filters, lib_units = lax.optimization_barrier((filters, lib_units))
     aerial, copies = call(
         lambda *refs: image_body(cols_wide, rows_narrow, *refs),
         (
@@ -571,22 +605,15 @@
         scratch=(
             pltpu.VMEM((wide, wide), bf16),
             pltpu.VMEM(spectrum, f32),
-            pltpu.VMEM((2, 2, GROUP * 2 * full, wide), bf16),
+            pltpu.VMEM((2, 3, GROUP * 2 * full, wide), bf16),
             pltpu.VMEM((2, GROUP, 2, wide, wide), bf16),
             pltpu.VMEM((tile, tile), f32),
             pltpu.VMEM((real_count,) + spectrum, f32),
-            pltpu.SemaphoreType.DMA((real_count // (2 * GROUP),)),
+            pltpu.SemaphoreType.DMA((2,)),
         ),
         hbm=(2,),
         flops=6 << 30,
         name="image",
-    )
-    lib_units = call(
-        library_body,
-        jax.ShapeDtypeStruct(library.shape, bf16),
-        (library,),
-        flops=1 << 30,
-        name="library",
     )
     gathered = lax.all_to_all(copies, both, 0, 0, tiled=True).reshape(device_count * CAP, SIGD)
     slab = call(

time: 50.7 us -> 50 us (0.986)
  blocking collectives: 9.67 us -> 22.4 us
  waiting for transfers between devices: 14.6 us -> 3.58 us
  starting transfers between devices: 10 us -> 7.34 us
  local copies, waits for them, and re-layouts: 0.68 us -> 1.26 us
    all_to_all x0 -> x1, blocking collectives: none -> 12.7 us  [per_device(): lax.all_to_all(copies, both, 0, 0, tiled=True)]
    all_to_all x1 -> x0, waiting for transfers between devices: 9.55 us -> none  [per_device(): lax.all_to_all(copies, both, 0, 0, tiled=True)]
    all_to_all x1 -> x0, starting transfers between devices: 2.67 us -> none  [per_device(): lax.all_to_all(copies, both, 0, 0, tiled=True)]
    all_to_all x1, waiting for transfers between devices: 5.04 us -> 3.58 us  [per_device(): got = lax.all_to_all(sent, both, 0, 0, tiled=True)]
    unnamed x14, local copies, waits for them, and re-layouts: 0.68 us -> 1.26 us
  transfers between devices with their start and end apart: 2 -> 1, of which waited for: 2 -> 1; matrix products, arithmetic and copies ran while one was open for 0% -> 0% of each run, Pallas kernels for 10% -> 11%
where the time goes in v5:
time: 50 us; the launch traced here: 49.7 us
  blocking collectives  22.4 us (45%)
  Pallas kernels  13.8 us (28%)
  starting transfers between devices  7.34 us (15%)
  waiting for transfers between devices  3.58 us (7%)
  local copies, waits for them, and re-layouts  1.26 us (3%)
  between operations  0.75 us (2%)
  other arithmetic  0.58 us (1%)
    pallas_call x5, Pallas kernels, call(): pl.pallas_call(body, out_shape=out_shape, in_specs=[pl.BlockSpec(memory_s...  13.8 us
    all_to_all x1, blocking collectives, per_device(): lax.all_to_all(copies, both, 0, 0, tiled=True)  12.7 us
    all_to_all x1, blocking collectives, per_device(): lax.all_to_all(slab, both, 0, 0, tiled=True)[:, :clip_count // device_count]  9.67 us
    all_to_all x1, starting transfers between devices, per_device(): got = lax.all_to_all(sent, both, 0, 0, tiled=True)  7.34 us
    all_to_all x1, waiting for transfers between devices, per_device(): got = lax.all_to_all(sent, both, 0, 0, tiled=True)  3.58 us
    unnamed x14, local copies, waits for them, and re-layouts  1.26 us
  transfers between devices with their start and end apart: 1, of which 1 were waited for; matrix products, arithmetic and copies ran while one was open for 0% of the time, Pallas kernels for 11%

profile of v5, /device:TPU:0, one launch (start us, length us, event | category | flops | bytes accessed | tf_op | source)
XLA Modules:
  0.0 49.7 jit_solution(674799370484828549)
XLA Ops:
  0.6 0.0 copy-start.1
  0.6 1.6 %edges.1 = (bf16[128,128]{1,0:T(8,128)(2,1)S(1)}, bf16[32,32,128]{2,1,0:T(8,128)(2,1)}) custom-call(s32[128,128]{1,0:T(8,128)} %refs_0_.2, bf16[128,128]{1,0:T(8,128)(2,1)} %refs_1_.1), custom_call_target="tpu_custom_call" | custom-call | bytes 1048576 | tf_op jit(solution)/shard_map/edges/pallas_call | solution.py:493
  2.3 7.3 %all-to-all-start = ((bf16[32,32,128]{2,1,0:T(8,128)(2,1)}), bf16[32,32,128]{2,1,0:T(8,128)(2,1)S(1)}, u32[]{:S(2)}, u32[]{:S(2)}) async-start(bf16[32,32,128]{2,1,0:T(8,128)(2,1)} %get-tuple-element.12), calls=%async_computation | async-start | bytes 524288 | tf_op jit(solution)/shard_map/all_to_all | solution.py:547
  9.6 0.0 copy-start
  9.6 1.2 %copy-done = bf16[2048,256]{1,0:T(8,128)(2,1)S(1)} copy-done((bf16[2048,256]{1,0:T(8,128)(2,1)S(1)}, bf16[2048,256]{1,0:T(8,128)(2,1)}, u32[]{:S(2)}) %copy-start) | copy-done | bytes 1048600
  10.9 0.7 %library.1.refs_2_ = bf16[2048,256]{1,0:T(8,128)(2,1)S(1)} custom-call(bf16[2048,256]{1,0:T(8,128)(2,1)S(1)} %copy-done), custom_call_target="tpu_custom_call" | custom-call | flops 1073741824 | bytes 1048576 | tf_op jit(solution)/shard_map/library/pallas_call | solution.py:493
  11.5 0.0 copy-done.1
  11.5 0.0 copy-start.3
  11.5 0.0 copy-start.4
  11.5 0.0 copy-start.5
  11.6 0.0 copy-start.6
  11.6 4.7 %filters.1 = (f32[16,2,96,256]{3,2,1,0:T(8,128)}, bf16[2,256,128]{2,1,0:T(8,128)(2,1)S(1)}, bf16[2,256,128]{2,1,0:T(8,128)(2,1)S(1)}) custom-call(f32[8]{0:T(128)S(1)} %copy-done.1, f32[16,64,64]{2,1,0:T(8,128)} %bitcast.13, bf16[192,384]{1,0:T(8,128)(2,1)} %constant.38.clone.refs_2_, bf16[384,256]{1,0:T(8,128)(2,1)} %constant.39.clone.refs_3_, ...), custom_call_target="tpu_custom_call" | custom-call | flops 4294967296 | bytes 1048576 | tf_op jit(solution)/shard_map/filters/pallas_call | solution.py:493
  16.3 3.6 %all-to-all-done.refs_1_ = bf16[32,32,128]{2,1,0:T(8,128)(2,1)S(1)} async-done(((bf16[32,32,128]{2,1,0:T(8,128)(2,1)}), bf16[32,32,128]{2,1,0:T(8,128)(2,1)S(1)}, u32[]{:S(2)}, u32[]{:S(2)}) %all-to-all-start) | async-done | bytes 262176 | tf_op jit(solution)/shard_map/all_to_all | solution.py:547
  19.9 0.0 copy-done.3
  19.9 0.0 copy-done.4
  19.9 0.0 copy-done.5
  19.9 0.0 copy-done.6
  19.9 0.0 copy-start.2
  19.9 5.6 %image.1 = (f32[128,128]{1,0:T(8,128)}, bf16[32,16,256]{2,1,0:T(8,128)(2,1)S(1)}) custom-call(bf16[128,128]{1,0:T(8,128)(2,1)S(1)} %get-tuple-element.11.refs_0_, bf16[32,32,128]{2,1,0:T(8,128)(2,1)S(1)} %all-to-all-done.refs_1_, f32[16,2,96,256]{3,2,1,0:T(8,128)} %get-tuple-element.14.refs_2_, bf16[2,256,128]{2,1,0:T(8,128)(2,1)S(1)} %get-tuple-element.15.refs_3_, ...), custom_call_target="tpu_custom_call" | custom-call | flops 6442450944 | bytes 1048576 | tf_op jit(solution)/shard_map/image/pallas_call | solution.py:493
  25.5 12.7 %all_to_all.22 = bf16[32,16,256]{2,1,0:T(8,128)(2,1)S(1)} all-to-all(bf16[32,16,256]{2,1,0:T(8,128)(2,1)S(1)} %get-tuple-element.18), channel_id=1, replica_groups=mesh['wide'=8,'narrow'=4] {'wide','narrow'}, dimensions={0} | all-to-all | bytes 524288 | tf_op jit(solution)/shard_map/all_to_all | solution.py:618
  38.2 0.0 copy-done.2
  38.2 1.2 %match.1 = f32[32,128]{1,0:T(8,128)S(1)} custom-call(s32[1,128]{1,0:T(1,128)S(1)} %bitcast.10, bf16[512,256]{1,0:T(8,128)(2,1)S(1)} %bitcast.7, bf16[2048,256]{1,0:T(8,128)(2,1)S(1)} %library.1.refs_2_), custom_call_target="tpu_custom_call" | custom-call | flops 1073741824 | bytes 1048576 | tf_op jit(solution)/shard_map/match/pallas_call | solution.py:493
  39.4 9.7 %all_to_all.23 = f32[32,1,128]{2,1,0:T(1,128)S(1)} all-to-all(f32[32,1,128]{2,1,0:T(1,128)S(1)} %bitcast.8), channel_id=1, replica_groups=mesh['wide'=8,'narrow'=4] {'wide','narrow'}, dimensions={0} | all-to-all | bytes 32768 | tf_op jit(solution)/shard_map/all_to_all | solution.py:627
  49.2 0.5 %negate_multiply_fusion = f32[4]{0:T(128)} fusion(f32[4]{0:T(128)S(1)} %slice_reduce_fusion, f32[4]{0:T(128)S(1)} %exponential_reduce_fusion), kind=kLoop, calls=%fused_computation.2 | loop fusion | flops 12 | bytes 48 | tf_op jit(solution)/shard_map/div | solution.py:630
  (2 shorter events, 0.0 us)
Async XLA Ops:
  0.6 10.9 %copy-start.1 = (f32[8]{0:T(128)S(1)}, f32[8]{0:T(128)}, u32[]{:S(2)}) copy-start(f32[8]{0:T(128)} %refs_0_.3) | copy-start | bytes 100
  2.3 17.6 %all-to-all-start = ((bf16[32,32,128]{2,1,0:T(8,128)(2,1)}), bf16[32,32,128]{2,1,0:T(8,128)(2,1)S(1)}, u32[]{:S(2)}, u32[]{:S(2)}) async-start(bf16[32,32,128]{2,1,0:T(8,128)(2,1)} %get-tuple-element.12), calls=%async_computation | async-start | bytes 524288 | tf_op jit(solution)/shard_map/all_to_all | solution.py:547
  9.6 1.2 %copy-start = (bf16[2048,256]{1,0:T(8,128)(2,1)S(1)}, bf16[2048,256]{1,0:T(8,128)(2,1)}, u32[]{:S(2)}) copy-start(bf16[2048,256]{1,0:T(8,128)(2,1)} %library_ref.1) | copy-start | bytes 3145732
  11.5 8.3 %copy-start.3 = (bf16[3,256,256]{2,1,0:T(8,128)(2,1)S(1)}, bf16[3,256,256]{2,1,0:T(8,128)(2,1)}, u32[]{:S(2)}) copy-start(bf16[3,256,256]{2,1,0:T(8,128)(2,1)} %constant.47.refs_6_) | copy-start | bytes 1179652
  11.5 8.3 %copy-start.4 = (bf16[3,192,256]{2,1,0:T(8,128)(2,1)S(1)}, bf16[3,192,256]{2,1,0:T(8,128)(2,1)}, u32[]{:S(2)}) copy-start(bf16[3,192,256]{2,1,0:T(8,128)(2,1)} %constant.43.refs_5_) | copy-start | bytes 884740
  11.5 8.3 %copy-start.5 = (bf16[2,128,256]{2,1,0:T(8,128)(2,1)S(1)}, bf16[2,128,256]{2,1,0:T(8,128)(2,1)}, u32[]{:S(2)}) copy-start(bf16[2,128,256]{2,1,0:T(8,128)(2,1)} %constant.50.refs_8_) | copy-start | bytes 393220
  11.6 8.3 %copy-start.6 = (bf16[256,256]{1,0:T(8,128)(2,1)S(1)}, bf16[256,256]{1,0:T(8,128)(2,1)}, u32[]{:S(2)}) copy-start(bf16[256,256]{1,0:T(8,128)(2,1)} %constant.35.clone.refs_7_) | copy-start | bytes 393220
  19.9 18.4 %copy-start.2 = (s32[128]{0:T(128)S(1)}, s32[128]{0:T(128)}, u32[]{:S(2)}) copy-start(s32[128]{0:T(128)} %param.23) | copy-start | bytes 1540

commit v6 on v5

--- a/solution.py
+++ b/solution.py
@@ -24,11 +24,6 @@
 
 def ceil_to(value, step):
     return -(-value // step) * step
-
-
-def halves(table):
-    high = table.astype(bf16)
-    return high, (table - high.astype(np.float64)).astype(bf16)
 
 
 def thirds(table):
@@ -47,6 +42,8 @@
     place = np.where(place < tile + KSIZE // 2, place, place - full)
     taps = np.arange(KSIZE) - KSIZE // 2
     odd = np.arange(half) + 0.5
+    extra = (lanes - half) // 2
+    again = np.concatenate([odd, odd[:extra], odd[:extra]])
 
     def padded(table, rows, cols):
         out = np.zeros((rows, cols))
@@ -60,16 +57,30 @@
 
     angle = unit * odd[:, None] * place[None, :]
     rows_in = padded(np.concatenate([np.cos(angle), -np.sin(angle)]), full, wide)
-    cols_in = side_by_side(unit * place[:, None] * odd[None, :], wide)
+    cols_in = side_by_side(unit * place[:, None] * again[None, :], wide)
     angle = unit * odd[:, None] * np.arange(tile)[None, :]
-    cols_out = np.concatenate(
-        [padded(np.cos(angle), lanes, tile), padded(np.sin(angle), lanes, tile)]
-    )
+    cols_out = []
+    for part in (np.cos(angle), np.sin(angle)):
+        high, middle, low = thirds(part)
+        empty = np.zeros_like(low[:extra])
+        cols_out.append(np.concatenate([high, middle], axis=1))
+        cols_out.append(np.concatenate([low[:extra], empty], axis=1))
+        cols_out.append(np.concatenate([high[:extra], middle[:extra]], axis=1))
+    cols_out = np.concatenate(cols_out)
     angle = unit * np.arange(tile)[:, None] * odd[None, :]
-    rows_out = padded(np.concatenate([np.cos(angle), -np.sin(angle)], axis=1), tile, wide)
+    pieces = [thirds(np.cos(angle)), thirds(-np.sin(angle))]
+    firsts = [piece[0] for piece in pieces]
+    lows = [piece[2][:, :extra] for piece in pieces]
+    heads = [piece[0][:, :extra] for piece in pieces]
+    seconds = [piece[1] for piece in pieces]
+    empty = np.zeros((tile, wide - full), bf16)
+    rows_out = (
+        np.concatenate(firsts + lows + heads, axis=1),
+        np.concatenate(seconds + [empty], axis=1),
+    )
     angle = unit * odd[:, None] * taps[None, :]
     taps_rows = np.concatenate([np.cos(angle), np.sin(angle)]) * (2.0 / (full * full))
-    taps_cols = side_by_side(unit * taps[:, None] * odd[None, :], KSIZE)
+    taps_cols = side_by_side(unit * taps[:, None] * again[None, :], KSIZE)
     high, middle, low = thirds(taps_rows)
     taps_rows = np.concatenate([high, middle, low, high, middle, high], axis=1)
     high, middle, low = thirds(taps_cols)
@@ -77,8 +88,8 @@
     return {
         "rows_in": thirds(rows_in),
         "cols_in": thirds(cols_in),
-        "cols_out": np.concatenate(halves(cols_out), axis=1),
-        "rows_out": halves(rows_out),
+        "cols_out": cols_out,
+        "rows_out": rows_out,
         "taps_rows": taps_rows,
         "taps_cols": taps_cols,
     }
@@ -238,9 +249,11 @@
     cols_hbm,
     tile_hbm,
     corner_hbm,
+    library_hbm,
     out_hbm,
     rb_ref,
     cb_ref,
+    units_ref,
     out_ref,
     mixed_ref,
     taps_ref,
@@ -248,8 +261,10 @@
     cols_ref,
     tile_ref,
     corner_ref,
+    library_ref,
     sems,
     out_sems,
+    library_sem,
 ):
     pairs = (
         (taps_hbm, taps_ref),
@@ -258,7 +273,10 @@
         (tile_hbm, tile_ref),
         (corner_hbm, corner_ref),
     )
-    for copy in fetched(pairs, sems):
+    needed = fetched(pairs, sems)
+    library = pltpu.make_async_copy(library_hbm, library_ref, library_sem)
+    library.start()
+    for copy in needed:
         copy.wait()
     finished = [
         pltpu.make_async_copy(out_ref.at[index], out_hbm.at[index], out_sems.at[index])
@@ -285,6 +303,10 @@
         high, low = split(shifted_basis(corner.astype(jnp.int32), tile))
         basis_ref[0] = high
         basis_ref[1] = low
+    library.wait()
+    rows = library_ref[...].astype(f32)
+    mean_square = jnp.mean(rows * rows, axis=1, keepdims=True)
+    units_ref[...] = (rows * (1.0 / (KSIG * jnp.sqrt(mean_square + 1e-06)))).astype(bf16)
     for copy in finished:
         copy.wait()
 
@@ -356,7 +378,7 @@
     mask_ref[full:, :] = jnp.zeros((wide - full, wide), bf16)
     for place in range(2):
         for member in range(mid_ref.shape[1]):
-            mid_ref[place, member, :, full:, :] = jnp.zeros((2, wide - full, wide), bf16)
+            mid_ref[place, member, 1, full:, :] = jnp.zeros((wide - full, wide), bf16)
     mask = mask_ref[...]
     rows = (dot(rows_in_ref[2], mask) + dot(rows_in_ref[1], mask)) + dot(rows_in_ref[0], mask)
     high, middle, low = split3(rows)
@@ -367,6 +389,9 @@
     spec_ref[0, :, lanes:] = both[:half, :lanes] - both[half:, lanes:]
     spec_ref[1, :, :lanes] = both[half:, :lanes] - both[:half, lanes:]
     spec_ref[1, :, lanes:] = both[half:, :lanes] + both[:half, lanes:]
+
+    extra = (lanes - half) // 2
+    column = iota((half, lanes), 1)
 
     def multiply(index):
         place = prod_ref.at[index % 2]
@@ -382,20 +407,31 @@
                 (half, lanes, real[:, :lanes] - real[:, lanes:]),
             )
             for down, lane, piece in pieces:
-                for order, value in enumerate(split3(piece)):
-                    place[order, base + down : base + down + half, lane : lane + lanes] = value
+                high, middle, low = split3(piece)
+                value = jnp.where(column < half + extra, high.astype(f32), low.astype(f32))
+                place[0, base + down : base + down + half, lane : lane + lanes] = value.astype(bf16)
+                value = jnp.where(column < half, middle.astype(f32), 0.0)
+                place[1, base + down : base + down + half, lane : lane + lanes] = value.astype(bf16)
 
     def along_cols(index):
         source = prod_ref.at[index % 2]
         table = cols_out_ref[...]
-        cols = dot(source[2], table) + dot(source[1], table) + dot(source[0], table)
+        cols = dot(source[1], table) + dot(source[0], table)
         for part in range(2 * group):
             place = mid_ref.at[index % 2, part // 2]
             base = part * full
             lane = part % 2 * tile
-            high, low = split(cols[base : base + full, :tile] + cols[base : base + full, tile:])
+            value = cols[base : base + full, tile:] + cols[base : base + full, :tile]
+            high, low = split(value)
             place[0, :full, lane : lane + tile] = high
             place[1, :full, lane : lane + tile] = low
+            for order, first in enumerate((0, half)):
+                slow = slice(first, first + extra)
+                down = full + order * extra
+                place[0, down : down + extra, lane : lane + tile] = high[slow]
+                rest = split3(value[slow])[2]
+                down += 2 * extra
+                place[0, down : down + extra, lane : lane + tile] = rest
 
     def along_rows(index):
         value = None
@@ -436,12 +472,6 @@
     mean_square = jnp.mean(signature * signature, axis=1, keepdims=True)
     units = (signature / (KSIG * jnp.sqrt(mean_square + 1e-06))).astype(bf16)
     units_ref[...] = jnp.broadcast_to(units[None], units_ref.shape)
-
-
-def library_body(library_ref, out_ref):
-    rows = library_ref[...].astype(f32)
-    mean_square = jnp.mean(rows * rows, axis=1, keepdims=True)
-    out_ref[...] = (rows * (1.0 / (KSIG * jnp.sqrt(mean_square + 1e-06)))).astype(bf16)
 
 
 def match_body(cols_wide, rows_narrow, tile_ref, gathered_ref, library_ref, out_ref):
@@ -549,9 +579,14 @@
     tile_line = clip_tile.reshape(1, clip_count)
     spectrum = (2, half, wide)
     basis = jax.ShapeDtypeStruct((2, CAP * KSIG, tile), bf16)
-    filters, row_basis, col_basis = call(
+    filters, row_basis, col_basis, lib_units = call(
         lambda *refs: filters_body(cols_wide, *refs),
-        (pltpu.HBM((real_count,) + spectrum, f32), basis, basis),
+        (
+            pltpu.HBM((real_count,) + spectrum, f32),
+            basis,
+            basis,
+            jax.ShapeDtypeStruct(library.shape, bf16),
+        ),
         (
             kernel_weight,
             kernels.reshape(real_count, KSIZE, KSIZE),
@@ -559,6 +594,7 @@
             table["taps_cols"],
             tile_line,
             clip_corner,
+            library,
         ),
         scratch=(
             pltpu.VMEM((real_count,) + spectrum, f32),
@@ -568,23 +604,17 @@
             pltpu.VMEM(table["taps_cols"].shape, bf16),
             pltpu.VMEM((1, clip_count), jnp.int32),
             pltpu.VMEM((2, clip_count), jnp.int32),
+            pltpu.VMEM(library.shape, bf16),
             pltpu.SemaphoreType.DMA((5,)),
             pltpu.SemaphoreType.DMA((real_count,)),
+            pltpu.SemaphoreType.DMA(()),
         ),
         smem=(0,),
-        hbm=(1, 2, 3, 4, 5),
-        out=(pl.BlockSpec(memory_space=pltpu.HBM), VMEM_SPEC, VMEM_SPEC),
+        hbm=(1, 2, 3, 4, 5, 6),
+        out=(pl.BlockSpec(memory_space=pltpu.HBM), VMEM_SPEC, VMEM_SPEC, VMEM_SPEC),
         flops=4 << 30,
         name="filters",
     )
-    lib_units = call(
-        library_body,
-        jax.ShapeDtypeStruct(library.shape, bf16),
-        (library,),
-        flops=1 << 30,
-        name="library",
-    )
-    filters, lib_units = lax.optimization_barrier((filters, lib_units))
     aerial, copies = call(
         lambda *refs: image_body(cols_wide, rows_narrow, *refs),
         (
@@ -605,7 +635,7 @@
         scratch=(
             pltpu.VMEM((wide, wide), bf16),
             pltpu.VMEM(spectrum, f32),
-            pltpu.VMEM((2, 3, GROUP * 2 * full, wide), bf16),
+            pltpu.VMEM((2, 2, GROUP * 2 * full, wide), bf16),
             pltpu.VMEM((2, GROUP, 2, wide, wide), bf16),
             pltpu.VMEM((tile, tile), f32),
             pltpu.VMEM((real_count,) + spectrum, f32),

time: 50 us -> 49.5 us (0.990)
  waiting for transfers between devices: 3.58 us -> 4.67 us
  Pallas kernels: 13.8 us -> 12.9 us
  local copies, waits for them, and re-layouts: 1.26 us -> 0.67 us
    all_to_all x1, waiting for transfers between devices: 3.58 us -> 4.67 us  [per_device(): got = lax.all_to_all(sent, both, 0, 0, tiled=True)]
    pallas_call x5 -> x4, Pallas kernels: 13.8 us -> 12.9 us  [call(): pl.pallas_call(body, out_shape=out_shape, in_specs=[pl.BlockSpec(memory_s...]
    unnamed x14 -> x12, local copies, waits for them, and re-layouts: 1.26 us -> 0.67 us
  transfers between devices with their start and end apart: 1 -> 1, of which waited for: 1 -> 1; matrix products, arithmetic and copies ran while one was open for 0% -> 0% of each run, Pallas kernels for 11% -> 10%
where the time goes in v6:
time: 49.5 us; the launch traced here: 49.2 us
  blocking collectives  22.4 us (45%)
  Pallas kernels  12.9 us (26%)
  starting transfers between devices  7.36 us (15%)
  waiting for transfers between devices  4.67 us (9%)
  between operations  0.71 us (1%)
  local copies, waits for them, and re-layouts  0.67 us (1%)
  other arithmetic  0.58 us (1%)
    pallas_call x4, Pallas kernels, call(): pl.pallas_call(body, out_shape=out_shape, in_specs=[pl.BlockSpec(memory_s...  12.9 us
    all_to_all x1, blocking collectives, per_device(): lax.all_to_all(copies, both, 0, 0, tiled=True)  12.7 us
    all_to_all x1, blocking collectives, per_device(): lax.all_to_all(slab, both, 0, 0, tiled=True)[:, :clip_count // device_count]  9.67 us
    all_to_all x1, starting transfers between devices, per_device(): got = lax.all_to_all(sent, both, 0, 0, tiled=True)  7.36 us
    all_to_all x1, waiting for transfers between devices, per_device(): got = lax.all_to_all(sent, both, 0, 0, tiled=True)  4.67 us
  transfers between devices with their start and end apart: 1, of which 1 were waited for; matrix products, arithmetic and copies ran while one was open for 0% of the time, Pallas kernels for 10%

profile of v6, /device:TPU:0, one launch (start us, length us, event | category | flops | bytes accessed | tf_op | source)
XLA Modules:
  0.0 49.2 jit_solution(14424715022059608171)
XLA Ops:
  0.6 1.6 %edges.1 = (bf16[128,128]{1,0:T(8,128)(2,1)S(1)}, bf16[32,32,128]{2,1,0:T(8,128)(2,1)}) custom-call(s32[128,128]{1,0:T(8,128)} %refs_0_.2, bf16[128,128]{1,0:T(8,128)(2,1)} %refs_1_.1), custom_call_target="tpu_custom_call" | custom-call | bytes 1048576 | tf_op jit(solution)/shard_map/edges/pallas_call | solution.py:523
  2.3 7.4 %all-to-all-start = ((bf16[32,32,128]{2,1,0:T(8,128)(2,1)}), bf16[32,32,128]{2,1,0:T(8,128)(2,1)S(1)}, u32[]{:S(2)}, u32[]{:S(2)}) async-start(bf16[32,32,128]{2,1,0:T(8,128)(2,1)} %get-tuple-element.11), calls=%async_computation | async-start | bytes 524288 | tf_op jit(solution)/shard_map/all_to_all | solution.py:577
  9.6 0.0 copy-start
  9.6 0.6 %copy-done = f32[8]{0:T(128)S(1)} copy-done((f32[8]{0:T(128)S(1)}, f32[8]{0:T(128)}, u32[]{:S(2)}) %copy-start) | copy-done | bytes 56
  10.3 0.0 copy-start.2
  10.3 0.0 copy-start.3
  10.3 0.0 copy-start.4
  10.3 0.0 copy-start.5
  10.3 4.9 %filters.1 = (f32[16,2,96,256]{3,2,1,0:T(8,128)}, bf16[2,256,128]{2,1,0:T(8,128)(2,1)S(1)}, bf16[2,256,128]{2,1,0:T(8,128)(2,1)S(1)}, bf16[2048,256]{1,0:T(8,128)(2,1)S(1)}) custom-call(f32[8]{0:T(128)S(1)} %copy-done, f32[16,64,64]{2,1,0:T(8,128)} %bitcast.13, bf16[192,384]{1,0:T(8,128)(2,1)} %constant.38.clone.refs_2_, ...), custom_call_target="tpu_custom_call" | custom-call | flops 4294967296 | bytes 1048576 | tf_op jit(solution)/shard_map/filters/pallas_call | solution.py:523
  15.2 4.7 %all-to-all-done.refs_1_ = bf16[32,32,128]{2,1,0:T(8,128)(2,1)S(1)} async-done(((bf16[32,32,128]{2,1,0:T(8,128)(2,1)}), bf16[32,32,128]{2,1,0:T(8,128)(2,1)S(1)}, u32[]{:S(2)}, u32[]{:S(2)}) %all-to-all-start) | async-done | bytes 262176 | tf_op jit(solution)/shard_map/all_to_all | solution.py:577
  19.9 0.0 copy-done.2
  19.9 0.0 copy-done.3
  19.9 0.0 copy-done.4
  19.9 0.0 copy-done.5
  19.9 0.0 copy-start.1
  19.9 5.2 %image.1 = (f32[128,128]{1,0:T(8,128)}, bf16[32,16,256]{2,1,0:T(8,128)(2,1)S(1)}) custom-call(bf16[128,128]{1,0:T(8,128)(2,1)S(1)} %get-tuple-element.10.refs_0_, bf16[32,32,128]{2,1,0:T(8,128)(2,1)S(1)} %all-to-all-done.refs_1_, f32[16,2,96,256]{3,2,1,0:T(8,128)} %get-tuple-element.12.refs_2_, bf16[2,256,128]{2,1,0:T(8,128)(2,1)S(1)} %get-tuple-element.13.refs_3_, ...), custom_call_target="tpu_custom_call" | custom-call | flops 6442450944 | bytes 1048576 | tf_op jit(solution)/shard_map/image/pallas_call | solution.py:523
  25.1 12.7 %all_to_all.22 = bf16[32,16,256]{2,1,0:T(8,128)(2,1)S(1)} all-to-all(bf16[32,16,256]{2,1,0:T(8,128)(2,1)S(1)} %get-tuple-element.16), channel_id=1, replica_groups=mesh['wide'=8,'narrow'=4] {'wide','narrow'}, dimensions={0} | all-to-all | bytes 524288 | tf_op jit(solution)/shard_map/all_to_all | solution.py:648
  37.8 0.0 copy-done.1
  37.8 1.2 %match.1 = f32[32,128]{1,0:T(8,128)S(1)} custom-call(s32[1,128]{1,0:T(1,128)S(1)} %bitcast.10, bf16[512,256]{1,0:T(8,128)(2,1)S(1)} %bitcast.7, bf16[2048,256]{1,0:T(8,128)(2,1)S(1)} %get-tuple-element.17.refs_2_), custom_call_target="tpu_custom_call" | custom-call | flops 1073741824 | bytes 1048576 | tf_op jit(solution)/shard_map/match/pallas_call | solution.py:523
  39.0 9.7 %all_to_all.23 = f32[32,1,128]{2,1,0:T(1,128)S(1)} all-to-all(f32[32,1,128]{2,1,0:T(1,128)S(1)} %bitcast.8), channel_id=1, replica_groups=mesh['wide'=8,'narrow'=4] {'wide','narrow'}, dimensions={0} | all-to-all | bytes 32768 | tf_op jit(solution)/shard_map/all_to_all | solution.py:657
  48.7 0.5 %negate_multiply_fusion = f32[4]{0:T(128)} fusion(f32[4]{0:T(128)S(1)} %slice_reduce_fusion, f32[4]{0:T(128)S(1)} %exponential_reduce_fusion), kind=kLoop, calls=%fused_computation.2 | loop fusion | flops 12 | bytes 48 | tf_op jit(solution)/shard_map/div | solution.py:660
  (2 shorter events, 0.0 us)
Async XLA Ops:
  2.3 17.6 %all-to-all-start = ((bf16[32,32,128]{2,1,0:T(8,128)(2,1)}), bf16[32,32,128]{2,1,0:T(8,128)(2,1)S(1)}, u32[]{:S(2)}, u32[]{:S(2)}) async-start(bf16[32,32,128]{2,1,0:T(8,128)(2,1)} %get-tuple-element.11), calls=%async_computation | async-start | bytes 524288 | tf_op jit(solution)/shard_map/all_to_all | solution.py:577
  9.6 0.7 %copy-start = (f32[8]{0:T(128)S(1)}, f32[8]{0:T(128)}, u32[]{:S(2)}) copy-start(f32[8]{0:T(128)} %refs_0_.3) | copy-start | bytes 100
  10.3 9.6 %copy-start.2 = (bf16[3,256,256]{2,1,0:T(8,128)(2,1)S(1)}, bf16[3,256,256]{2,1,0:T(8,128)(2,1)}, u32[]{:S(2)}) copy-start(bf16[3,256,256]{2,1,0:T(8,128)(2,1)} %constant.47.refs_6_) | copy-start | bytes 1179652
  10.3 9.6 %copy-start.3 = (bf16[3,192,256]{2,1,0:T(8,128)(2,1)S(1)}, bf16[3,192,256]{2,1,0:T(8,128)(2,1)}, u32[]{:S(2)}) copy-start(bf16[3,192,256]{2,1,0:T(8,128)(2,1)} %constant.43.refs_5_) | copy-start | bytes 884740
  10.3 9.6 %copy-start.4 = (bf16[2,128,256]{2,1,0:T(8,128)(2,1)S(1)}, bf16[2,128,256]{2,1,0:T(8,128)(2,1)}, u32[]{:S(2)}) copy-start(bf16[2,128,256]{2,1,0:T(8,128)(2,1)} %constant.50.refs_8_) | copy-start | bytes 393220
  10.3 9.6 %copy-start.5 = (bf16[256,256]{1,0:T(8,128)(2,1)S(1)}, bf16[256,256]{1,0:T(8,128)(2,1)}, u32[]{:S(2)}) copy-start(bf16[256,256]{1,0:T(8,128)(2,1)} %constant.35.clone.refs_7_) | copy-start | bytes 393220
  19.9 17.9 %copy-start.1 = (s32[128]{0:T(128)S(1)}, s32[128]{0:T(128)}, u32[]{:S(2)}) copy-start(s32[128]{0:T(128)} %param.23) | copy-start | bytes 1540

commit v7 on v6

--- a/solution.py
+++ b/solution.py
@@ -14,7 +14,7 @@
 CAP = 16
 SIGD = KSIG * KSIG
 LANES = 128
-GROUP = 2
+GROUP = 4
 
 sharpness = 400.0
 f32 = jnp.float32
@@ -474,7 +474,9 @@
     units_ref[...] = jnp.broadcast_to(units[None], units_ref.shape)
 
 
-def match_body(cols_wide, rows_narrow, tile_ref, gathered_ref, library_ref, out_ref):
+def match_body(
+    cols_wide, rows_narrow, tile_ref, gathered_ref, library_ref, out_ref, logits_ref
+):
     clip_count = tile_ref.shape[1]
     slot_count = gathered_ref.shape[0]
     device_count = out_ref.shape[0]
@@ -494,12 +496,30 @@
         place = (holder * CAP + rank).astype(jnp.int32)
         pick = (iota((LANES, slot_count), 1) == place).astype(f32).astype(bf16)
         units = dot(pick, gathered_ref[...]).astype(bf16)
-        cosine = lax.dot_general(
-            library_ref[...], units, (((1,), (1,)), ((), ())), preferred_element_type=f32
-        )
-        logits = sharpness * (cosine - 1.0)
-        peak = jnp.max(logits, axis=0, keepdims=True)
-        total = jnp.sum(jnp.exp(logits - peak), axis=0, keepdims=True)
+        rows = min(512, library_ref.shape[0])
+        steps = library_ref.shape[0] // rows
+
+        def logits_of(step):
+            cosine = lax.dot_general(
+                library_ref[step * rows : (step + 1) * rows],
+                units,
+                (((1,), (1,)), ((), ())),
+                preferred_element_type=f32,
+            )
+            return sharpness * (cosine - 1.0)
+
+        peak = None
+        for step in range(steps):
+            logits = logits_of(step)
+            logits_ref[step * rows : (step + 1) * rows] = logits
+            local = jnp.max(logits.reshape(rows // 8, 8, LANES), axis=0)
+            peak = local if peak is None else jnp.maximum(peak, local)
+        peak = jnp.max(peak, axis=0, keepdims=True)
+        total = jnp.zeros((8, LANES), f32)
+        for step in range(steps):
+            logits = logits_ref[step * rows : (step + 1) * rows]
+            total += jnp.sum(jnp.exp(logits - peak).reshape(rows // 8, 8, LANES), axis=0)
+        total = jnp.sum(total, axis=0, keepdims=True)
         peaks.append(peak + jnp.log(total))
     slab = peaks[0] if len(peaks) == 1 else jnp.concatenate(peaks, axis=1)
     shape = (device_count, clip_count)
@@ -650,6 +670,7 @@
         lambda *refs: match_body(cols_wide, rows_narrow, *refs),
         jax.ShapeDtypeStruct((device_count, LANES), f32),
         (tile_line, gathered, lib_units),
+        scratch=(pltpu.VMEM((library.shape[0], LANES), f32),),
         limit=40,
         flops=1 << 30,
         name="match",

time: 49.5 us -> 49 us (0.990)
  Pallas kernels: 12.9 us -> 12.3 us
    pallas_call x4, Pallas kernels: 12.9 us -> 12.3 us  [call(): pl.pallas_call(body, out_shape=out_shape, in_specs=[pl.BlockSpec(memory_s...]
where the time goes in v7:
time: 49 us; the launch traced here: 48.7 us
  blocking collectives  22.4 us (46%)
  Pallas kernels  12.3 us (25%)
  starting transfers between devices  7.36 us (15%)
  waiting for transfers between devices  4.67 us (10%)
  between operations  0.71 us (1%)
  local copies, waits for them, and re-layouts  0.67 us (1%)
  other arithmetic  0.58 us (1%)
    all_to_all x1, blocking collectives, per_device(): lax.all_to_all(copies, both, 0, 0, tiled=True)  12.7 us
    pallas_call x4, Pallas kernels, call(): pl.pallas_call(body, out_shape=out_shape, in_specs=[pl.BlockSpec(memory_s...  12.3 us
    all_to_all x1, blocking collectives, per_device(): lax.all_to_all(slab, both, 0, 0, tiled=True)[:, :clip_count // device_count]  9.67 us
    all_to_all x1, starting transfers between devices, per_device(): got = lax.all_to_all(sent, both, 0, 0, tiled=True)  7.36 us
    all_to_all x1, waiting for transfers between devices, per_device(): got = lax.all_to_all(sent, both, 0, 0, tiled=True)  4.67 us
  transfers between devices with their start and end apart: 1, of which 1 were waited for; matrix products, arithmetic and copies ran while one was open for 0% of the time, Pallas kernels for 10%

profile of v7, /device:TPU:0, one launch (start us, length us, event | category | flops | bytes accessed | tf_op | source)
XLA Modules:
  0.0 48.7 jit_solution(6527851821322491682)
XLA Ops:
  0.6 1.6 %edges.1 = (bf16[128,128]{1,0:T(8,128)(2,1)S(1)}, bf16[32,32,128]{2,1,0:T(8,128)(2,1)}) custom-call(s32[128,128]{1,0:T(8,128)} %refs_0_.2, bf16[128,128]{1,0:T(8,128)(2,1)} %refs_1_.1), custom_call_target="tpu_custom_call" | custom-call | bytes 1048576 | tf_op jit(solution)/shard_map/edges/pallas_call | solution.py:543
  2.3 7.4 %all-to-all-start = ((bf16[32,32,128]{2,1,0:T(8,128)(2,1)}), bf16[32,32,128]{2,1,0:T(8,128)(2,1)S(1)}, u32[]{:S(2)}, u32[]{:S(2)}) async-start(bf16[32,32,128]{2,1,0:T(8,128)(2,1)} %get-tuple-element.11), calls=%async_computation | async-start | bytes 524288 | tf_op jit(solution)/shard_map/all_to_all | solution.py:597
  9.6 0.0 copy-start
  9.6 0.6 %copy-done = f32[8]{0:T(128)S(1)} copy-done((f32[8]{0:T(128)S(1)}, f32[8]{0:T(128)}, u32[]{:S(2)}) %copy-start) | copy-done | bytes 56
  10.3 0.0 copy-start.2
  10.3 0.0 copy-start.3
  10.3 0.0 copy-start.4
  10.3 0.0 copy-start.5
  10.3 4.9 %filters.1 = (f32[16,2,96,256]{3,2,1,0:T(8,128)}, bf16[2,256,128]{2,1,0:T(8,128)(2,1)S(1)}, bf16[2,256,128]{2,1,0:T(8,128)(2,1)S(1)}, bf16[2048,256]{1,0:T(8,128)(2,1)S(1)}) custom-call(f32[8]{0:T(128)S(1)} %copy-done, f32[16,64,64]{2,1,0:T(8,128)} %bitcast.13, bf16[192,384]{1,0:T(8,128)(2,1)} %constant.38.clone.refs_2_, ...), custom_call_target="tpu_custom_call" | custom-call | flops 4294967296 | bytes 1048576 | tf_op jit(solution)/shard_map/filters/pallas_call | solution.py:543
  15.2 4.7 %all-to-all-done.refs_1_ = bf16[32,32,128]{2,1,0:T(8,128)(2,1)S(1)} async-done(((bf16[32,32,128]{2,1,0:T(8,128)(2,1)}), bf16[32,32,128]{2,1,0:T(8,128)(2,1)S(1)}, u32[]{:S(2)}, u32[]{:S(2)}) %all-to-all-start) | async-done | bytes 262176 | tf_op jit(solution)/shard_map/all_to_all | solution.py:597
  19.9 0.0 copy-done.2
  19.9 0.0 copy-done.3
  19.9 0.0 copy-done.4
  19.9 0.0 copy-done.5
  19.9 0.0 copy-start.1
  19.9 4.9 %image.1 = (f32[128,128]{1,0:T(8,128)}, bf16[32,16,256]{2,1,0:T(8,128)(2,1)S(1)}) custom-call(bf16[128,128]{1,0:T(8,128)(2,1)S(1)} %get-tuple-element.10.refs_0_, bf16[32,32,128]{2,1,0:T(8,128)(2,1)S(1)} %all-to-all-done.refs_1_, f32[16,2,96,256]{3,2,1,0:T(8,128)} %get-tuple-element.12.refs_2_, bf16[2,256,128]{2,1,0:T(8,128)(2,1)S(1)} %get-tuple-element.13.refs_3_, ...), custom_call_target="tpu_custom_call" | custom-call | flops 6442450944 | bytes 1048576 | tf_op jit(solution)/shard_map/image/pallas_call | solution.py:543
  24.7 12.7 %all_to_all.22 = bf16[32,16,256]{2,1,0:T(8,128)(2,1)S(1)} all-to-all(bf16[32,16,256]{2,1,0:T(8,128)(2,1)S(1)} %get-tuple-element.16), channel_id=1, replica_groups=mesh['wide'=8,'narrow'=4] {'wide','narrow'}, dimensions={0} | all-to-all | bytes 524288 | tf_op jit(solution)/shard_map/all_to_all | solution.py:668
  37.4 0.0 copy-done.1
  37.4 1.0 %match.1 = f32[32,128]{1,0:T(8,128)S(1)} custom-call(s32[1,128]{1,0:T(1,128)S(1)} %bitcast.10, bf16[512,256]{1,0:T(8,128)(2,1)S(1)} %bitcast.7, bf16[2048,256]{1,0:T(8,128)(2,1)S(1)} %get-tuple-element.17.refs_2_), custom_call_target="tpu_custom_call" | custom-call | flops 1073741824 | bytes 1048576 | tf_op jit(solution)/shard_map/match/pallas_call | solution.py:543
  38.4 9.7 %all_to_all.23 = f32[32,1,128]{2,1,0:T(1,128)S(1)} all-to-all(f32[32,1,128]{2,1,0:T(1,128)S(1)} %bitcast.8), channel_id=1, replica_groups=mesh['wide'=8,'narrow'=4] {'wide','narrow'}, dimensions={0} | all-to-all | bytes 32768 | tf_op jit(solution)/shard_map/all_to_all | solution.py:678
  48.2 0.5 %negate_multiply_fusion = f32[4]{0:T(128)} fusion(f32[4]{0:T(128)S(1)} %slice_reduce_fusion, f32[4]{0:T(128)S(1)} %exponential_reduce_fusion), kind=kLoop, calls=%fused_computation.2 | loop fusion | flops 12 | bytes 48 | tf_op jit(solution)/shard_map/div | solution.py:681
  (2 shorter events, 0.0 us)
Async XLA Ops:
  2.3 17.6 %all-to-all-start = ((bf16[32,32,128]{2,1,0:T(8,128)(2,1)}), bf16[32,32,128]{2,1,0:T(8,128)(2,1)S(1)}, u32[]{:S(2)}, u32[]{:S(2)}) async-start(bf16[32,32,128]{2,1,0:T(8,128)(2,1)} %get-tuple-element.11), calls=%async_computation | async-start | bytes 524288 | tf_op jit(solution)/shard_map/all_to_all | solution.py:597
  9.6 0.7 %copy-start = (f32[8]{0:T(128)S(1)}, f32[8]{0:T(128)}, u32[]{:S(2)}) copy-start(f32[8]{0:T(128)} %refs_0_.3) | copy-start | bytes 100
  10.3 9.6 %copy-start.2 = (bf16[3,256,256]{2,1,0:T(8,128)(2,1)S(1)}, bf16[3,256,256]{2,1,0:T(8,128)(2,1)}, u32[]{:S(2)}) copy-start(bf16[3,256,256]{2,1,0:T(8,128)(2,1)} %constant.47.refs_6_) | copy-start | bytes 1179652
  10.3 9.6 %copy-start.3 = (bf16[3,192,256]{2,1,0:T(8,128)(2,1)S(1)}, bf16[3,192,256]{2,1,0:T(8,128)(2,1)}, u32[]{:S(2)}) copy-start(bf16[3,192,256]{2,1,0:T(8,128)(2,1)} %constant.43.refs_5_) | copy-start | bytes 884740
  10.3 9.6 %copy-start.4 = (bf16[2,128,256]{2,1,0:T(8,128)(2,1)S(1)}, bf16[2,128,256]{2,1,0:T(8,128)(2,1)}, u32[]{:S(2)}) copy-start(bf16[2,128,256]{2,1,0:T(8,128)(2,1)} %constant.50.refs_8_) | copy-start | bytes 393220
  10.3 9.6 %copy-start.5 = (bf16[256,256]{1,0:T(8,128)(2,1)S(1)}, bf16[256,256]{1,0:T(8,128)(2,1)}, u32[]{:S(2)}) copy-start(bf16[256,256]{1,0:T(8,128)(2,1)} %constant.35.clone.refs_7_) | copy-start | bytes 393220
  19.9 17.6 %copy-start.1 = (s32[128]{0:T(128)S(1)}, s32[128]{0:T(128)}, u32[]{:S(2)}) copy-start(s32[128]{0:T(128)} %param.23) | copy-start | bytes 1540
